TPU v7x, 32 devices: a whole 2x2x4 slice. The times are simulated.
32 devices in a mesh: dp: 8 (over z, y), fsdp: 4 (over x, core).
Axes of the slice: x: 2, y: 2, z: 4, core: 2. Of those that a mesh axis runs over, the one named last changes fastest.
Arguments:
- layer_input: bfloat16 [16, 4, 256, 768], P(None, 'fsdp', 'dp'), may hold values from -6 to 6
- teacher: bfloat16 [16, 4, 256, 768], P('dp', 'fsdp'), may hold values from -6 to 6
- lengths: int32 [16], replicated, may hold values from 1 to 1024, 14336 in all
- dealing: int32 [16], replicated, may hold values from 0 to 15, each once
- attn_routes: int32 [16, 128], replicated, may hold values from 0 to 1023, as said below
- ffn_routes: int32 [16, 128], replicated, may hold values from 0 to 1023, as said below
- ffn_scores: float32 [16, 128], replicated, may hold values from 0.25 to 1
- gain_attn: bfloat16 [768], P(('dp', 'fsdp')), may hold values from 0.5 to 1.5
- gain_ffn: bfloat16 [768], P(('dp', 'fsdp')), may hold values from 0.5 to 1.5
- light_qkv: bfloat16 [768, 1536], P(('dp', 'fsdp')), may hold values from -0.21875 to 0.21875
- light_out: bfloat16 [512, 768], P(('dp', 'fsdp')), may hold values from -3 to 3
- heavy_qkv: bfloat16 [768, 2304], P(('dp', 'fsdp')), may hold values from -0.21875 to 0.21875
- heavy_out: bfloat16 [768, 768], P(('dp', 'fsdp')), may hold values from -2.5 to 2.5
- light_in: bfloat16 [768, 2048], P(('dp', 'fsdp')), may hold values from -0.21875 to 0.21875
- light_down: bfloat16 [1024, 768], P(('dp', 'fsdp')), may hold values from -0.1875 to 0.1875
- heavy_in: bfloat16 [768, 8192], P(('dp', 'fsdp')), may hold values from -0.21875 to 0.21875
- heavy_down: bfloat16 [4096, 768], P(('dp', 'fsdp')), may hold values from -0.09375 to 0.09375
Outputs:
- loss: float32 [], replicated
- input_grad: float32 [16, 4, 256, 768], P(None, 'fsdp', 'dp')
- gain_attn_grad: float32 [768], P(('dp', 'fsdp'))
- gain_ffn_grad: float32 [768], P(('dp', 'fsdp'))
- light_qkv_grad: float32 [768, 1536], P(('dp', 'fsdp'))
- light_out_grad: float32 [512, 768], P(('dp', 'fsdp'))
- heavy_qkv_grad: float32 [768, 2304], P(('dp', 'fsdp'))
- heavy_out_grad: float32 [768, 768], P(('dp', 'fsdp'))
- light_in_grad: float32 [768, 2048], P(('dp', 'fsdp'))
- light_down_grad: float32 [1024, 768], P(('dp', 'fsdp'))
- heavy_in_grad: float32 [768, 8192], P(('dp', 'fsdp'))
- heavy_down_grad: float32 [4096, 768], P(('dp', 'fsdp'))
Inputs may be any that keep to these rules, and one draw needn't show every extreme that they name: `attn_routes`: each row names 128 different positions of its sequence; at most 64 of them lie in one of the aligned blocks of 256 positions, and exactly 64 in one such block. `ffn_routes`: each row names 128 different positions of its sequence; at most 64 of them lie in one of the aligned blocks of 256 positions, and exactly 64 in one such block. `dealing`: each sequence once.
All inputs are finite; a program needn't handle non-finite values.
Results may differ from a plain program's by a relative error of at most 0.01.
The roundings to bfloat16 on the way count: a program that leaves them out, or rounds other values in their place, can miss the bound.
Values may be sent and summed in bfloat16 or wider, within the bound.
A program may use at most 256 MiB of HBM per device.

v0:
```python
import jax
import jax.numpy as jnp
from jax import lax
from jax.sharding import PartitionSpec as P

D = 768
HL = 8
HH = 12
DH = 64
FL = 1024
FH = 4096
WIN = 128
CAP = 64


EPSILON = 1e-06
MASKED = -1000000000.0
SCORE_SCALE = 0.125
PRECISE = lax.Precision.HIGHEST


def extended(cells, sides, width):
    for axis, dim in sides:
        count = lax.axis_size(axis)
        ends = count - 1
        head = lax.slice_in_dim(cells, 0, width, axis=dim)
        tail = lax.slice_in_dim(cells, cells.shape[dim] - width, cells.shape[dim], axis=dim)
        cells = jnp.concatenate(
            [
                lax.ppermute(tail, axis, [(i, (i + 1) % count) for i in range(ends)]),
                cells,
                lax.ppermute(head, axis, [((i + 1) % count, i) for i in range(ends)]),
            ],
            axis=dim,
        )
    return cells


def shifted_2(block, axis, distance):
    devices = range(lax.axis_size(axis))
    route = [(i - distance, i) for i in devices if i - distance in devices]
    return lax.ppermute(block, axis, route)


def rms_norm(value, gain):
    return value * lax.rsqrt(jnp.mean(value * value, axis=-1, keepdims=True) + EPSILON) * gain


def geglu(gate, upper):
    return jax.nn.gelu(gate, approximate=True) * upper


def geglu_back(up_proj, d_act):
    half_width = up_proj.shape[-1] // 2
    _, pullback = jax.vjp(geglu, up_proj[..., :half_width], up_proj[..., half_width:])
    d_gate, d_upper = pullback(d_act)
    return jnp.concatenate([d_gate, d_upper], axis=-1)


def flat_lanes(matrix):
    return matrix.reshape(-1, 128)


def with_columns(flat, columns):
    return flat.reshape(-1, columns)


def weight_columns():
    return (3 * HL * DH, D, 3 * HH * DH, D, 2 * FL, D, 2 * FH, D)


def flat_set(gain_a, gain_b, matrices):
    return (gain_a, gain_b) + tuple((flat_lanes(matrix) for matrix in matrices))


def unflat_set(values):
    shaped = tuple(
        (with_columns(flat, columns) for flat, columns in zip(values[2:], weight_columns()))
    )
    return (values[0], values[1]) + shaped


def routing(routes, piece, piece_len):
    owned_here = routes // piece_len == piece
    inside = routes - piece * piece_len
    slot_index = jnp.cumsum(owned_here.astype(jnp.int32), axis=1) - 1
    slot_hot = owned_here[..., None] & (slot_index[..., None] == jnp.arange(CAP)[None, None, :])
    place_hot = owned_here[..., None] & (inside[..., None] == jnp.arange(piece_len)[None, None, :])
    select = jnp.einsum("src,srp->scp", slot_hot.astype(jnp.float32), place_hot.astype(jnp.float32))
    filled = jnp.any(slot_hot, axis=1)
    placed = jnp.sum(jnp.where(slot_hot, routes[..., None], 0), axis=1)
    return (select, slot_hot.astype(jnp.float32), jnp.where(filled, placed, -1))


def split_heads(rows, heads):
    return rows.reshape(rows.shape[0], rows.shape[1], heads, -1)


def head_scores(queries, key_rows, allowed, heads):
    scores = (
        jnp.einsum(
            "sqhd,skhd->shqk",
            split_heads(queries, heads),
            split_heads(key_rows, heads),
            preferred_element_type=jnp.float32,
        )
        * SCORE_SCALE
    )
    return jnp.where(allowed[:, None], scores, MASKED)


def attend_forward(queries, key_rows, value_rows, allowed, heads):
    scores = head_scores(queries, key_rows, allowed, heads)
    row_max = jnp.max(scores, axis=-1, keepdims=True)
    shifted = jnp.exp(scores - row_max)
    row_sum = jnp.sum(shifted, axis=-1, keepdims=True)
    attn_prob = (shifted / row_sum).astype(jnp.bfloat16)
    attended = jnp.einsum(
        "shqk,skhd->sqhd",
        attn_prob,
        split_heads(value_rows, heads),
        preferred_element_type=jnp.float32,
    )
    return (attended.reshape(queries.shape).astype(jnp.bfloat16), row_max + jnp.log(row_sum))


def attend_backward(queries, key_rows, value_rows, allowed, log_sum, d_attended, heads):
    scores = head_scores(queries, key_rows, allowed, heads)
    attn_prob = jnp.exp(scores - log_sum)
    d_heads = split_heads(d_attended, heads)
    d_prob = jnp.einsum(
        "sqhd,skhd->shqk",
        d_heads,
        split_heads(value_rows, heads),
        preferred_element_type=jnp.float32,
    )
    row_dot = jnp.sum(attn_prob * d_prob, axis=-1, keepdims=True)
    d_scores = (attn_prob * (d_prob - row_dot)).astype(jnp.bfloat16)
    d_query = (
        jnp.einsum(
            "shqk,skhd->sqhd",
            d_scores,
            split_heads(key_rows, heads),
            preferred_element_type=jnp.float32,
        )
        * SCORE_SCALE
    )
    d_key = (
        jnp.einsum(
            "shqk,sqhd->skhd",
            d_scores,
            split_heads(queries, heads),
            preferred_element_type=jnp.float32,
        )
        * SCORE_SCALE
    )
    d_value = jnp.einsum(
        "shqk,sqhd->skhd",
        attn_prob.astype(jnp.bfloat16),
        d_heads,
        preferred_element_type=jnp.float32,
    )
    return (
        d_query.reshape(queries.shape),
        d_key.reshape(key_rows.shape),
        d_value.reshape(value_rows.shape),
    )


def project(left, right):
    return jnp.einsum("spd,de->spe", left, right, preferred_element_type=jnp.float32)


def project_back(left, right):
    return jnp.einsum("spe,de->spd", left, right, preferred_element_type=jnp.float32)


def weight_grad(left, right):
    return jnp.einsum("spd,spe->de", left, right, preferred_element_type=jnp.float32)


def local(
    layer_input,
    teacher,
    lengths,
    dealing,
    attn_routes,
    ffn_routes,
    ffn_scores,
    gain_attn,
    gain_ffn,
    light_qkv,
    light_out,
    heavy_qkv,
    heavy_out,
    light_in,
    light_down,
    heavy_in,
    heavy_down,
):
    data_count = lax.axis_size("dp")
    piece_count = lax.axis_size("fsdp")
    data_index = lax.axis_index("dp")
    piece_index = lax.axis_index("fsdp")
    seqs_all = dealing.shape[0]
    seq_group = seqs_all // data_count
    ordered = jnp.take(layer_input, dealing, axis=0)
    dealt_rows = lax.all_to_all(ordered, "dp", split_axis=0, concat_axis=2, tiled=True)
    inputs = dealt_rows[:, 0].astype(jnp.float32)
    targets = teacher[:, 0].astype(jnp.float32)
    chosen = lax.dynamic_slice_in_dim(dealing, data_index * seq_group, seq_group)
    seq_lengths = jnp.take(lengths, chosen)
    attn_pick = jnp.take(attn_routes, chosen, axis=0)
    ffn_pick = jnp.take(ffn_routes, chosen, axis=0)
    score_pick = jnp.take(ffn_scores, chosen, axis=0)
    token_count = jnp.sum(lengths).astype(jnp.float32)
    matrices = (
        light_qkv,
        light_out,
        heavy_qkv,
        heavy_out,
        light_in,
        light_down,
        heavy_in,
        heavy_down,
    )
    flat_fwd = flat_set(gain_attn, gain_ffn, matrices)
    gathered = unflat_set(
        (
            lax.all_gather(flat_fwd[0], ("dp", "fsdp"), axis=0, tiled=True),
            lax.all_gather(flat_fwd[1], ("dp", "fsdp"), axis=0, tiled=True),
            lax.all_gather(flat_fwd[2], ("dp", "fsdp"), axis=0, tiled=True),
            lax.all_gather(flat_fwd[3], ("dp", "fsdp"), axis=0, tiled=True),
            lax.all_gather(flat_fwd[4], ("dp", "fsdp"), axis=0, tiled=True),
            lax.all_gather(flat_fwd[5], ("dp", "fsdp"), axis=0, tiled=True),
            lax.all_gather(flat_fwd[6], ("dp", "fsdp"), axis=0, tiled=True),
            lax.all_gather(flat_fwd[7], ("dp", "fsdp"), axis=0, tiled=True),
            lax.all_gather(flat_fwd[8], ("dp", "fsdp"), axis=0, tiled=True),
            lax.all_gather(flat_fwd[9], ("dp", "fsdp"), axis=0, tiled=True),
        )
    )
    g_attn, g_ffn, w_lqkv, w_lout, w_hqkv, w_hout, w_lin, w_ldown, w_hin, w_hdown = gathered
    gain_one = g_attn.astype(jnp.float32)
    gain_two = g_ffn.astype(jnp.float32)
    tokens = inputs.shape[1]
    width_light = HL * DH
    width_heavy = HH * DH
    positions = piece_index * tokens + jnp.arange(tokens)
    valid_mask = positions[None, :] < seq_lengths[:, None]
    normed = rms_norm(inputs, gain_one).astype(jnp.bfloat16)
    light_proj = project(normed, w_lqkv)
    l_query = light_proj[..., :width_light].astype(jnp.bfloat16)
    l_keys = light_proj[..., width_light : 2 * width_light].astype(jnp.bfloat16)
    l_values = light_proj[..., 2 * width_light :].astype(jnp.bfloat16)
    rim_pair = extended(jnp.concatenate([l_keys, l_values], axis=-1), (("fsdp", 1),), WIN)
    rim_keys = rim_pair[..., :width_light]
    rim_values = rim_pair[..., width_light:]
    key_pos = piece_index * tokens - WIN + jnp.arange(tokens + 2 * WIN)
    within_reach = jnp.abs(positions[:, None] - key_pos[None, :]) <= WIN
    live_key = (key_pos[None, :] >= 0) & (key_pos[None, :] < seq_lengths[:, None])
    light_allowed = within_reach[None] & (
        live_key[:, None, :] | (positions[:, None] == key_pos[None, :])[None]
    )
    l_att, l_lse = attend_forward(l_query, rim_keys, rim_values, light_allowed, HL)
    light_branch = project(l_att, w_lout)
    a_select, a_hot, a_spot = routing(attn_pick, piece_index, tokens)
    a_rows = jnp.einsum(
        "scp,spd->scd", a_select.astype(jnp.bfloat16), normed, preferred_element_type=jnp.float32
    ).astype(jnp.bfloat16)
    heavy_proj = project(a_rows, w_hqkv)
    h_query = heavy_proj[..., :width_heavy].astype(jnp.bfloat16)
    kv_own = heavy_proj[..., width_heavy:].astype(jnp.bfloat16)
    kv_every = lax.all_gather(kv_own, "fsdp", axis=1, tiled=True)
    all_spots = jnp.concatenate(
        [routing(attn_pick, other_piece, tokens)[2] for other_piece in range(piece_count)], axis=1
    )
    heavy_allowed = ((all_spots >= 0) & (all_spots < seq_lengths[:, None]))[:, None, :] | (
        a_spot[:, :, None] == all_spots[:, None, :]
    )
    hv_keys = kv_every[..., :width_heavy]
    hv_values = kv_every[..., width_heavy:]
    h_att, h_lse = attend_forward(h_query, hv_keys, hv_values, heavy_allowed, HH)
    heavy_branch = project(h_att, w_hout)
    spread_attn = jnp.einsum("scp,scd->spd", a_select, heavy_branch, precision=PRECISE)
    hidden = inputs + light_branch + spread_attn
    normed_two = rms_norm(hidden, gain_two).astype(jnp.bfloat16)
    light_up = project(normed_two, w_lin)
    light_mid = geglu(light_up[..., :FL], light_up[..., FL:]).astype(jnp.bfloat16)
    light_ffn = project(light_mid, w_ldown)
    f_select, f_hot, f_spot = routing(ffn_pick, piece_index, tokens)
    f_rows = jnp.einsum(
        "scp,spd->scd",
        f_select.astype(jnp.bfloat16),
        normed_two,
        preferred_element_type=jnp.float32,
    ).astype(jnp.bfloat16)
    heavy_up = project(f_rows, w_hin)
    heavy_mid = geglu(heavy_up[..., :FH], heavy_up[..., FH:]).astype(jnp.bfloat16)
    heavy_ffn = project(heavy_mid, w_hdown)
    slot_score = jnp.einsum("src,sr->sc", f_hot, score_pick, precision=PRECISE)
    spread_ffn = jnp.einsum(
        "scp,scd->spd", f_select, heavy_ffn * slot_score[..., None], precision=PRECISE
    )
    output = hidden + light_ffn + spread_ffn
    misfit = output - targets
    weight_mask = valid_mask[..., None].astype(jnp.float32)
    partial_loss = jnp.sum(weight_mask * misfit * misfit)
    loss_value = lax.psum(partial_loss, ("dp", "fsdp")) / (D * token_count)
    d_out = 2.0 * weight_mask * misfit / (D * token_count)
    back_full = unflat_set(
        (
            lax.all_gather(flat_fwd[0], ("dp", "fsdp"), axis=0, tiled=True),
            lax.all_gather(flat_fwd[1], ("dp", "fsdp"), axis=0, tiled=True),
            lax.all_gather(flat_fwd[2], ("dp", "fsdp"), axis=0, tiled=True),
            lax.all_gather(flat_fwd[3], ("dp", "fsdp"), axis=0, tiled=True),
            lax.all_gather(flat_fwd[4], ("dp", "fsdp"), axis=0, tiled=True),
            lax.all_gather(flat_fwd[5], ("dp", "fsdp"), axis=0, tiled=True),
            lax.all_gather(flat_fwd[6], ("dp", "fsdp"), axis=0, tiled=True),
            lax.all_gather(flat_fwd[7], ("dp", "fsdp"), axis=0, tiled=True),
            lax.all_gather(flat_fwd[8], ("dp", "fsdp"), axis=0, tiled=True),
            lax.all_gather(flat_fwd[9], ("dp", "fsdp"), axis=0, tiled=True),
        )
    )
    b_attn, b_ffn, b_lqkv, b_lout, b_hqkv, b_hout, b_lin, b_ldown, b_hin, b_hdown = back_full
    back_one = b_attn.astype(jnp.float32)
    back_two = b_ffn.astype(jnp.float32)
    d_heavy_ffn = (
        jnp.einsum("scp,spd->scd", f_select, d_out, precision=PRECISE) * slot_score[..., None]
    ).astype(jnp.bfloat16)
    grad_hdown = weight_grad(heavy_mid, d_heavy_ffn)
    d_heavy_mid = project_back(d_heavy_ffn, b_hdown)
    d_heavy_up = geglu_back(heavy_up, d_heavy_mid).astype(jnp.bfloat16)
    grad_hin = weight_grad(f_rows, d_heavy_up)
    d_f_rows = project_back(d_heavy_up, b_hin)
    d_norm_two = jnp.einsum("scp,scd->spd", f_select, d_f_rows, precision=PRECISE)
    d_light = d_out.astype(jnp.bfloat16)
    grad_ldown = weight_grad(light_mid, d_light)
    d_light_mid = project_back(d_light, b_ldown)
    d_light_up = geglu_back(light_up, d_light_mid).astype(jnp.bfloat16)
    grad_lin = weight_grad(normed_two, d_light_up)
    d_norm_two = d_norm_two + project_back(d_light_up, b_lin)
    _, second_pull = jax.vjp(rms_norm, hidden, back_two)
    d_hidden_norm, grad_gain_two = second_pull(d_norm_two)
    d_hidden = d_out + d_hidden_norm
    d_heavy_attn = jnp.einsum("scp,spd->scd", a_select, d_hidden, precision=PRECISE).astype(
        jnp.bfloat16
    )
    grad_hout = weight_grad(h_att, d_heavy_attn)
    d_h_att = project_back(d_heavy_attn, b_hout).astype(jnp.bfloat16)
    dq_heavy, dk_heavy, dv_heavy = attend_backward(
        h_query, hv_keys, hv_values, heavy_allowed, h_lse, d_h_att, HH
    )
    kv_grads = lax.psum_scatter(
        jnp.concatenate([dk_heavy, dv_heavy], axis=-1).astype(jnp.bfloat16),
        "fsdp",
        scatter_dimension=1,
        tiled=True,
    ).astype(jnp.float32)
    d_h_proj = jnp.concatenate([dq_heavy, kv_grads], axis=-1).astype(jnp.bfloat16)
    grad_hqkv = weight_grad(a_rows, d_h_proj)
    d_a_rows = project_back(d_h_proj, b_hqkv)
    d_normed = jnp.einsum("scp,scd->spd", a_select, d_a_rows, precision=PRECISE)
    d_light_attn = d_hidden.astype(jnp.bfloat16)
    grad_lout = weight_grad(l_att, d_light_attn)
    d_l_att = project_back(d_light_attn, b_lout).astype(jnp.bfloat16)
    dq_light, dk_light, dv_light = attend_backward(
        l_query, rim_keys, rim_values, light_allowed, l_lse, d_l_att, HL
    )
    rim_grads = jnp.concatenate([dk_light, dv_light], axis=-1)
    from_right = shifted_2(rim_grads[:, :WIN].astype(jnp.bfloat16), "fsdp", -1).astype(jnp.float32)
    from_left = shifted_2(rim_grads[:, tokens + WIN :].astype(jnp.bfloat16), "fsdp", 1).astype(
        jnp.float32
    )
    own_grads = rim_grads[:, WIN : WIN + tokens]
    own_grads = (
        own_grads
        + jnp.pad(from_left, ((0, 0), (0, tokens - WIN), (0, 0)))
        + jnp.pad(from_right, ((0, 0), (tokens - WIN, 0), (0, 0)))
    )
    d_l_proj = jnp.concatenate([dq_light, own_grads], axis=-1).astype(jnp.bfloat16)
    grad_lqkv = weight_grad(normed, d_l_proj)
    d_normed = d_normed + project_back(d_l_proj, b_lqkv)
    _, first_pull = jax.vjp(rms_norm, inputs, back_one)
    d_inputs_norm, grad_gain_one = first_pull(d_normed)
    d_inputs = d_hidden + d_inputs_norm
    returned = lax.all_to_all(
        d_inputs[:, None].astype(jnp.bfloat16), "dp", split_axis=2, concat_axis=0, tiled=True
    ).astype(jnp.float32)
    order_all = jnp.arange(seqs_all)
    inverse = jnp.sum(
        jnp.where(dealing[None, :] == order_all[:, None], order_all[None, :], 0), axis=1
    )
    d_layer = jnp.take(returned, inverse, axis=0)
    grad_flat = flat_set(
        grad_gain_one,
        grad_gain_two,
        (grad_lqkv, grad_lout, grad_hqkv, grad_hout, grad_lin, grad_ldown, grad_hin, grad_hdown),
    )
    owned_flat = (
        lax.psum_scatter(grad_flat[0], ("dp", "fsdp"), scatter_dimension=0, tiled=True),
        lax.psum_scatter(grad_flat[1], ("dp", "fsdp"), scatter_dimension=0, tiled=True),
        lax.psum_scatter(grad_flat[2], ("dp", "fsdp"), scatter_dimension=0, tiled=True),
        lax.psum_scatter(grad_flat[3], ("dp", "fsdp"), scatter_dimension=0, tiled=True),
        lax.psum_scatter(grad_flat[4], ("dp", "fsdp"), scatter_dimension=0, tiled=True),
        lax.psum_scatter(grad_flat[5], ("dp", "fsdp"), scatter_dimension=0, tiled=True),
        lax.psum_scatter(grad_flat[6], ("dp", "fsdp"), scatter_dimension=0, tiled=True),
        lax.psum_scatter(grad_flat[7], ("dp", "fsdp"), scatter_dimension=0, tiled=True),
        lax.psum_scatter(grad_flat[8], ("dp", "fsdp"), scatter_dimension=0, tiled=True),
        lax.psum_scatter(grad_flat[9], ("dp", "fsdp"), scatter_dimension=0, tiled=True),
    )
    owned_grads = unflat_set(owned_flat)
    return (
        loss_value,
        d_layer,
        owned_grads[0],
        owned_grads[1],
        owned_grads[2],
        owned_grads[3],
        owned_grads[4],
        owned_grads[5],
        owned_grads[6],
        owned_grads[7],
        owned_grads[8],
        owned_grads[9],
    )


def solution(mesh):
    placed = (
        P(None, "fsdp", "dp", None),
        P("dp", "fsdp", None, None),
        P(),
        P(),
        P(),
        P(),
        P(),
        P(("dp", "fsdp")),
        P(("dp", "fsdp")),
        P(("dp", "fsdp"), None),
        P(("dp", "fsdp"), None),
        P(("dp", "fsdp"), None),
        P(("dp", "fsdp"), None),
        P(("dp", "fsdp"), None),
        P(("dp", "fsdp"), None),
        P(("dp", "fsdp"), None),
        P(("dp", "fsdp"), None),
    )
    return jax.shard_map(
        local,
        mesh=mesh,
        in_specs=placed,
        out_specs=(
            P(),
            P(None, "fsdp", "dp", None),
            P(("dp", "fsdp")),
            P(("dp", "fsdp")),
            P(("dp", "fsdp"), None),
            P(("dp", "fsdp"), None),
            P(("dp", "fsdp"), None),
            P(("dp", "fsdp"), None),
            P(("dp", "fsdp"), None),
            P(("dp", "fsdp"), None),
            P(("dp", "fsdp"), None),
            P(("dp", "fsdp"), None),
        ),
        check_vma=False,
    )
```

profile of v0, /device:TPU:0, one launch (start us, length us, event | category | flops | bytes accessed | tf_op | source)
XLA Modules:
  0.0 1705.2 jit_solution(13142866561375623902)
XLA Ops:
  17.8 7.3 all-to-all-start
  25.7 43.4 %all-reduce.7 = (bf16[768]{0:T(1024)(128)(2,1)S(1)}, bf16[768]{0:T(1024)(128)(2,1)}) all-reduce(bf16[768]{0:T(1024)(128)(2,1)S(1)} %dynamic-update-slice, bf16[768]{0:T(1024)(128)(2,1)S(1)} %dynamic-update-slice.1), channel_id=1, replica_groups=mesh['dp'=8,'fsdp'=4] {'dp','fsdp'}, use_global_device_ids=true, to_apply=%add.2 | all-reduce | flops 1536 | bytes 6144
  74.5 4.2 all-gather.11.cloned.1.call-done
  78.6 7.6 reshape.747
  86.2 2.7 convolution_convert_fusion
  100.1 44.7 %all_gather.45 = bf16[3072,128]{1,0:T(8,128)(2,1)} all-gather(bf16[96,128]{1,0:T(8,128)(2,1)S(1)} %reshape.632), channel_id=1, replica_groups=mesh['dp'=8,'fsdp'=4] {'dp','fsdp'}, dimensions={0}, use_global_device_ids=true | all-gather | bytes 811008 | tf_op jit(solution)/shard_map/all_gather | solution.py:233
  145.9 5.7 reshape.745
  151.5 3.0 convolution_convert_fusion.1
  156.9 3.0 collective-permute-start
  165.5 29.4 %all-gather.15.cloned.1.call-done = bf16[4608,128]{1,0:T(8,128)(2,1)} async-done(((bf16[144,128]{1,0:T(8,128)(2,1)}), bf16[4608,128]{1,0:T(8,128)(2,1)}) %all-gather.15.cloned.1.call-update) | async-done | bytes 1179664 | tf_op jit(solution)/shard_map/all_gather | solution.py:235
  197.4 54.6 %all-gather.19.cloned.1.call-done = bf16[6144,128]{1,0:T(8,128)(2,1)} async-done(((bf16[192,128]{1,0:T(8,128)(2,1)}), bf16[6144,128]{1,0:T(8,128)(2,1)}) %all-gather.19.cloned.1.call-update) | async-done | bytes 1572880 | tf_op jit(solution)/shard_map/all_gather | solution.py:237
  252.0 4.0 reshape.750
  269.5 3.0 fusion.107
  275.8 3.4 fusion.36
  279.2 34.0 %all-gather.17.cloned.1.call-done = bf16[12288,128]{1,0:T(8,128)(2,1)} async-done(((bf16[384,128]{1,0:T(8,128)(2,1)}), bf16[12288,128]{1,0:T(8,128)(2,1)}) %all-gather.17.cloned.1.call-update) | async-done | bytes 3145744 | tf_op jit(solution)/shard_map/all_gather | solution.py:236
  313.2 6.0 reshape.749
  320.1 13.5 all-gather.13.cloned.1.call-done
  333.7 2.6 fusion.105
  337.7 2.6 copy.142
  355.9 50.7 %all-gather.23.cloned.1.call-done = bf16[24576,128]{1,0:T(8,128)(2,1)} async-done(((bf16[768,128]{1,0:T(8,128)(2,1)}), bf16[24576,128]{1,0:T(8,128)(2,1)}) %all-gather.23.cloned.1.call-update) | async-done | bytes 6291472 | tf_op jit(solution)/shard_map/all_gather | solution.py:239
  406.7 11.7 reshape.752
  418.3 85.7 %all-gather.21.cloned.1.call-done = bf16[49152,128]{1,0:T(8,128)(2,1)} async-done(((bf16[1536,128]{1,0:T(8,128)(2,1)}), bf16[49152,128]{1,0:T(8,128)(2,1)}) %all-gather.21.cloned.1.call-update) | async-done | bytes 12582928 | tf_op jit(solution)/shard_map/all_gather | solution.py:238
  504.0 19.7 %reshape.751 = bf16[768,8192,1]{1,0,2:T(8,128)(2,1)} reshape(bf16[49152,128]{1,0:T(8,128)(2,1)} %all-gather.21.cloned.1.call-done) | data formatting | bytes 25165824 | tf_op jit(solution)/shard_map/reshape | solution.py:65
  523.8 6.5 fusion.112
  539.6 4.3 fusion.20
  545.8 8.9 fusion.35
  564.5 2.9 convolution_convert_fusion.2
  567.4 3.6 multiply_reduce_fusion.4
  580.2 2.6 pad_maximum_fusion.4
  582.9 3.4 convolution_bitcast_fusion.7
  589.2 3.0 convolution_bitcast_fusion.6
  592.3 3.2 reshape.663
  596.2 4.5 convolution_bitcast_fusion.5
  600.6 4.4 reshape.667
  606.5 3.0 convolution_convert_fusion.3
  611.5 6.2 fusion.3
  617.8 2.9 copy.155
  620.7 6.8 multiply_reduce_fusion
  627.5 4.6 multiply_convert_fusion
  632.1 2.7 convolution_multiply_fusion
  634.9 3.0 copy.154
  637.8 2.7 fusion.2
  641.7 2.9 collective-permute-start.2
  653.4 3.7 convolution_bitcast_fusion.3
  657.1 5.6 reshape.657
  663.0 6.0 convolution_bitcast_fusion.4
  669.0 7.2 reshape.665
  680.7 5.0 convolution_bitcast_fusion.2
  685.8 7.9 reshape.661
  694.7 6.4 convolution_bitcast_fusion.1
  701.0 13.3 reshape.671
  715.7 11.6 convolution_bitcast_fusion
  727.3 27.0 %reshape.669 = f32[49152,128]{1,0:T(8,128)} reshape(f32[768,8192]{1,0:T(8,128)} %convolution_bitcast_fusion) | data formatting | bytes 50331648 | tf_op jit(solution)/shard_map/reshape | solution.py:61
  755.3 3.4 fusion.49
  764.0 3.8 all-to-all-start.1
  769.4 45.1 %all-reduce.6 = (f32[]{:T(128)}, f32[768]{0:T(1024)S(1)}, f32[768]{0:T(1024)S(1)}) all-reduce(f32[]{:T(128)} %get-tuple-element.102, f32[768]{0:T(1024)S(1)} %get-tuple-element.63, f32[768]{0:T(1024)S(1)} %copy-done.73), channel_id=1, replica_groups=mesh['dp'=8,'fsdp'=4] {'dp','fsdp'}, use_global_device_ids=true, to_apply=%region_23.25 | all-reduce | flops 1537 | bytes 12296 | tf_op jit(solution)/shard_map/psum | solution.py:308
  816.3 5.4 reduce-scatter.18.cloned.1.call-done
  823.3 104.2 %reduce-scatter.22.cloned.1.call-done = f32[192,128]{1,0:T(8,128)} async-done(((f32[6144,128]{1,0:T(8,128)}), f32[192,128]{1,0:T(8,128)}) %reduce-scatter.22.cloned.1.call-update) | async-done | bytes 98320 | tf_op jit(solution)/shard_map/reduce_scatter | solution.py:407
  931.2 2.8 fusion.29
  934.1 104.9 %reduce-scatter.12.cloned.1.call-done = f32[288,128]{1,0:T(8,128)} async-done(((f32[9216,128]{1,0:T(8,128)}), f32[288,128]{1,0:T(8,128)}) %reduce-scatter.12.cloned.1.call-update) | async-done | bytes 147472 | tf_op jit(solution)/shard_map/reduce_scatter | solution.py:402
  1040.5 118.4 %reduce-scatter.20.cloned.1.call-done = f32[384,128]{1,0:T(8,128)} async-done(((f32[12288,128]{1,0:T(8,128)}), f32[384,128]{1,0:T(8,128)}) %reduce-scatter.20.cloned.1.call-update) | async-done | bytes 196624 | tf_op jit(solution)/shard_map/reduce_scatter | solution.py:406
  1160.5 122.4 %reduce-scatter.16.cloned.1.call-done = f32[432,128]{1,0:T(8,128)} async-done(((f32[13824,128]{1,0:T(8,128)}), f32[432,128]{1,0:T(8,128)}) %reduce-scatter.16.cloned.1.call-update) | async-done | bytes 221200 | tf_op jit(solution)/shard_map/reduce_scatter | solution.py:404
  1284.5 159.9 %reduce-scatter.26.cloned.1.call-done = f32[768,128]{1,0:T(8,128)} async-done(((f32[24576,128]{1,0:T(8,128)}), f32[768,128]{1,0:T(8,128)}) %reduce-scatter.26.cloned.1.call-update) | async-done | bytes 393232 | tf_op jit(solution)/shard_map/reduce_scatter | solution.py:409
  1446.3 249.0 %reduce-scatter.24.cloned.1.call-done = f32[1536,128]{1,0:T(8,128)} async-done(((f32[49152,128]{1,0:T(8,128)}), f32[1536,128]{1,0:T(8,128)}) %reduce-scatter.24.cloned.1.call-update) | async-done | bytes 786448 | tf_op jit(solution)/shard_map/reduce_scatter | solution.py:408
  (411 shorter events, 149.2 us)
Async XLA Ops:
  7.2 9.0 copy-start
  7.2 9.6 copy-start.105
  7.2 71.4 %all-gather.11.cloned.1.call-start = ((), (), s32[]{:S(2)}) async-start(), calls=%async_computation.12 | async-start | bytes 3649536 | tf_op jit(solution)/shard_map/all_gather | solution.py:234
  9.0 136.8 %all-gather.9.cloned.1.call-start = ((), (), s32[]{:S(2)}) async-start(), calls=%async_computation.11 | async-start | bytes 2433024 | tf_op jit(solution)/shard_map/all_gather | solution.py:232
  10.7 184.1 %all-gather.15.cloned.1.call-start = ((), (), s32[]{:S(2)}) async-start(), calls=%async_computation.14 | async-start | bytes 1216512 | tf_op jit(solution)/shard_map/all_gather | solution.py:235
  12.3 239.8 %all-gather.19.cloned.1.call-start = ((), (), s32[]{:S(2)}) async-start(), calls=%async_computation.16 | async-start | bytes 1622016 | tf_op jit(solution)/shard_map/all_gather | solution.py:237
  13.8 299.4 %all-gather.17.cloned.1.call-start = ((), (), s32[]{:S(2)}) async-start(), calls=%async_computation.15 | async-start | bytes 3244032 | tf_op jit(solution)/shard_map/all_gather | solution.py:236
  16.1 9.0 copy-start.107
  16.2 9.3 copy-start.108
  16.2 53.5 %copy-start.86 = (s32[16,128]{1,0:T(8,128)S(1)}, s32[16,128]{1,0:T(8,128)}, u32[]{:S(2)}) copy-start(s32[16,128]{1,0:T(8,128)} %param.24) | copy-start | bytes 24580
  16.2 54.1 %copy-start.87 = (s32[16,128]{1,0:T(8,128)S(1)}, s32[16,128]{1,0:T(8,128)}, u32[]{:S(2)}) copy-start(s32[16,128]{1,0:T(8,128)} %param.23) | copy-start | bytes 24580
  17.8 54.9 %all-to-all-start = ((bf16[16,1,32,768]{3,2,1,0:T(8,128)(2,1)}), bf16[16,1,32,768]{3,2,1,0:T(8,128)(2,1)S(1)}, u32[]{:S(2)}, u32[]{:S(2)}) async-start(bf16[16,1,32,768]{3,2,1,0:T(8,128)(2,1)} %bitcast_select_fusion.1), calls=%async_computation | async-start | bytes 1572864 | tf_op jit(solution)/shard_map/all_to_all | solution.py:208
  25.1 308.6 %all-gather.13.cloned.1.call-start = ((), (), s32[]{:S(2)}) async-start(), calls=%async_computation.13 | async-start | bytes 1966080 | tf_op jit(solution)/shard_map/all_gather | solution.py:273
  74.5 11.8 copy-start.35
  86.2 5.6 copy-start.61
  88.9 55.8 %copy-start.37 = (bf16[2,64,2304]{2,1,0:T(8,128)(2,1)}, bf16[2,64,2304]{2,1,0:T(8,128)(2,1)S(1)}, u32[]{:S(2)}) copy-start(bf16[2,64,2304]{2,1,0:T(8,128)(2,1)S(1)} %convolution_convert_fusion) | copy-start | bytes 1769476
  89.0 5.7 copy-start.98
  89.0 6.0 copy-start.97
  89.0 6.3 copy-start.96
  89.0 6.6 copy-start.95
  89.0 6.9 copy-start.68
  89.0 7.0 copy-start.89
  89.1 7.1 copy-start.75
  89.1 7.1 copy-start.92
  89.1 7.1 copy-start.94
  89.1 7.3 copy-start.90
  89.1 7.3 copy-start.91
  89.1 7.4 copy-start.79
  89.1 7.7 copy-start.102
  89.1 7.7 copy-start.85
  89.1 8.5 copy-start.77
  89.1 10.0 copy-start.104
  90.0 316.7 %all-gather.23.cloned.1.call-start = ((), (), s32[]{:S(2)}) async-start(), calls=%async_computation.18 | async-start | bytes 6488064 | tf_op jit(solution)/shard_map/all_gather | solution.py:239
  91.8 412.2 %all-gather.21.cloned.1.call-start = ((), (), s32[]{:S(2)}) async-start(), calls=%async_computation.17 | async-start | bytes 12976128 | tf_op jit(solution)/shard_map/all_gather | solution.py:238
  92.9 587.9 %reduce-scatter.10.cloned.1.call-start = ((), (), s32[]{:S(2)}) async-start(), calls=%async_computation.19 | async-start | bytes 1966080 | tf_op jit(solution)/shard_map/reduce_scatter | solution.py:353
  145.9 5.7 copy-start.59
  155.7 7.7 copy-start.100
  155.7 7.7 copy-start.32
  156.9 104.6 %collective-permute-start = (bf16[2,128,1024]{2,1,0:T(8,128)(2,1)}, bf16[2,128,1024]{2,1,0:T(8,128)(2,1)}, u32[]{:S(2)}, u32[]{:S(2)}) collective-permute-start(bf16[2,128,1024]{2,1,0:T(8,128)(2,1)} %get-tuple-element.103), channel_id=1, source_target_pairs={{0,1},{1,2},{2,3},{4,5},{5,6},{6,7},{8,9},{9,10},{10,11},{12,13},{... | collective-permute-start | bytes 1572872 | tf_op jit(solution)/shard_map/ppermute | solution.py:30
  159.9 101.6 %collective-permute-start.1 = (bf16[2,128,1024]{2,1,0:T(8,128)(2,1)}, bf16[2,128,1024]{2,1,0:T(8,128)(2,1)}, u32[]{:S(2)}, u32[]{:S(2)}) collective-permute-start(bf16[2,128,1024]{2,1,0:T(8,128)(2,1)} %get-tuple-element.104), channel_id=1, source_target_pairs={{1,0},{2,1},{3,2},{5,4},{6,5},{7,6},{9,8},{10,9},{11,10},{13,12},{... | collective-permute-start | bytes 1572872 | tf_op jit(solution)/shard_map/ppermute | solution.py:32
  197.4 145.8 %copy-start.12 = (bf16[768,768,1]{1,0,2:T(8,128)(2,1)}, bf16[768,768,1]{1,0,2:T(8,128)(2,1)S(1)}, u32[]{:S(2)}) copy-start(bf16[768,768,1]{1,0,2:T(8,128)(2,1)S(1)} %reshape.748) | copy-start | bytes 3538948
  261.5 8.1 copy-start.20
  279.2 40.0 %slice-start = ((bf16[2,64,2304]{2,1,0:T(8,128)(2,1)}), bf16[2,64,768]{2,1,0:T(8,128)(2,1)S(1)}, s32[]{:S(2)}) async-start(bf16[2,64,2304]{2,1,0:T(8,128)(2,1)} %copy-done.37), calls=%async_computation.28 | async-start | bytes 393216 | tf_op jit(solution)/shard_map/slice | solution.py:271
  349.0 174.7 %copy-start.44 = (bf16[2,64,768]{2,1,0:T(8,128)(2,1)}, bf16[2,64,768]{2,1,0:T(8,128)(2,1)S(1)}, u32[]{:S(2)}) copy-start(bf16[2,64,768]{2,1,0:T(8,128)(2,1)S(1)} %convolution_convert_fusion.7) | copy-start | bytes 589828
  523.8 7.3 copy-start.11
  535.8 21.2 %copy-start.19 = (f32[2,256,768]{2,1,0:T(8,128)}, f32[2,256,768]{2,1,0:T(8,128)S(1)}, u32[]{:S(2)}) copy-start(f32[2,256,768]{2,1,0:T(8,128)S(1)} %convert_subtract_fusion) | copy-start | bytes 4718596
  538.3 5.6 copy-start.53
  538.3 5.6 copy-start.54
  582.8 185.1 %reduce-scatter.14.cloned.1.call-start = ((), (), s32[]{:S(2)}) async-start(), calls=%async_computation.21 | async-start | bytes 1622016 | tf_op jit(solution)/shard_map/reduce_scatter | solution.py:403
  588.8 232.9 %reduce-scatter.18.cloned.1.call-start = ((), (), s32[]{:S(2)}) async-start(), calls=%async_computation.23 | async-start | bytes 2433024 | tf_op jit(solution)/shard_map/reduce_scatter | solution.py:405
  595.5 332.0 %reduce-scatter.22.cloned.1.call-start = ((), (), s32[]{:S(2)}) async-start(), calls=%async_computation.25 | async-start | bytes 3244032 | tf_op jit(solution)/shard_map/reduce_scatter | solution.py:407
  605.1 433.9 %reduce-scatter.12.cloned.1.call-start = ((), (), s32[]{:S(2)}) async-start(), calls=%async_computation.20 | async-start | bytes 4866048 | tf_op jit(solution)/shard_map/reduce_scatter | solution.py:402
  620.7 6.8 copy-start.63
  637.8 8.0 copy-start.10
  641.7 8.5 collective-permute-start.2
  644.6 5.6 collective-permute-start.3
  662.8 496.1 %reduce-scatter.20.cloned.1.call-start = ((), (), s32[]{:S(2)}) async-start(), calls=%async_computation.24 | async-start | bytes 6488064 | tf_op jit(solution)/shard_map/reduce_scatter | solution.py:406
  676.2 606.7 %reduce-scatter.16.cloned.1.call-start = ((), (), s32[]{:S(2)}) async-start(), calls=%async_computation.22 | async-start | bytes 7299072 | tf_op jit(solution)/shard_map/reduce_scatter | solution.py:404
  693.8 750.7 %reduce-scatter.26.cloned.1.call-start = ((), (), s32[]{:S(2)}) async-start(), calls=%async_computation.27 | async-start | bytes 12976128 | tf_op jit(solution)/shard_map/reduce_scatter | solution.py:409
  714.4 980.8 %reduce-scatter.24.cloned.1.call-start = ((), (), s32[]{:S(2)}) async-start(), calls=%async_computation.26 | async-start | bytes 25952256 | tf_op jit(solution)/shard_map/reduce_scatter | solution.py:408
  762.3 5.5 copy-start.106
  762.3 7.1 copy-start.73
  764.0 165.0 %all-to-all-start.1 = ((bf16[2,1,256,768]{3,0,1,2:T(2,128)(2,1)}), bf16[2,1,256,768]{3,0,1,2:T(2,128)(2,1)S(1)}, u32[]{:S(2)}, u32[]{:S(2)}) async-start(bf16[2,1,256,768]{3,0,1,2:T(2,128)(2,1)} %copy.157), calls=%async_computation.2 | async-start | bytes 1572864 | tf_op jit(solution)/shard_map/all_to_all | solution.py:386
  931.2 766.1 %copy-start.1 = (bf16[16,1,32,768]{3,2,1,0:T(8,128)(2,1)S(1)}, bf16[16,1,32,768]{3,2,1,0:T(8,128)(2,1)}, u32[]{:S(2)}) copy-start(bf16[16,1,32,768]{3,2,1,0:T(8,128)(2,1)} %param.19) | copy-start | bytes 2359300
  (69 other events, 156.9 us)
Sparse Core Ops, SparseCore 0:
  11.5 67.0 all-gather.10
  82.1 57.6 all-gather.8
  142.7 52.1 all-gather.14
  198.1 53.8 all-gather.18
  255.3 57.8 all-gather.16
  315.2 18.4 all-gather.12
  337.1 69.5 all-gather.22
  409.5 94.4 all-gather.20
  582.9 26.4 reduce-scatter.9
  615.3 97.0 reduce-scatter.13
  718.5 103.1 reduce-scatter.17
  827.0 100.4 reduce-scatter.21
  933.0 105.9 reduce-scatter.11
  1045.4 113.4 reduce-scatter.19
  1164.4 118.4 reduce-scatter.15
  1289.8 154.5 reduce-scatter.25
  1450.7 244.4 reduce-scatter.23
where the time goes:
time: 1720 us; the launch traced here: 1710 us
  waiting for transfers between devices  1140 us (66%)
  local copies, waits for them, and re-layouts  221 us (13%)
  matrix products  137 us (8%)
  blocking collectives  133 us (8%)
  other arithmetic  37.8 us (2%)
  starting transfers between devices  21 us (1%)
  between operations  18.2 us (1%)
    reduce_scatter x1, waiting for transfers between devices, local(): lax.psum_scatter(grad_flat[8], ('dp', 'fsdp'), scatter_dimension=0, tiled...  249 us
    reduce_scatter x1, waiting for transfers between devices, local(): lax.psum_scatter(grad_flat[9], ('dp', 'fsdp'), scatter_dimension=0, tiled...  160 us
    reduce_scatter x1, waiting for transfers between devices, local(): lax.psum_scatter(grad_flat[4], ('dp', 'fsdp'), scatter_dimension=0, tiled...  122 us
    reduce_scatter x1, waiting for transfers between devices, local(): lax.psum_scatter(grad_flat[6], ('dp', 'fsdp'), scatter_dimension=0, tiled...  118 us
    reduce_scatter x1, waiting for transfers between devices, local(): lax.psum_scatter(grad_flat[2], ('dp', 'fsdp'), scatter_dimension=0, tiled...  105 us
    reduce_scatter x1, waiting for transfers between devices, local(): lax.psum_scatter(grad_flat[7], ('dp', 'fsdp'), scatter_dimension=0, tiled...  104 us
    all_gather x1, waiting for transfers between devices, local(): lax.all_gather(flat_fwd[8], ('dp', 'fsdp'), axis=0, tiled=True)  85.7 us
    reshape x16, local copies, waits for them, and re-layouts, flat_lanes(): return matrix.reshape(-1, 128)  81.9 us
  transfers between devices with their start and end apart: 23, of which 14 were waited for; matrix products, arithmetic and copies ran while one was open for 18% of the time, Pallas kernels for 0%

commit v1 on v0

v1 whole, which is shorter than its diff:
```python
import functools
import jax
import jax.numpy as jnp
from jax import lax
from jax.experimental import pallas as pl
from jax.experimental.pallas import tpu as pltpu
from jax.sharding import PartitionSpec as P

D = 768
HL = 8
HH = 12
DH = 64
FL = 1024
FH = 4096
WIN = 128
CAP = 64

EPSILON = 1e-06
MASKED = -1000000000.0
SCORE_SCALE = 0.125
MESH = pl.DeviceIdType.MESH
BF = jnp.bfloat16
F32 = jnp.float32
ANY = pl.BlockSpec(memory_space=pl.ANY)
VM = pl.BlockSpec(memory_space=pltpu.VMEM)
DMA = pltpu.SemaphoreType.DMA
VMEM_BYTES = 60 * 1024 * 1024


def place():
    d = lax.axis_index("dp")
    f = lax.axis_index("fsdp")
    return d // 2, d % 2, f // 2, f % 2


def at(hi, lo, x, c):
    return (hi * 2 + lo, x * 2 + c)


def meet(peers):
    barrier = pltpu.get_barrier_semaphore()
    for peer in peers:
        pl.semaphore_signal(barrier, inc=1, device_id=peer, device_id_type=MESH)
    pl.semaphore_wait(barrier, len(peers))


def send(src, dst, send_sem, recv_sem, peer):
    copy = pltpu.make_async_remote_copy(
        src_ref=src,
        dst_ref=dst,
        send_sem=send_sem,
        recv_sem=recv_sem,
        device_id=peer,
        device_id_type=MESH,
    )
    copy.start()
    return copy


def keep(src, dst, sem):
    copy = pltpu.make_async_copy(src, dst, sem)
    copy.start()
    return copy


def quad_peers():
    hi, lo, x, c = place()
    return [(lo, 1 - x), (1 - lo, x), (1 - lo, 1 - x)]


def call(kernel, out_shape, operands, in_specs, out_specs, scratch, collective_id):
    return pl.pallas_call(
        kernel,
        out_shape=out_shape,
        in_specs=in_specs,
        out_specs=out_specs,
        scratch_shapes=scratch,
        compiler_params=pltpu.CompilerParams(
            collective_id=collective_id, has_side_effects=True, vmem_limit_bytes=VMEM_BYTES
        ),
    )(*operands)


def deal_kernel(deal_ref, x_ref, o_ref, sem):
    count = o_ref.shape[0]

    def begin(i, carry):
        pltpu.make_async_copy(x_ref.at[deal_ref[i]], o_ref.at[i], sem.at[i]).start()
        return carry

    def finish(i, carry):
        pltpu.make_async_copy(x_ref.at[deal_ref[i]], o_ref.at[i], sem.at[i]).wait()
        return carry

    lax.fori_loop(0, count, begin, 0)
    lax.fori_loop(0, count, finish, 0)


def deal_rows(dealing, rows):
    return pl.pallas_call(
        deal_kernel,
        out_shape=jax.ShapeDtypeStruct(rows.shape, rows.dtype),
        in_specs=[pl.BlockSpec(memory_space=pltpu.SMEM), ANY],
        out_specs=ANY,
        scratch_shapes=[DMA((rows.shape[0],))],
    )(dealing, rows)


def undeal_kernel(deal_ref, x_ref, o_ref):
    def body(i, carry):
        o_ref[deal_ref[i]] = x_ref[i].astype(F32)
        return carry

    lax.fori_loop(0, x_ref.shape[0], body, 0)


def undeal_rows(dealing, rows):
    return pl.pallas_call(
        undeal_kernel,
        out_shape=jax.ShapeDtypeStruct(rows.shape, F32),
        in_specs=[pl.BlockSpec(memory_space=pltpu.SMEM), VM],
        out_specs=VM,
        compiler_params=pltpu.CompilerParams(vmem_limit_bytes=VMEM_BYTES),
    )(dealing, rows)


def packed(matrix):
    rows, columns = matrix.shape
    if rows % 8 == 0:
        return matrix
    return matrix.reshape(rows * columns // 128, 128)


def unpacked(gathered, rows, columns):
    return gathered.reshape(-1, rows, columns).reshape(-1, columns)


def gather_kernel(dp, nw, *refs):
    nz = dp // 2
    xin, ws, hin, hdn = refs[0], refs[1 : 1 + nw], refs[1 + nw], refs[2 + nw]
    outs = refs[3 + nw :]
    xo, wos, hin_o, hdn_o = outs[0], outs[1 : 1 + nw], outs[1 + nw], outs[2 + nw]
    loc, xs, xr, zs, zr, ps, pr, cs, cr, hs, hr = outs[3 + nw :]
    hi, lo, x, c = place()
    d = hi * 2 + lo
    f = x * 2 + c
    plane = (lo * 2 + x) * 2 + c
    group = xin.shape[0] // dp
    dp_peers = [(lax.rem(d + k, dp), f) for k in range(1, dp)]
    rest = [(a, b, e) for a in (0, 1) for b in (0, 1) for e in (0, 1) if a or b or e]
    flat8 = []
    for a, b, e in rest:
        l2 = 1 - lo if a else lo
        x2 = 1 - x if b else x
        c2 = 1 - c if e else c
        flat8.append((l2, x2, c2))
    meet(dp_peers + [at(hi, *p) for (a, b, e), p in zip(rest, flat8) if b or e])
    locals_ = [keep(ws[w], wos[w].at[hi, lo, x, c], loc.at[w]) for w in range(nw)]
    locals_.append(keep(xin.at[pl.ds(d * group, group)], xo.at[:, d], loc.at[nw]))
    locals_.append(keep(hin.at[plane], hin_o.at[hi, plane], loc.at[nw + 1]))
    locals_.append(keep(hdn, hdn_o.at[hi], loc.at[nw + 2]))
    x_sends = []
    for k, peer in enumerate(dp_peers):
        x_sends.append(
            send(xin.at[pl.ds(peer[0] * group, group)], xo.at[:, d], xs.at[k], xr.at[k], peer)
        )
    z_peers = [at(lax.rem(hi + k, nz), lo, x, c) for k in range(1, nz)]
    z_sends = [
        [
            send(ws[w], wos[w].at[hi, lo, x, c], zs.at[w, k], zr.at[w, k], peer)
            for k, peer in enumerate(z_peers)
        ]
        for w in range(nw)
    ]
    h_sends = []
    for k, (l2, x2, c2) in enumerate(flat8):
        h_sends.append(
            send(
                hin.at[(l2 * 2 + x2) * 2 + c2],
                hin_o.at[hi, plane],
                hs.at[0, k],
                hr.at[0, k],
                at(hi, l2, x2, c2),
            )
        )
    quad = quad_peers()
    partner = at(hi, lo, x, 1 - c)
    p_sends, c_sends = [], []

    def forward_plane(w):
        locals_[w].wait()
        for copy in z_sends[w]:
            copy.wait()
        column = wos[w].at[:, lo, x, c]
        p_sends.append(
            [
                send(column, column, ps.at[w, k], pr.at[w, k], at(hi, l2, x2, c))
                for k, (l2, x2) in enumerate(quad)
            ]
        )
        c_sends.append([send(column, column, cs.at[w, 0], cr.at[w, 0], partner)])

    def forward_core(w):
        for k, (l2, x2) in enumerate(quad):
            p_sends[w][k].wait()
            column = wos[w].at[:, l2, x2, c]
            c_sends[w].append(send(column, column, cs.at[w, k + 1], cr.at[w, k + 1], partner))

    for w in range(nw):
        forward_plane(w)
        if w >= 1:
            forward_core(w - 1)
    for copy in h_sends:
        copy.wait()
    locals_[nw + 1].wait()
    late = []
    for k, peer in enumerate(z_peers):
        late.append(send(hin_o.at[hi], hin_o.at[hi], hs.at[1, k], hr.at[1, k], peer))
        late.append(send(hdn, hdn_o.at[hi], hs.at[2, k], hr.at[2, k], peer))
    forward_core(nw - 1)
    locals_[nw].wait()
    locals_[nw + 2].wait()
    for copy in x_sends + late:
        copy.wait()
    for copies in c_sends:
        for copy in copies:
            copy.wait()


def gather_all(dp, xin, weights, hin, hdn):
    nz = dp // 2
    nw = len(weights)
    seqs, rows, _ = xin.shape
    shapes = [jax.ShapeDtypeStruct((seqs // dp, dp, rows, D), BF)]
    shapes += [jax.ShapeDtypeStruct((nz, 2, 2, 2) + w.shape, BF) for w in weights]
    shapes.append(jax.ShapeDtypeStruct((nz,) + hin.shape, BF))
    shapes.append(jax.ShapeDtypeStruct((nz,) + hdn.shape, BF))
    most = max(7, nz)
    scratch = [
        DMA((nw + 3,)),
        DMA((dp,)),
        DMA((dp,)),
        DMA((nw, nz)),
        DMA((nw, nz)),
        DMA((nw, 3)),
        DMA((nw, 3)),
        DMA((nw, 4)),
        DMA((nw, 4)),
        DMA((3, most)),
        DMA((3, most)),
    ]
    return call(
        functools.partial(gather_kernel, dp, nw),
        shapes,
        [xin, *weights, hin, hdn],
        [ANY] * (3 + nw),
        [ANY] * (3 + nw),
        scratch,
        1,
    )


def rim_exchange(left, right, from_left, from_right, ls, lr, rs, rr):
    d = lax.axis_index("dp")
    f = lax.axis_index("fsdp")
    last = lax.axis_size("fsdp") - 1

    def down():
        return pltpu.make_async_remote_copy(
            src_ref=left,
            dst_ref=from_right,
            send_sem=ls,
            recv_sem=lr,
            device_id=(d, lax.max(f - 1, 0)),
            device_id_type=MESH,
        )

    def up():
        return pltpu.make_async_remote_copy(
            src_ref=right,
            dst_ref=from_left,
            send_sem=rs,
            recv_sem=rr,
            device_id=(d, lax.min(f + 1, last)),
            device_id_type=MESH,
        )

    @pl.when(f > 0)
    def _():
        down().start()

    @pl.when(f < last)
    def _():
        up().start()

    @pl.when(f == 0)
    def _():
        from_left[...] = jnp.zeros(from_left.shape, from_left.dtype)

    @pl.when(f == last)
    def _():
        from_right[...] = jnp.zeros(from_right.shape, from_right.dtype)

    def finish():
        @pl.when(f > 0)
        def _():
            down().wait_send()
            up().wait_recv()

        @pl.when(f < last)
        def _():
            up().wait_send()
            down().wait_recv()

    return finish


def line_peers():
    hi, lo, x, c = place()
    return [at(hi, lo, x, 1 - c), at(hi, lo, 1 - x, c), at(hi, lo, 1 - x, 1 - c)]


def keys_kernel(left, right, kv, from_left, from_right, every, own, ls, lr, rs, rr, ss, sr):
    hi, lo, x, c = place()
    f = x * 2 + c
    meet(line_peers())
    finish = rim_exchange(left, right, from_left, from_right, ls, lr, rs, rr)
    mine = keep(kv, every.at[:, f], own)
    across = send(kv, every.at[:, f], ss.at[0], sr.at[0], at(hi, lo, 1 - x, c))
    beside = send(kv, every.at[:, f], ss.at[1], sr.at[1], at(hi, lo, x, 1 - c))
    across.wait()
    other = every.at[:, (1 - x) * 2 + c]
    relay = send(other, other, ss.at[2], sr.at[2], at(hi, lo, x, 1 - c))
    mine.wait()
    beside.wait()
    relay.wait()
    finish()


def exchange_keys(left, right, kv):
    group, cap, width = kv.shape
    return call(
        keys_kernel,
        [
            jax.ShapeDtypeStruct(left.shape, BF),
            jax.ShapeDtypeStruct(right.shape, BF),
            jax.ShapeDtypeStruct((group, 4, cap, width), BF),
        ],
        [left, right, kv],
        [VM] * 3,
        [VM] * 3,
        [DMA, DMA, DMA, DMA, DMA, DMA((3,)), DMA((3,))],
        2,
    )


def key_grads_kernel(left, right, part, from_left, from_right, total, got, far, ls, lr, rs, rr, ss, sr):
    hi, lo, x, c = place()
    meet(line_peers())
    finish = rim_exchange(left, right, from_left, from_right, ls, lr, rs, rr)
    beside = [
        send(
            part.at[:, b * 2 + 1 - c], got.at[b], ss.at[b], sr.at[b], at(hi, lo, x, 1 - c)
        )
        for b in (0, 1)
    ]
    for copy in beside:
        copy.wait()
    for b in (0, 1):
        got[b] = (got[b].astype(F32) + part[:, b * 2 + c].astype(F32)).astype(BF)
    across = send(got.at[1 - x], far, ss.at[2], sr.at[2], at(hi, lo, 1 - x, c))
    across.wait()
    total[...] = got[x].astype(F32) + far[...].astype(F32)
    finish()


def exchange_key_grads(left, right, part):
    group, _, cap, width = part.shape
    return call(
        key_grads_kernel,
        [
            jax.ShapeDtypeStruct(left.shape, BF),
            jax.ShapeDtypeStruct(right.shape, BF),
            jax.ShapeDtypeStruct((group, cap, width), F32),
        ],
        [left, right, part],
        [VM] * 3,
        [VM] * 3,
        [
            pltpu.VMEM((2, group, cap, width), BF),
            pltpu.VMEM((group, cap, width), BF),
            DMA,
            DMA,
            DMA,
            DMA,
            DMA((3,)),
            DMA((3,)),
        ],
        3,
    )


def plane_meet():
    hi, lo, x, c = place()
    meet([at(hi, l2, x2, c) for l2, x2 in quad_peers()] + [at(hi, lo, x, 1 - c)])


def plane_gather_kernel(rows, every, own, ss, sr, cs, cr):
    hi, lo, x, c = place()
    quad = quad_peers()
    partner = at(hi, lo, x, 1 - c)
    plane_meet()
    spot = every.at[lo, x, c]
    mine = keep(rows, spot, own)
    out = [
        send(rows, spot, ss.at[k], sr.at[k], at(hi, l2, x2, c)) for k, (l2, x2) in enumerate(quad)
    ]
    back = [send(rows, spot, cs.at[3], cr.at[3], partner)]
    for k, (l2, x2) in enumerate(quad):
        out[k].wait()
        other = every.at[l2, x2, c]
        back.append(send(other, other, cs.at[k], cr.at[k], partner))
    mine.wait()
    for copy in back:
        copy.wait()


def plane_gather(rows, collective_id):
    return call(
        plane_gather_kernel,
        jax.ShapeDtypeStruct((2, 2, 2) + rows.shape, BF),
        [rows],
        [ANY],
        ANY,
        [DMA, DMA((3,)), DMA((3,)), DMA((4,)), DMA((4,))],
        collective_id,
    )


def plane_sum_kernel(part, total, near, far, ss, sr, cs, cr):
    hi, lo, x, c = place()
    quad = quad_peers()
    partner = at(hi, lo, x, 1 - c)
    plane_meet()
    spots = quad + [(lo, x)]
    back = [
        send(part.at[l2, x2, 1 - c], near.at[l2, x2], cs.at[k], cr.at[k], partner)
        for k, (l2, x2) in enumerate(spots)
    ]
    out = []
    for k, (l2, x2) in enumerate(spots):
        back[k].wait()
        near[l2, x2] = (near[l2, x2].astype(F32) + part[l2, x2, c].astype(F32)).astype(BF)
        if k < 3:
            out.append(
                send(near.at[l2, x2], far.at[k], ss.at[k], sr.at[k], at(hi, l2, x2, c))
            )
    for copy in out:
        copy.wait()
    total[...] = (
        near[lo, x].astype(F32)
        + far[0].astype(F32)
        + far[1].astype(F32)
        + far[2].astype(F32)
    )


def plane_sum(part, collective_id):
    shape = part.shape[3:]
    return call(
        plane_sum_kernel,
        jax.ShapeDtypeStruct(shape, F32),
        [part],
        [VM],
        VM,
        [
            pltpu.VMEM((2, 2) + shape, BF),
            pltpu.VMEM((3,) + shape, BF),
            DMA((3,)),
            DMA((3,)),
            DMA((4,)),
            DMA((4,)),
        ],
        collective_id,
    )


def scatter_kernel(dp, nw, *refs):
    nz = dp // 2
    dx, stats, gs, hin, hdn = refs[0], refs[1], refs[2 : 2 + nw], refs[2 + nw], refs[3 + nw]
    outs = refs[4 + nw :]
    dxo, total, gos, hin_o, hdn_o = outs[0], outs[1], outs[2 : 2 + nw], outs[2 + nw], outs[3 + nw]
    scr = outs[4 + nw :]
    nears, fars, sums, ends = (scr[i * nw : (i + 1) * nw] for i in range(4))
    hin_r, hin_s, hdn_r, sc, sp, sz, acc, acc2 = scr[4 * nw : 4 * nw + 8]
    own, xs, xr, cs, cr, ps, pr, zs, zr, hs, hr, ts, tr = scr[4 * nw + 8 :]
    hi, lo, x, c = place()
    d = hi * 2 + lo
    f = x * 2 + c
    plane = (lo * 2 + x) * 2 + c
    dp_peers = [(lax.rem(d + k, dp), f) for k in range(1, dp)]
    rest = [(a, b, e) for a in (0, 1) for b in (0, 1) for e in (0, 1) if a or b or e]
    flat8 = []
    for a, b, e in rest:
        l2 = 1 - lo if a else lo
        x2 = 1 - x if b else x
        c2 = 1 - c if e else c
        flat8.append((l2, x2, c2))
    meet(dp_peers + [at(hi, *p) for (a, b, e), p in zip(rest, flat8) if b or e])
    partner = at(hi, lo, x, 1 - c)
    quad = quad_peers()
    z_index = [lax.rem(hi + k, nz) for k in range(1, nz)]
    z_peers = [at(z, lo, x, c) for z in z_index]
    c_sends = [
        send(gs[w].at[:, :, :, 1 - c], nears[w], cs.at[w], cr.at[w], partner) for w in range(nw)
    ]
    t_c = send(stats, sc, ts.at[0], tr.at[0], partner)
    mine = keep(dx.at[:, d], dxo.at[d], own)
    x_sends = [
        send(dx.at[:, peer[0]], dxo.at[d], xs.at[k], xr.at[k], peer)
        for k, peer in enumerate(dp_peers)
    ]
    h_sends = []
    for k, z in enumerate(z_index):
        h_sends.append(send(hin.at[z], hin_r.at[k], hs.at[1, k], hr.at[1, k], z_peers[k]))
        h_sends.append(send(hdn.at[z], hdn_r.at[k], hs.at[2, k], hr.at[2, k], z_peers[k]))
    p_sends, z_sends = [], []
    t_c.wait()
    acc[...] = stats[...] + sc[...]
    t_p = [
        send(acc, sp.at[k], ts.at[1 + k], tr.at[1 + k], at(hi, l2, x2, c))
        for k, (l2, x2) in enumerate(quad)
    ]

    def add_core(w):
        c_sends[w].wait()
        near, g = nears[w], gs[w]

        def body(i, carry):
            z, a, b = i // 4, (i // 2) % 2, i % 2
            near[z, a, b] = (near[z, a, b].astype(F32) + g[z, a, b, c].astype(F32)).astype(BF)
            return carry

        lax.fori_loop(0, nz * 4, body, 0)
        p_sends.append(
            [
                send(near.at[:, l2, x2], fars[w].at[k], ps.at[w, k], pr.at[w, k], at(hi, l2, x2, c))
                for k, (l2, x2) in enumerate(quad)
            ]
        )

    def add_plane(w):
        for copy in p_sends[w]:
            copy.wait()
        near, far, part = nears[w], fars[w], sums[w]

        def body(z, carry):
            part[z] = (
                near[z, lo, x].astype(F32)
                + far[0, z].astype(F32)
                + far[1, z].astype(F32)
                + far[2, z].astype(F32)
            ).astype(BF)
            return carry

        lax.fori_loop(0, nz, body, 0)
        z_sends.append(
            [
                send(part.at[z], ends[w].at[k], zs.at[w, k], zr.at[w, k], z_peers[k])
                for k, z in enumerate(z_index)
            ]
        )

    def add_line(w):
        for copy in z_sends[w]:
            copy.wait()
        gos[w][...] = sums[w][hi].astype(F32)
        for k in range(nz - 1):
            gos[w][...] += ends[w][k].astype(F32)

    for w in range(nw):
        add_core(w)
        if w >= 2:
            add_plane(w - 2)
    for copy in t_p:
        copy.wait()
    acc2[...] = acc[...] + sp[0] + sp[1] + sp[2]
    t_z = [send(acc2, sz.at[k], ts.at[4 + k], tr.at[4 + k], z_peers[k]) for k in range(nz - 1)]
    for copy in h_sends:
        copy.wait()

    def body(i, carry):
        value = hin[hi, i].astype(F32)
        for k in range(nz - 1):
            value += hin_r[k, i].astype(F32)
        hin_s[i] = value.astype(BF)
        return carry

    lax.fori_loop(0, 8, body, 0)
    hin_o[plane] = hin_s[plane]
    a_sends = [
        send(
            hin_s.at[(l2 * 2 + x2) * 2 + c2],
            hin_o.at[plane],
            hs.at[0, k],
            hr.at[0, k],
            at(hi, l2, x2, c2),
        )
        for k, (l2, x2, c2) in enumerate(flat8)
    ]
    hdn_o[...] = hdn[hi].astype(F32)
    for k in range(nz - 1):
        hdn_o[...] += hdn_r[k].astype(F32)
    for w in range(max(nw - 2, 0), nw):
        add_plane(w)
    for copy in t_z:
        copy.wait()
    total[...] = acc2[...]
    for k in range(nz - 1):
        total[...] += sz[k]
    for w in range(nw):
        add_line(w)
    mine.wait()
    for copy in x_sends + a_sends:
        copy.wait()


def scatter_all(dp, dx, stats, grads, hin, hdn):
    nz = dp // 2
    nw = len(grads)
    group, _, rows, _ = dx.shape
    tiles = [g.shape[4:] for g in grads]
    most = max(7, nz)
    scratch = [pltpu.VMEM((nz, 2, 2) + t, BF) for t in tiles]
    scratch += [pltpu.VMEM((3, nz) + t, BF) for t in tiles]
    scratch += [pltpu.VMEM((nz,) + t, BF) for t in tiles]
    scratch += [pltpu.VMEM((nz - 1,) + t, BF) for t in tiles]
    scratch += [
        pltpu.VMEM((nz - 1,) + hin.shape[1:], BF),
        pltpu.VMEM(hin.shape[1:], BF),
        pltpu.VMEM((nz - 1,) + hdn.shape[1:], BF),
        pltpu.VMEM(stats.shape, F32),
        pltpu.VMEM((3,) + stats.shape, F32),
        pltpu.VMEM((nz - 1,) + stats.shape, F32),
        pltpu.VMEM(stats.shape, F32),
        pltpu.VMEM(stats.shape, F32),
        DMA,
        DMA((dp,)),
        DMA((dp,)),
        DMA((nw,)),
        DMA((nw,)),
        DMA((nw, 3)),
        DMA((nw, 3)),
        DMA((nw, nz)),
        DMA((nw, nz)),
        DMA((3, most)),
        DMA((3, most)),
        DMA((4 + nz,)),
        DMA((4 + nz,)),
    ]
    shapes = [jax.ShapeDtypeStruct((dp, group, rows, D), BF), jax.ShapeDtypeStruct(stats.shape, F32)]
    shapes += [jax.ShapeDtypeStruct(t, F32) for t in tiles]
    shapes.append(jax.ShapeDtypeStruct(hin.shape[1:], BF))
    shapes.append(jax.ShapeDtypeStruct(hdn.shape[1:], F32))
    return call(
        functools.partial(scatter_kernel, dp, nw),
        shapes,
        [dx, stats, *grads, hin, hdn],
        [ANY] + [VM] * (3 + nw),
        [ANY] + [VM] * (3 + nw),
        scratch,
        4,
    )


def rms_norm(value, gain):
    return value * lax.rsqrt(jnp.mean(value * value, axis=-1, keepdims=True) + EPSILON) * gain


def geglu(gate, upper):
    return jax.nn.gelu(gate, approximate=True) * upper


def geglu_back(up_proj, d_act):
    half_width = up_proj.shape[-1] // 2
    _, pullback = jax.vjp(geglu, up_proj[..., :half_width], up_proj[..., half_width:])
    d_gate, d_upper = pullback(d_act)
    return jnp.concatenate([d_gate, d_upper], axis=-1).astype(BF)


def split_heads(rows, heads):
    return rows.reshape(rows.shape[0], rows.shape[1], heads, -1)


def head_scores(queries, key_rows, allowed, heads):
    scores = (
        jnp.einsum(
            "sqhd,skhd->shqk",
            split_heads(queries, heads),
            split_heads(key_rows, heads),
            preferred_element_type=F32,
        )
        * SCORE_SCALE
    )
    return jnp.where(allowed[:, None], scores, MASKED)


def attend_forward(queries, key_rows, value_rows, allowed, heads):
    scores = head_scores(queries, key_rows, allowed, heads)
    row_max = jnp.max(scores, axis=-1, keepdims=True)
    shifted = jnp.exp(scores - row_max)
    row_sum = jnp.sum(shifted, axis=-1, keepdims=True)
    attn_prob = (shifted / row_sum).astype(BF)
    attended = jnp.einsum(
        "shqk,skhd->sqhd", attn_prob, split_heads(value_rows, heads), preferred_element_type=F32
    )
    return (attended.reshape(queries.shape).astype(BF), row_max + jnp.log(row_sum))


def attend_backward(queries, key_rows, value_rows, allowed, log_sum, d_attended, heads):
    scores = head_scores(queries, key_rows, allowed, heads)
    attn_prob = jnp.exp(scores - log_sum)
    d_heads = split_heads(d_attended, heads)
    d_prob = jnp.einsum(
        "sqhd,skhd->shqk", d_heads, split_heads(value_rows, heads), preferred_element_type=F32
    )
    row_dot = jnp.sum(attn_prob * d_prob, axis=-1, keepdims=True)
    d_scores = (attn_prob * (d_prob - row_dot)).astype(BF)
    d_query = (
        jnp.einsum(
            "shqk,skhd->sqhd", d_scores, split_heads(key_rows, heads), preferred_element_type=F32
        )
        * SCORE_SCALE
    )
    d_key = (
        jnp.einsum(
            "shqk,sqhd->skhd", d_scores, split_heads(queries, heads), preferred_element_type=F32
        )
        * SCORE_SCALE
    )
    d_value = jnp.einsum(
        "shqk,sqhd->skhd", attn_prob.astype(BF), d_heads, preferred_element_type=F32
    )
    return (
        d_query.reshape(queries.shape),
        d_key.reshape(key_rows.shape),
        d_value.reshape(value_rows.shape),
    )


def mul(left, right):
    return jnp.einsum("...d,de->...e", left, right, preferred_element_type=F32)


def mul_back(left, right):
    return jnp.einsum("...e,de->...d", left, right, preferred_element_type=F32)


def weight_grad(left, right):
    a = left.reshape(-1, left.shape[-1])
    b = right.reshape(-1, right.shape[-1])
    return jnp.einsum("pd,pe->de", a, b, preferred_element_type=F32)


def pick(spec, hot, value):
    high = value.astype(BF)
    rest = (value - high.astype(F32)).astype(BF)
    return jnp.einsum(spec, hot, high, preferred_element_type=F32) + jnp.einsum(
        spec, hot, rest, preferred_element_type=F32
    )


def routing(routes, pieces, piece_len):
    places = jnp.arange(pieces * piece_len)
    routed = jnp.any(routes[:, None, :] == places[None, :, None], axis=-1)
    routed = routed.reshape(-1, pieces, piece_len)
    before = jnp.arange(piece_len)[:, None] < jnp.arange(piece_len)[None, :]
    rank = jnp.einsum(
        "skp,pq->skq", routed.astype(BF), before.astype(BF), preferred_element_type=F32
    )
    slots = jnp.arange(CAP, dtype=F32)
    hot = routed[:, :, None, :] & (rank[:, :, None, :] == slots[None, None, :, None])
    filled = jnp.any(hot, axis=-1)
    spots = jnp.sum(jnp.where(hot, places.reshape(1, pieces, 1, piece_len), 0), axis=-1)
    return hot, jnp.where(filled, spots, -1)


def local(
    layer_input,
    teacher,
    lengths,
    dealing,
    attn_routes,
    ffn_routes,
    ffn_scores,
    gain_attn,
    gain_ffn,
    light_qkv,
    light_out,
    heavy_qkv,
    heavy_out,
    light_in,
    light_down,
    heavy_in,
    heavy_down,
):
    dp = lax.axis_size("dp")
    pieces = lax.axis_size("fsdp")
    data_index = lax.axis_index("dp")
    piece = lax.axis_index("fsdp")
    nz = dp // 2
    n = dp * pieces
    seqs = dealing.shape[0]
    group = seqs // dp
    gain_len = gain_attn.shape[0]
    hidden_units = heavy_in.shape[1] // 2 // n
    xin = deal_rows(dealing, layer_input[:, 0])
    gains = jnp.pad(
        jnp.stack([gain_attn, gain_ffn]), ((0, 6), (0, 128 - gain_len))
    )
    matrices = (light_qkv, heavy_qkv, light_out, heavy_out, light_in, light_down)
    hin_rows = heavy_in.shape[0]
    hin_src = (
        heavy_in.reshape(hin_rows, 2, nz, 8, hidden_units)
        .transpose(3, 0, 1, 2, 4)
        .reshape(8, hin_rows, 2 * nz * hidden_units)
    )
    if hin_rows % 8:
        hin_src = hin_src.reshape(8, -1, 128)
    got = gather_all(dp, xin, [gains] + [packed(m) for m in matrices], hin_src, heavy_down)
    tokens = layer_input.shape[2] * dp
    inputs = got[0].reshape(group, tokens, D).astype(F32)
    gain_rows = got[1].reshape(n, 8, 128)
    gain_one = gain_rows[:, 0, :gain_len].reshape(-1).astype(F32)
    gain_two = gain_rows[:, 1, :gain_len].reshape(-1).astype(F32)
    w_lqkv, w_hqkv, w_lout, w_hout, w_lin, w_ldown = (
        unpacked(full, *m.shape) for full, m in zip(got[2:8], matrices)
    )
    w_hin = unpacked(got[8], hin_rows, 2 * nz * hidden_units)
    w_hdown = got[9].reshape(-1, D)
    chosen = lax.dynamic_slice_in_dim(dealing, data_index * group, group)
    one = (chosen[:, None] == jnp.arange(seqs)[None, :])
    seq_lengths = jnp.sum(jnp.where(one, lengths[None, :], 0), axis=1)
    attn_pick = jnp.sum(jnp.where(one[:, :, None], attn_routes[None], 0), axis=1)
    ffn_pick = jnp.sum(jnp.where(one[:, :, None], ffn_routes[None], 0), axis=1)
    score_pick = jnp.sum(jnp.where(one[:, :, None], ffn_scores[None], 0.0), axis=1)
    token_count = jnp.sum(lengths).astype(F32)
    positions = piece * tokens + jnp.arange(tokens)
    valid_mask = positions[None, :] < seq_lengths[:, None]
    a_hot, a_spots = routing(attn_pick, pieces, tokens)
    f_hot, f_spots = routing(ffn_pick, pieces, tokens)
    a_select = lax.dynamic_index_in_dim(a_hot, piece, 1, False).astype(BF)
    f_select = lax.dynamic_index_in_dim(f_hot, piece, 1, False).astype(BF)
    a_spot = lax.dynamic_index_in_dim(a_spots, piece, 1, False)
    f_spot = lax.dynamic_index_in_dim(f_spots, piece, 1, False)
    slot_score = jnp.sum(
        jnp.where(f_spot[:, :, None] == ffn_pick[:, None, :], score_pick[:, None, :], 0.0), axis=-1
    )
    targets = teacher[:, 0].astype(F32)
    width_light = HL * DH
    width_heavy = HH * DH
    normed = rms_norm(inputs, gain_one).astype(BF)
    light_proj = mul(normed, w_lqkv).astype(BF)
    l_query = light_proj[..., :width_light]
    own_pair = light_proj[..., width_light:]
    a_rows = jnp.einsum("scp,spd->scd", a_select, normed, preferred_element_type=F32).astype(BF)
    heavy_proj = mul(a_rows, w_hqkv).astype(BF)
    h_query = heavy_proj[..., :width_heavy]
    from_left, from_right, kv_every = exchange_keys(
        own_pair[:, :WIN], own_pair[:, tokens - WIN :], heavy_proj[..., width_heavy:]
    )
    rim_pair = jnp.concatenate([from_left, own_pair, from_right], axis=1)
    rim_keys = rim_pair[..., :width_light]
    rim_values = rim_pair[..., width_light:]
    key_pos = piece * tokens - WIN + jnp.arange(tokens + 2 * WIN)
    within_reach = (jnp.abs(positions[:, None] - key_pos[None, :]) <= WIN) & (key_pos >= 0)[None, :]
    live_key = key_pos[None, :] < seq_lengths[:, None]
    light_allowed = within_reach[None] & (
        live_key[:, None, :] | (positions[:, None] == key_pos[None, :])[None]
    )
    l_att, l_lse = attend_forward(l_query, rim_keys, rim_values, light_allowed, HL)
    light_branch = mul(l_att, w_lout)
    kv_every = kv_every.reshape(group, pieces * CAP, 2 * width_heavy)
    all_spots = a_spots.reshape(group, pieces * CAP)
    heavy_allowed = ((all_spots >= 0) & (all_spots < seq_lengths[:, None]))[:, None, :] | (
        a_spot[:, :, None] == all_spots[:, None, :]
    )
    hv_keys = kv_every[..., :width_heavy]
    hv_values = kv_every[..., width_heavy:]
    h_att, h_lse = attend_forward(h_query, hv_keys, hv_values, heavy_allowed, HH)
    heavy_branch = mul(h_att, w_hout)
    hidden = inputs + light_branch + pick("scp,scd->spd", a_select, heavy_branch)
    normed_two = rms_norm(hidden, gain_two).astype(BF)
    f_rows = jnp.einsum("scp,spd->scd", f_select, normed_two, preferred_element_type=F32).astype(BF)
    t_rows = plane_gather(f_rows.reshape(group * CAP, D), 5).reshape(-1, D)
    heavy_up = mul(t_rows, w_hin)
    half = heavy_up.shape[-1] // 2
    heavy_mid = geglu(heavy_up[..., :half], heavy_up[..., half:]).astype(BF)
    heavy_part = mul(heavy_mid, w_hdown).astype(BF)
    heavy_ffn = plane_sum(heavy_part.reshape(2, 2, 2, group * CAP, D), 6).reshape(group, CAP, D)
    light_up = mul(normed_two, w_lin)
    light_mid = geglu(light_up[..., :FL], light_up[..., FL:]).astype(BF)
    light_ffn = mul(light_mid, w_ldown)
    output = hidden + light_ffn + pick("scp,scd->spd", f_select, heavy_ffn * slot_score[..., None])
    misfit = output - targets
    weight_mask = valid_mask[..., None].astype(F32)
    partial_loss = jnp.sum(weight_mask * misfit * misfit)
    d_out = 2.0 * weight_mask * misfit / (D * token_count)
    d_heavy_ffn = (pick("scp,spd->scd", f_select, d_out) * slot_score[..., None]).astype(BF)
    t_grad = plane_gather(d_heavy_ffn.reshape(group * CAP, D), 7).reshape(-1, D)
    grad_hdown = weight_grad(heavy_mid, t_grad)
    d_heavy_mid = mul_back(t_grad, w_hdown)
    d_heavy_up = geglu_back(heavy_up, d_heavy_mid)
    grad_hin = weight_grad(t_rows, d_heavy_up)
    d_f_part = mul_back(d_heavy_up, w_hin).astype(BF)
    d_f_rows = plane_sum(d_f_part.reshape(2, 2, 2, group * CAP, D), 8).reshape(group, CAP, D)
    d_light = d_out.astype(BF)
    grad_ldown = weight_grad(light_mid, d_light)
    d_light_mid = mul_back(d_light, w_ldown)
    d_light_up = geglu_back(light_up, d_light_mid)
    grad_lin = weight_grad(normed_two, d_light_up)
    d_norm_two = pick("scp,scd->spd", f_select, d_f_rows) + mul_back(d_light_up, w_lin)
    _, second_pull = jax.vjp(rms_norm, hidden, gain_two)
    d_hidden_norm, grad_gain_two = second_pull(d_norm_two)
    d_hidden = d_out + d_hidden_norm
    d_heavy_attn = pick("scp,spd->scd", a_select, d_hidden).astype(BF)
    grad_hout = weight_grad(h_att, d_heavy_attn)
    d_h_att = mul_back(d_heavy_attn, w_hout).astype(BF)
    dq_heavy, dk_heavy, dv_heavy = attend_backward(
        h_query, hv_keys, hv_values, heavy_allowed, h_lse, d_h_att, HH
    )
    kv_part = jnp.concatenate([dk_heavy, dv_heavy], axis=-1).astype(BF)
    d_light_attn = d_hidden.astype(BF)
    grad_lout = weight_grad(l_att, d_light_attn)
    d_l_att = mul_back(d_light_attn, w_lout).astype(BF)
    dq_light, dk_light, dv_light = attend_backward(
        l_query, rim_keys, rim_values, light_allowed, l_lse, d_l_att, HL
    )
    rim_grads = jnp.concatenate([dk_light, dv_light], axis=-1)
    back_left, back_right, kv_grads = exchange_key_grads(
        rim_grads[:, :WIN].astype(BF),
        rim_grads[:, tokens + WIN :].astype(BF),
        kv_part.reshape(group, pieces, CAP, 2 * width_heavy),
    )
    d_h_proj = jnp.concatenate([dq_heavy.astype(BF), kv_grads.astype(BF)], axis=-1)
    grad_hqkv = weight_grad(a_rows, d_h_proj)
    d_a_rows = mul_back(d_h_proj, w_hqkv)
    own_grads = rim_grads[:, WIN : WIN + tokens]
    own_grads = jnp.concatenate(
        [
            own_grads[:, :WIN] + back_left.astype(F32),
            own_grads[:, WIN : tokens - WIN],
            own_grads[:, tokens - WIN :] + back_right.astype(F32),
        ],
        axis=1,
    )
    d_l_proj = jnp.concatenate([dq_light.astype(BF), own_grads.astype(BF)], axis=-1)
    grad_lqkv = weight_grad(normed, d_l_proj)
    d_normed = pick("scp,scd->spd", a_select, d_a_rows) + mul_back(d_l_proj, w_lqkv)
    _, first_pull = jax.vjp(rms_norm, inputs, gain_one)
    d_inputs_norm, grad_gain_one = first_pull(d_normed)
    d_inputs = d_hidden + d_inputs_norm
    rows = tokens // dp
    stats = jnp.concatenate(
        [
            grad_gain_one.reshape(-1, 128),
            grad_gain_two.reshape(-1, 128),
            jnp.broadcast_to(partial_loss, (4, 128)),
        ]
    )
    grads = (grad_lin, grad_ldown, grad_hout, grad_lout, grad_hqkv, grad_lqkv)
    shards = (light_in, light_down, heavy_out, light_out, heavy_qkv, light_qkv)
    sent = [
        packed_full(grad.astype(BF), shard.shape, nz) for grad, shard in zip(grads, shards)
    ]
    hin_tile = hin_src.shape[1:]
    done = scatter_all(
        dp,
        d_inputs.astype(BF).reshape(group, dp, rows, D),
        stats,
        sent,
        grad_hin.astype(BF).reshape((nz, 8) + hin_tile),
        grad_hdown.astype(BF).reshape(nz, -1, D),
    )
    d_layer = undeal_rows(dealing, done[0].reshape(seqs, rows, D))[:, None]
    summed = done[1]
    mine = data_index * pieces + piece
    loss_value = summed[12, 0] / (D * token_count)
    own_one = lax.dynamic_slice_in_dim(summed[:6].reshape(-1), mine * gain_len, gain_len)
    own_two = lax.dynamic_slice_in_dim(summed[6:12].reshape(-1), mine * gain_len, gain_len)
    g_lin, g_ldown, g_hout, g_lout, g_hqkv, g_lqkv = (
        full.reshape(shard.shape) for full, shard in zip(done[2:8], shards)
    )
    g_hin = (
        done[8]
        .astype(F32)
        .reshape(8, hin_rows, 2, nz, hidden_units)
        .transpose(1, 2, 3, 0, 4)
        .reshape(heavy_in.shape)
    )
    return (
        loss_value,
        d_layer,
        own_one,
        own_two,
        g_lqkv,
        g_lout,
        g_hqkv,
        g_hout,
        g_lin,
        g_ldown,
        g_hin,
        done[9].reshape(heavy_down.shape),
    )


def packed_full(grad, shard_shape, nz):
    rows, columns = shard_shape
    if rows % 8 == 0:
        return grad.reshape(nz, 2, 2, 2, rows, columns)
    return grad.reshape(nz, 2, 2, 2, rows * columns // 128, 128)


def solution(mesh):
    split = P(("dp", "fsdp"))
    matrix = P(("dp", "fsdp"), None)
    placed = (
        P(None, "fsdp", "dp", None),
        P("dp", "fsdp", None, None),
        P(),
        P(),
        P(),
        P(),
        P(),
        split,
        split,
    ) + (matrix,) * 8
    return jax.shard_map(
        local,
        mesh=mesh,
        in_specs=placed,
        out_specs=(P(), P(None, "fsdp", "dp", None), split, split) + (matrix,) * 8,
        check_vma=False,
    )
```

time: 1720 us -> 589 us (0.34)
  waiting for transfers between devices: 1140 us -> 0 us
  Pallas kernels: 0 us -> 398 us
  local copies, waits for them, and re-layouts: 221 us -> 52 us
  blocking collectives: 133 us -> 0 us
  matrix products: 137 us -> 90.5 us
  starting transfers between devices: 21 us -> 0 us
    reduce_scatter x9 -> x0, waiting for transfers between devices: 864 us -> none  [the longest x1 249 us: local(): lax.psum_scatter(grad_flat[8], ('dp', 'fsdp'), scatter_dimension=0, tiled...]
    pallas_call x0 -> x10, Pallas kernels: none -> 398 us  [the longest x8 370 us: call(): pl.pallas_call(kernel, out_shape=out_shape, in_specs=in_specs, out_specs=...]
    all_gather x8 -> x0, waiting for transfers between devices: 272 us -> none  [the longest x1 85.7 us: local(): lax.all_gather(flat_fwd[8], ('dp', 'fsdp'), axis=0, tiled=True)]
    reshape x34 -> x5, local copies, waits for them, and re-layouts: 157 us -> 2.73 us  [the longest x1 1.01 us: local(): hin_src = heavy_in.reshape(hin_rows, 2, nz, 8, hidden_units).transpose(3,...]
    psum x1 -> x0, blocking collectives: 45.1 us -> none  [local(): loss_value = lax.psum(partial_loss, ('dp', 'fsdp')) / (D * token_count)]
    all_gather x1 -> x0, blocking collectives: 44.7 us -> none  [local(): lax.all_gather(flat_fwd[3], ('dp', 'fsdp'), axis=0, tiled=True)]
    unnamed x1 -> x0, blocking collectives: 43.4 us -> none
    dot_general x37 -> x42, matrix products: 110 us -> 72.8 us  [the longest x8 20.6 us: weight_grad(): return jnp.einsum('pd,pe->de', a, b, preferred_element_type=F32)]
  transfers between devices with their start and end apart: 23 -> 0, of which waited for: 14 -> 0; matrix products, arithmetic and copies ran while one was open for 18% -> 0% of each run, Pallas kernels for 0% -> 0%
where the time goes in v1:
time: 589 us; the launch traced here: 582 us
  Pallas kernels  398 us (68%)
  matrix products  90.5 us (15%)
  local copies, waits for them, and re-layouts  52 us (9%)
  other arithmetic  36.8 us (6%)
    pallas_call x8, Pallas kernels, call(): pl.pallas_call(kernel, out_shape=out_shape, in_specs=in_specs, out_specs=...  370 us
    pallas_call x1, Pallas kernels, deal_rows(): pl.pallas_call(deal_kernel, out_shape=jax.ShapeDtypeStruct(rows.shape, ro...  25.7 us
    dot_general x8, matrix products, weight_grad(): return jnp.einsum('pd,pe->de', a, b, preferred_element_type=F32)  20.6 us
    dot_general x8, matrix products, mul_back(): return jnp.einsum('...e,de->...d', left, right, preferred_element_type=F32)  18.6 us
    unnamed x165, local copies, waits for them, and re-layouts  16.8 us
    dot_general x8, matrix products, mul(): return jnp.einsum('...d,de->...e', left, right, preferred_element_type=F32)  15.7 us

profile of v1, /device:TPU:0, one launch (start us, length us, event | category | flops | bytes accessed | tf_op | source)
XLA Modules:
  0.0 582.3 jit_solution(6001235818126832753)
XLA Ops:
  1.4 1.3 reduce_sum.206
  6.6 1.3 fusion.99.refs_1_
  15.8 25.7 %shard_map.256.refs_0_ = bf16[16,32,768]{2,1,0:T(8,128)(2,1)} custom-call(s32[16]{0:T(128)} %deal_ref.3, bf16[16,32,768]{2,1,0:T(8,128)(2,1)} %bitcast.311), custom_call_target="tpu_custom_call" | custom-call | tf_op jit(solution)/shard_map/pallas_call | solution.py:100
  41.5 141.0 %shard_map.257 = (bf16[2,8,32,768]{3,2,1,0:T(8,128)(2,1)}, bf16[4,2,2,2,8,128]{5,4,3,2,1,0:T(8,128)(2,1)}, bf16[4,2,2,2,24,1536]{5,4,3,2,1,0:T(8,128)(2,1)}, bf1...) custom-call(bf16[16,32,768]{2,1,0:T(8,128)(2,1)} %shard_map.256.refs, ...), custom_call_target="tpu_custom_call" | custom-call | tf_op jit(solution)/shard_map/pallas_call | solution.py:72
  185.7 1.4 fusion.29
  188.4 1.4 fusion.27
  194.4 3.0 convolution_convert_fusion.1
  197.5 1.3 copy.101
  199.9 21.8 %shard_map.258 = (bf16[2,128,1024]{2,1,0:T(8,128)(2,1)}, bf16[2,128,1024]{2,1,0:T(8,128)(2,1)}, bf16[2,4,64,1536]{3,2,1,0:T(8,128)(2,1)}) custom-call(bf16[2,128,1024]{2,1,0:T(8,128)(2,1)} %get-tuple-element.124.left, bf16[2,128,1024]{2,1,0:T(8,128)(2,1)} %get-tuple-element.123.right, bf16[2,64,1536]{2,1,0:T(8,128)(2,1)} %slice.106.kv), custom_call_target="tpu_custom_call" | custom-call | tf_op jit(solution)/shard_map/pallas_call | solution.py:72
  221.7 1.4 pad_maximum_fusion.1
  223.0 1.2 fusion.118
  224.2 1.5 copy.102
  225.7 1.4 copy.100
  227.1 1.5 fusion.119
  230.0 1.6 fusion.122
  234.9 1.7 fusion.123
  236.7 1.9 fusion
  238.6 1.3 copy-done
  240.0 3.1 fusion.37
  246.0 14.2 %shard_map.259 = bf16[2,2,2,128,768]{4,3,2,1,0:T(8,128)(2,1)} custom-call(bf16[128,768]{1,0:T(8,128)(2,1)} %bitcast.310), custom_call_target="tpu_custom_call" | custom-call | tf_op jit(solution)/shard_map/pallas_call | solution.py:72
  260.2 3.8 fusion.127
  264.7 1.2 copy-done.22
  266.0 2.2 convolution_convert_fusion.2
  268.1 16.1 %shard_map.260 = f32[128,768]{1,0:T(8,128)} custom-call(bf16[2,2,2,128,768]{4,3,2,1,0:T(8,128)(2,1)} %bitcast.301), custom_call_target="tpu_custom_call" | custom-call | tf_op jit(solution)/shard_map/pallas_call | solution.py:72
  284.2 1.4 fusion.60
  285.7 3.9 fusion.125
  293.1 2.7 fusion.13
  295.8 3.0 fusion.35
  298.8 3.5 bitcast_convert_fusion.1
  303.6 2.2 bitcast_convert_fusion.3
  305.8 13.6 %shard_map.261 = bf16[2,2,2,128,768]{4,3,2,1,0:T(8,128)(2,1)} custom-call(bf16[128,768]{1,0:T(8,128)(2,1)} %bitcast.317), custom_call_target="tpu_custom_call" | custom-call | tf_op jit(solution)/shard_map/pallas_call | solution.py:72
  319.5 5.3 fusion.20
  324.8 1.9 convolution_convert_fusion.5
  326.7 3.0 convolution_convert_fusion.3
  329.7 3.0 convolution_convert_fusion.4
  332.7 16.1 %shard_map.262 = f32[128,768]{1,0:T(8,128)} custom-call(bf16[2,2,2,128,768]{4,3,2,1,0:T(8,128)(2,1)} %bitcast.300), custom_call_target="tpu_custom_call" | custom-call | tf_op jit(solution)/shard_map/pallas_call | solution.py:72
  348.9 1.8 fusion.70
  350.7 1.4 multiply_reduce_fusion.1
  352.1 2.7 fusion.115
  354.8 1.4 convolution_convert_fusion.7
  356.2 2.2 copy.115
  359.7 2.7 bitcast_convert_fusion.5
  364.7 1.6 bitcast_convert_fusion.4
  372.4 1.9 copy.121
  374.3 2.5 pad_maximum_fusion.4.part
  376.8 5.8 fusion.3
  382.5 1.9 copy.117
  384.5 5.5 multiply_reduce_fusion
  390.0 4.5 multiply_convert_fusion
  394.5 1.4 fusion.39
  395.9 2.2 convolution_multiply_fusion
  398.0 3.1 copy.116
  401.4 1.9 fusion.2
  404.3 20.7 %shard_map.263 = (bf16[2,128,1024]{2,1,0:T(8,128)(2,1)}, bf16[2,128,1024]{2,1,0:T(8,128)(2,1)}, f32[2,64,1536]{2,1,0:T(8,128)}) custom-call(bf16[2,128,1024]{2,1,0:T(8,128)(2,1)} %get-tuple-element.117.left, bf16[2,128,1024]{2,1,0:T(8,128)(2,1)} %get-tuple-element.116.right, bf16[2,4,64,1536]{3,2,1,0:T(8,128)(2,1)} %pad_maximum_fusion.4.part), custom_call_target="tpu_custom_call" | custom-call | tf_op jit(solution)/shard_map/pallas_call | solution.py:72
  425.1 2.0 fusion.47
  427.9 1.3 fusion.59
  429.6 1.4 fusion.55
  431.1 2.8 bitcast_convert_fusion.2
  436.7 1.3 fusion.23
  438.0 2.9 bitcast_convert_fusion
  440.9 126.6 %shard_map.264 = (bf16[8,2,32,768]{3,2,1,0:T(8,128)(2,1)}, f32[16,128]{1,0:T(8,128)}, f32[24,2048]{1,0:T(8,128)}, f32[32,768]{1,0:T(8,128)}, f32[24,768]{1,0:T(8...) custom-call(bf16[2,8,32,768]{3,2,1,0:T(8,128)(2,1)} %bitcast.282, ...), custom_call_target="tpu_custom_call" | custom-call | tf_op jit(solution)/shard_map/pallas_call | solution.py:72
  567.5 1.2 slice.100
  571.3 2.5 shard_map.265
  574.7 1.3 copy.148
  (255 shorter events, 57.2 us)
Async XLA Ops:
  182.5 9.2 %copy-start.4 = (bf16[4,2,2,2,24,2304]{5,4,3,2,1,0:T(8,128)(2,1)S(1)}, bf16[4,2,2,2,24,2304]{5,4,3,2,1,0:T(8,128)(2,1)}, u32[]{:S(2)}) copy-start(bf16[4,2,2,2,24,2304]{5,4,3,2,1,0:T(8,128)(2,1)} %get-tuple-element.41) | copy-start | bytes 10616836
  185.7 8.5 %copy-start.58 = (f32[768]{0:T(1024)}, f32[768]{0:T(1024)S(1)}, u32[]{:S(2)}) copy-start(f32[768]{0:T(1024)S(1)} %reshape.585) | copy-start | bytes 9220
  188.4 4.0 copy-start.66
  188.4 1.4 copy-start.64
  192.4 1.7 copy-start.1
  197.4 1.3 copy-start.21
  199.9 21.8 %slice-start = ((bf16[2,256,1536]{2,1,0:T(8,128)(2,1)}), bf16[2,256,1024]{2,1,0:T(8,128)(2,1)S(1)}, s32[]{:S(2)}) async-start(bf16[2,256,1536]{2,1,0:T(8,128)(2,1)} %copy-done.21), calls=%async_computation | async-start | bytes 2097152 | tf_op jit(solution)/shard_map/slice | solution.py:865
  225.7 9.0 %copy-start.8 = (bf16[2,512,512]{1,2,0:T(8,128)(2,1)}, bf16[2,512,512]{1,2,0:T(8,128)(2,1)S(1)}, u32[]{:S(2)}) copy-start(bf16[2,512,512]{1,2,0:T(8,128)(2,1)S(1)} %copy.102) | copy-start | bytes 3145732
  228.6 1.5 copy-start.57
  228.9 2.7 copy-start.10
  230.0 2.1 copy-start.33
  232.2 1.3 copy-start.16
  232.2 1.6 copy-start.44
  233.0 1.3 copy-start.39
  236.7 3.3 copy-start
  236.7 3.3 copy-start.23
  240.0 3.2 copy-start.2
  240.0 3.2 copy-start.48
  264.0 2.0 copy-start.22
  264.0 2.0 copy-start.77
  266.0 2.2 copy-start.41
  266.0 18.3 %copy-start.70 = (f32[2,64]{1,0:T(2,128)S(1)}, f32[2,64]{1,0:T(2,128)}, u32[]{:S(2)}) copy-start(f32[2,64]{1,0:T(2,128)} %select_reduce_fusion.2) | copy-start | bytes 1540
  289.6 1.4 copy-start.76
  291.0 1.3 copy-start.68
  293.1 9.4 %copy-start.14 = (f32[2,256,768]{2,1,0:T(8,128)}, f32[2,256,768]{2,1,0:T(8,128)S(1)}, u32[]{:S(2)}) copy-start(f32[2,256,768]{2,1,0:T(8,128)S(1)} %get-tuple-element.146) | copy-start | bytes 4718596
  293.1 2.7 copy-start.73
  295.8 3.0 copy-start.30
  319.4 5.4 copy-start.37
  319.4 5.4 copy-start.42
  324.8 1.9 copy-start.36
  326.7 3.0 copy-start.75
  348.9 1.8 copy-start.25
  348.9 1.8 copy-start.38
  350.7 1.4 copy-start.15
  350.7 1.4 copy-start.71
  352.1 2.7 copy-start.49
  354.7 1.4 copy-start.12
  356.2 6.5 %copy-start.6 = (f32[2,256,768]{2,1,0:T(8,128)S(1)}, f32[2,256,768]{2,1,0:T(8,128)}, u32[]{:S(2)}) copy-start(f32[2,256,768]{2,1,0:T(8,128)} %get-tuple-element.109) | copy-start | bytes 4718596
  358.3 4.1 copy-start.13
  362.4 1.3 copy-start.17
  364.7 2.1 copy-start.34
  367.5 1.5 copy-start.26
  374.3 2.5 copy-start.20
  389.9 4.5 copy-start.9
  394.5 1.4 copy-start.19
  425.1 2.1 copy-start.50
  425.1 2.9 copy-start.5
  425.1 2.9 copy-start.35
  427.9 1.7 copy-start.74
  429.6 1.4 copy-start.28
  431.0 2.9 copy-start.45
  431.0 3.3 copy-start.59
  431.1 3.3 copy-start.65
  435.0 1.6 copy-start.67
  435.0 1.6 copy-start.7
  436.7 1.3 copy-start.32
  567.5 6.3 %copy-start.53 = (bf16[8,24,1024]{2,1,0:T(8,128)(2,1)S(1)}, bf16[8,24,1024]{2,1,0:T(8,128)(2,1)}, u32[]{:S(2)}) copy-start(bf16[8,24,1024]{2,1,0:T(8,128)(2,1)} %get-tuple-element.62) | copy-start | bytes 1179652
  573.8 2.2 copy-start.56
  573.8 2.9 copy-start.63
  573.8 3.5 copy-start.54
  574.2 3.8 copy-start.61
  574.2 4.4 copy-start.55
  574.2 5.1 copy-start.60
  574.2 5.8 copy-start.52
  (15 other events, 14.7 us)

commit v2 on v1

--- a/solution.py
+++ b/solution.py
@@ -81,28 +81,21 @@
     )(*operands)
 
 
-def deal_kernel(deal_ref, x_ref, o_ref, sem):
-    count = o_ref.shape[0]
-
-    def begin(i, carry):
-        pltpu.make_async_copy(x_ref.at[deal_ref[i]], o_ref.at[i], sem.at[i]).start()
+def deal_kernel(deal_ref, x_ref, o_ref):
+    def body(i, carry):
+        o_ref[i] = x_ref[deal_ref[i]]
         return carry
 
-    def finish(i, carry):
-        pltpu.make_async_copy(x_ref.at[deal_ref[i]], o_ref.at[i], sem.at[i]).wait()
-        return carry
-
-    lax.fori_loop(0, count, begin, 0)
-    lax.fori_loop(0, count, finish, 0)
+    lax.fori_loop(0, o_ref.shape[0], body, 0)
 
 
 def deal_rows(dealing, rows):
     return pl.pallas_call(
         deal_kernel,
         out_shape=jax.ShapeDtypeStruct(rows.shape, rows.dtype),
-        in_specs=[pl.BlockSpec(memory_space=pltpu.SMEM), ANY],
-        out_specs=ANY,
-        scratch_shapes=[DMA((rows.shape[0],))],
+        in_specs=[pl.BlockSpec(memory_space=pltpu.SMEM), VM],
+        out_specs=VM,
+        compiler_params=pltpu.CompilerParams(vmem_limit_bytes=VMEM_BYTES),
     )(dealing, rows)
 
 
@@ -400,88 +393,349 @@
     )
 
 
-def plane_meet():
-    hi, lo, x, c = place()
-    meet([at(hi, l2, x2, c) for l2, x2 in quad_peers()] + [at(hi, lo, x, 1 - c)])
-
-
-def plane_gather_kernel(rows, every, own, ss, sr, cs, cr):
+def dot(left, right):
+    return jnp.dot(left, right, preferred_element_type=F32)
+
+
+def dot_back(left, right):
+    return lax.dot_general(left, right, (((1,), (1,)), ((), ())), preferred_element_type=F32)
+
+
+def dot_grad(left, right):
+    return lax.dot_general(left, right, (((0,), (0,)), ((), ())), preferred_element_type=F32)
+
+
+def halves(value):
+    high = value.astype(BF)
+    return high, (value - high.astype(F32)).astype(BF)
+
+
+def tiles(extent, step, body):
+    def run(i, carry):
+        body(pl.ds(pl.multiple_of(i * step, step), step))
+        return carry
+
+    lax.fori_loop(0, extent // step, run, 0)
+
+
+GELU_A = 0.7978845608028654
+GELU_B = 0.044715
+
+
+def gelu_parts(v):
+    square = v * v
+    t = jnp.tanh(GELU_A * v * (1.0 + GELU_B * square))
+    value = 0.5 * v * (1.0 + t)
+    slope = 0.5 * (1.0 + t) + 0.5 * v * (1.0 - t * t) * GELU_A * (1.0 + 3.0 * GELU_B * square)
+    return value, slope
+
+
+def gelu_value(v):
+    return 0.5 * v * (1.0 + jnp.tanh(GELU_A * v * (1.0 + GELU_B * v * v)))
+
+
+def ffn_kernel(
+    hidden,
+    select,
+    select_t,
+    score,
+    gain,
+    teach,
+    mask,
+    scale,
+    w_in,
+    w_dn,
+    w_hin,
+    w_hdn,
+    g_in,
+    g_dn,
+    g_hin,
+    g_hdn,
+    d_hidden,
+    stats,
+    hn,
+    every,
+    d_every,
+    up_l,
+    z,
+    up_h,
+    zh,
+    part,
+    near,
+    far,
+    near2,
+    far2,
+    out,
+    dl,
+    dup_l,
+    dup_h,
+    dhn,
+    ps,
+    pr,
+    cs,
+    cr,
+    qs,
+    qr,
+    es,
+    er,
+):
     hi, lo, x, c = place()
     quad = quad_peers()
     partner = at(hi, lo, x, 1 - c)
-    plane_meet()
-    spot = every.at[lo, x, c]
-    mine = keep(rows, spot, own)
-    out = [
-        send(rows, spot, ss.at[k], sr.at[k], at(hi, l2, x2, c)) for k, (l2, x2) in enumerate(quad)
-    ]
-    back = [send(rows, spot, cs.at[3], cr.at[3], partner)]
-    for k, (l2, x2) in enumerate(quad):
-        out[k].wait()
-        other = every.at[l2, x2, c]
-        back.append(send(other, other, cs.at[k], cr.at[k], partner))
-    mine.wait()
+    spots = [l2 * 2 + x2 for l2, x2 in quad]
+    home = lo * 2 + x
+    tokens = hidden.shape[0]
+    group, cap, width = select.shape
+    fl = z.shape[1]
+    fh = zh.shape[2]
+    rows_h = part.shape[1] * part.shape[2]
+    meet([at(hi, l2, x2, c) for l2, x2 in quad] + [partner])
+
+    def spread(buffer, i):
+        spot = buffer.at[c, home]
+        there = [
+            send(spot, spot, ps.at[i, k], pr.at[i, k], at(hi, l2, x2, c))
+            for k, (l2, x2) in enumerate(quad)
+        ]
+        return there, [send(spot, spot, cs.at[i, 3], cr.at[i, 3], partner)]
+
+    def relay(buffer, i, there, back):
+        for k, q in enumerate(spots):
+            there[k].wait()
+            other = buffer.at[c, q]
+            back.append(send(other, other, cs.at[i, k], cr.at[i, k], partner))
+
+    def fold(near_ref, far_ref, i, copy):
+        copy.wait()
+        there = []
+        for k, q in enumerate(spots):
+            near_ref[q] = (near_ref[q].astype(F32) + part[c, q].astype(F32)).astype(BF)
+            l2, x2 = quad[k]
+            there.append(
+                send(near_ref.at[q], far_ref.at[k], qs.at[i, k], qr.at[i, k], at(hi, l2, x2, c))
+            )
+        return there
+
+    def folded(near_ref, far_ref, there):
+        for copy in there:
+            copy.wait()
+        return (
+            near_ref[home].astype(F32)
+            + part[c, home].astype(F32)
+            + far_ref[0].astype(F32)
+            + far_ref[1].astype(F32)
+            + far_ref[2].astype(F32)
+        )
+
+    def norm(r):
+        h = hidden[r, :]
+        inv = lax.rsqrt(jnp.mean(h * h, axis=-1, keepdims=True) + EPSILON)
+        hn[r, :] = (h * inv * gain[...]).astype(BF)
+
+    tiles(tokens, 128, norm)
+    for s in range(group):
+        every[c, home, s * cap : (s + 1) * cap, :] = dot(
+            select[s], hn[s * width : (s + 1) * width, :]
+        ).astype(BF)
+    there, back = spread(every, 0)
+
+    def light_up(r):
+        a = hn[r, :]
+
+        def inner(j):
+            k = pl.ds(pl.multiple_of(j.start + fl, 256), 256)
+            g = dot(a, w_in[:, j])
+            u = dot(a, w_in[:, k])
+            up_l[r, j] = g
+            up_l[r, k] = u
+            z[r, j] = (gelu_value(g) * u).astype(BF)
+
+        tiles(fl, 256, inner)
+
+    tiles(tokens, 256, light_up)
+    relay(every, 0, there, back)
+
+    def light_down(r):
+        out[r, :] = hidden[r, :] + dot(z[r, :], w_dn[...])
+
+    tiles(tokens, 256, light_down)
     for copy in back:
         copy.wait()
 
-
-def plane_gather(rows, collective_id):
+    def heavy(e):
+        def up(i, carry):
+            a = every[e, pl.ds(2 * i, 2)].reshape(2 * group * cap, D)
+            r = pl.ds(pl.multiple_of(i * 256, 256), 256)
+            for j in range(0, fh, 256):
+                g = dot(a, w_hin[:, j : j + 256])
+                u = dot(a, w_hin[:, fh + j : fh + j + 256])
+                up_h[e, r, j : j + 256] = g
+                up_h[e, r, fh + j : fh + j + 256] = u
+                zh[e, r, j : j + 256] = (gelu_value(g) * u).astype(BF)
+            v = dot(zh[e, r, :], w_hdn[...]).astype(BF)
+            part[e, pl.ds(2 * i, 2)] = v.reshape(2, group * cap, D)
+            return carry
+
+        lax.fori_loop(0, 2, up, 0)
+
+    heavy(1 - c)
+    first = send(part.at[1 - c], near, es.at[0], er.at[0], partner)
+    heavy(c)
+    there = fold(near, far, 0, first)
+    hf = folded(near, far, there) * score[...]
+    hf_high, hf_low = halves(hf)
+    for s in range(group):
+        r = slice(s * width, (s + 1) * width)
+        q = slice(s * cap, (s + 1) * cap)
+        out[r, :] += dot(select_t[s], hf_high[q]) + dot(select_t[s], hf_low[q])
+    stats[...] = jnp.zeros(stats.shape, F32)
+
+    def misfit(r):
+        m = out[r, :] - teach[r, :].astype(F32)
+        stats[1:2, :] += jnp.sum(mask[r, :] * m * m, axis=0, keepdims=True)
+        d = scale[r, :] * m
+        out[r, :] = d
+        dl[r, :] = d.astype(BF)
+
+    tiles(tokens, 128, misfit)
+    for s in range(group):
+        high, low = halves(out[s * width : (s + 1) * width, :])
+        picked = dot(select[s], high) + dot(select[s], low)
+        q = slice(s * cap, (s + 1) * cap)
+        d_every[c, home, q, :] = (picked * score[q, :]).astype(BF)
+    there, back = spread(d_every, 1)
+
+    def light_back(r):
+        d = dl[r, :]
+
+        def inner(j):
+            k = pl.ds(pl.multiple_of(j.start + fl, 256), 256)
+            dz = dot_back(d, w_dn[j, :])
+            value, slope = gelu_parts(up_l[r, j])
+            dup_l[r, j] = (dz * up_l[r, k] * slope).astype(BF)
+            dup_l[r, k] = (dz * value).astype(BF)
+
+        tiles(fl, 256, inner)
+
+    tiles(tokens, 256, light_back)
+    relay(d_every, 1, there, back)
+
+    def light_grad(j):
+        g_dn[j, :] = dot_grad(z[:, j], dl[...]).astype(BF)
+
+    tiles(fl, 256, light_grad)
+    for copy in back:
+        copy.wait()
+
+    def heavy_back(e):
+        def run(i, carry):
+            d = d_every[e, pl.ds(2 * i, 2)].reshape(2 * group * cap, D)
+            r = pl.ds(pl.multiple_of(i * 256, 256), 256)
+            for j in range(0, fh, 256):
+                dz = dot_back(d, w_hdn[j : j + 256, :])
+                value, slope = gelu_parts(up_h[e, r, j : j + 256])
+                dup_h[e, r, j : j + 256] = (
+                    dz * up_h[e, r, fh + j : fh + j + 256] * slope
+                ).astype(BF)
+                dup_h[e, r, fh + j : fh + j + 256] = (dz * value).astype(BF)
+            v = dot_back(dup_h[e, r, :], w_hin[...]).astype(BF)
+            part[e, pl.ds(2 * i, 2)] = v.reshape(2, group * cap, D)
+            return carry
+
+        lax.fori_loop(0, 2, run, 0)
+
+    heavy_back(1 - c)
+    second = send(part.at[1 - c], near2, es.at[1], er.at[1], partner)
+    heavy_back(c)
+    there = fold(near2, far2, 1, second)
+
+    def light_in_grad(j):
+        g_in[:, j] = dot_grad(hn[...], dup_l[:, j]).astype(BF)
+
+    tiles(2 * fl, 256, light_in_grad)
+
+    def light_in_back(r):
+        dhn[r, :] = dot_back(dup_l[r, :], w_in[...])
+
+    tiles(tokens, 256, light_in_back)
+    every_rows = every[...].reshape(2 * rows_h, D)
+
+    def heavy_grad(j):
+        g_hin[:, j] = dot_grad(every_rows, dup_h[:, :, j].reshape(2 * rows_h, 256)).astype(BF)
+
+    tiles(2 * fh, 256, heavy_grad)
+    d_rows = d_every[...].reshape(2 * rows_h, D)
+
+    def heavy_down_grad(j):
+        g_hdn[j, :] = dot_grad(zh[:, :, j].reshape(2 * rows_h, 256), d_rows).astype(BF)
+
+    tiles(fh, 256, heavy_down_grad)
+    d_high, d_low = halves(folded(near2, far2, there))
+    for s in range(group):
+        r = slice(s * width, (s + 1) * width)
+        q = slice(s * cap, (s + 1) * cap)
+        dhn[r, :] += dot(select_t[s], d_high[q]) + dot(select_t[s], d_low[q])
+
+    def norm_back(r):
+        h = hidden[r, :]
+        inv = lax.rsqrt(jnp.mean(h * h, axis=-1, keepdims=True) + EPSILON)
+        d = dhn[r, :]
+        dh = d * h
+        stats[0:1, :] += jnp.sum(dh * inv, axis=0, keepdims=True)
+        mean = jnp.mean(gain[...] * dh, axis=-1, keepdims=True)
+        d_hidden[r, :] = out[r, :] + inv * gain[...] * d - h * (inv * inv * inv * mean)
+
+    tiles(tokens, 128, norm_back)
+
+
+def feed_forward(hidden, select, select_t, score, gain, teach, mask, scale, w_in, w_dn, w_hin, w_hdn):
+    tokens = hidden.shape[0]
+    group, cap, _ = select.shape
+    rows = group * cap
+    fl, fh = w_dn.shape[0], w_hdn.shape[0]
+    block = (2, 4, rows, D)
+    operands = [hidden, select, select_t, score, gain, teach, mask, scale, w_in, w_dn, w_hin, w_hdn]
     return call(
-        plane_gather_kernel,
-        jax.ShapeDtypeStruct((2, 2, 2) + rows.shape, BF),
-        [rows],
-        [ANY],
-        ANY,
-        [DMA, DMA((3,)), DMA((3,)), DMA((4,)), DMA((4,))],
-        collective_id,
-    )
-
-
-def plane_sum_kernel(part, total, near, far, ss, sr, cs, cr):
-    hi, lo, x, c = place()
-    quad = quad_peers()
-    partner = at(hi, lo, x, 1 - c)
-    plane_meet()
-    spots = quad + [(lo, x)]
-    back = [
-        send(part.at[l2, x2, 1 - c], near.at[l2, x2], cs.at[k], cr.at[k], partner)
-        for k, (l2, x2) in enumerate(spots)
-    ]
-    out = []
-    for k, (l2, x2) in enumerate(spots):
-        back[k].wait()
-        near[l2, x2] = (near[l2, x2].astype(F32) + part[l2, x2, c].astype(F32)).astype(BF)
-        if k < 3:
-            out.append(
-                send(near.at[l2, x2], far.at[k], ss.at[k], sr.at[k], at(hi, l2, x2, c))
-            )
-    for copy in out:
-        copy.wait()
-    total[...] = (
-        near[lo, x].astype(F32)
-        + far[0].astype(F32)
-        + far[1].astype(F32)
-        + far[2].astype(F32)
-    )
-
-
-def plane_sum(part, collective_id):
-    shape = part.shape[3:]
-    return call(
-        plane_sum_kernel,
-        jax.ShapeDtypeStruct(shape, F32),
-        [part],
-        [VM],
-        VM,
+        ffn_kernel,
         [
-            pltpu.VMEM((2, 2) + shape, BF),
-            pltpu.VMEM((3,) + shape, BF),
-            DMA((3,)),
-            DMA((3,)),
-            DMA((4,)),
-            DMA((4,)),
+            jax.ShapeDtypeStruct((D, 2 * fl), BF),
+            jax.ShapeDtypeStruct((fl, D), BF),
+            jax.ShapeDtypeStruct((D, 2 * fh), BF),
+            jax.ShapeDtypeStruct((fh, D), BF),
+            jax.ShapeDtypeStruct((tokens, D), F32),
+            jax.ShapeDtypeStruct((8, D), F32),
         ],
-        collective_id,
+        operands,
+        [VM] * len(operands),
+        [VM] * 6,
+        [
+            pltpu.VMEM((tokens, D), BF),
+            pltpu.VMEM(block, BF),
+            pltpu.VMEM(block, BF),
+            pltpu.VMEM((tokens, 2 * fl), F32),
+            pltpu.VMEM((tokens, fl), BF),
+            pltpu.VMEM((2, 4 * rows, 2 * fh), F32),
+            pltpu.VMEM((2, 4 * rows, fh), BF),
+            pltpu.VMEM(block, BF),
+            pltpu.VMEM(block[1:], BF),
+            pltpu.VMEM((3, rows, D), BF),
+            pltpu.VMEM(block[1:], BF),
+            pltpu.VMEM((3, rows, D), BF),
+            pltpu.VMEM((tokens, D), F32),
+            pltpu.VMEM((tokens, D), BF),
+            pltpu.VMEM((tokens, 2 * fl), BF),
+            pltpu.VMEM((2, 4 * rows, 2 * fh), BF),
+            pltpu.VMEM((tokens, D), F32),
+            DMA((2, 3)),
+            DMA((2, 3)),
+            DMA((2, 4)),
+            DMA((2, 4)),
+            DMA((2, 3)),
+            DMA((2, 3)),
+            DMA((2,)),
+            DMA((2,)),
+        ],
+        5,
     )
 
 
@@ -677,17 +931,6 @@
     return value * lax.rsqrt(jnp.mean(value * value, axis=-1, keepdims=True) + EPSILON) * gain
 
 
-def geglu(gate, upper):
-    return jax.nn.gelu(gate, approximate=True) * upper
-
-
-def geglu_back(up_proj, d_act):
-    half_width = up_proj.shape[-1] // 2
-    _, pullback = jax.vjp(geglu, up_proj[..., :half_width], up_proj[..., half_width:])
-    d_gate, d_upper = pullback(d_act)
-    return jnp.concatenate([d_gate, d_upper], axis=-1).astype(BF)
-
-
 def split_heads(rows, heads):
     return rows.reshape(rows.shape[0], rows.shape[1], heads, -1)
 
@@ -856,7 +1099,6 @@
     slot_score = jnp.sum(
         jnp.where(f_spot[:, :, None] == ffn_pick[:, None, :], score_pick[:, None, :], 0.0), axis=-1
     )
-    targets = teacher[:, 0].astype(F32)
     width_light = HL * DH
     width_heavy = HH * DH
     normed = rms_norm(inputs, gain_one).astype(BF)
@@ -890,39 +1132,22 @@
     h_att, h_lse = attend_forward(h_query, hv_keys, hv_values, heavy_allowed, HH)
     heavy_branch = mul(h_att, w_hout)
     hidden = inputs + light_branch + pick("scp,scd->spd", a_select, heavy_branch)
-    normed_two = rms_norm(hidden, gain_two).astype(BF)
-    f_rows = jnp.einsum("scp,spd->scd", f_select, normed_two, preferred_element_type=F32).astype(BF)
-    t_rows = plane_gather(f_rows.reshape(group * CAP, D), 5).reshape(-1, D)
-    heavy_up = mul(t_rows, w_hin)
-    half = heavy_up.shape[-1] // 2
-    heavy_mid = geglu(heavy_up[..., :half], heavy_up[..., half:]).astype(BF)
-    heavy_part = mul(heavy_mid, w_hdown).astype(BF)
-    heavy_ffn = plane_sum(heavy_part.reshape(2, 2, 2, group * CAP, D), 6).reshape(group, CAP, D)
-    light_up = mul(normed_two, w_lin)
-    light_mid = geglu(light_up[..., :FL], light_up[..., FL:]).astype(BF)
-    light_ffn = mul(light_mid, w_ldown)
-    output = hidden + light_ffn + pick("scp,scd->spd", f_select, heavy_ffn * slot_score[..., None])
-    misfit = output - targets
-    weight_mask = valid_mask[..., None].astype(F32)
-    partial_loss = jnp.sum(weight_mask * misfit * misfit)
-    d_out = 2.0 * weight_mask * misfit / (D * token_count)
-    d_heavy_ffn = (pick("scp,spd->scd", f_select, d_out) * slot_score[..., None]).astype(BF)
-    t_grad = plane_gather(d_heavy_ffn.reshape(group * CAP, D), 7).reshape(-1, D)
-    grad_hdown = weight_grad(heavy_mid, t_grad)
-    d_heavy_mid = mul_back(t_grad, w_hdown)
-    d_heavy_up = geglu_back(heavy_up, d_heavy_mid)
-    grad_hin = weight_grad(t_rows, d_heavy_up)
-    d_f_part = mul_back(d_heavy_up, w_hin).astype(BF)
-    d_f_rows = plane_sum(d_f_part.reshape(2, 2, 2, group * CAP, D), 8).reshape(group, CAP, D)
-    d_light = d_out.astype(BF)
-    grad_ldown = weight_grad(light_mid, d_light)
-    d_light_mid = mul_back(d_light, w_ldown)
-    d_light_up = geglu_back(light_up, d_light_mid)
-    grad_lin = weight_grad(normed_two, d_light_up)
-    d_norm_two = pick("scp,scd->spd", f_select, d_f_rows) + mul_back(d_light_up, w_lin)
-    _, second_pull = jax.vjp(rms_norm, hidden, gain_two)
-    d_hidden_norm, grad_gain_two = second_pull(d_norm_two)
-    d_hidden = d_out + d_hidden_norm
+    weight_mask = valid_mask.reshape(-1, 1).astype(F32)
+    grad_lin, grad_ldown, grad_hin, grad_hdown, d_hidden, ffn_stats = feed_forward(
+        hidden.reshape(-1, D),
+        f_select,
+        f_select.swapaxes(1, 2),
+        slot_score.reshape(-1, 1),
+        gain_two.reshape(1, D),
+        teacher.reshape(-1, D),
+        weight_mask,
+        2.0 * weight_mask / (D * token_count),
+        w_lin,
+        w_ldown,
+        w_hin,
+        w_hdown,
+    )
+    d_hidden = d_hidden.reshape(group, tokens, D)
     d_heavy_attn = pick("scp,spd->scd", a_select, d_hidden).astype(BF)
     grad_hout = weight_grad(h_att, d_heavy_attn)
     d_h_att = mul_back(d_heavy_attn, w_hout).astype(BF)
@@ -964,8 +1189,8 @@
     stats = jnp.concatenate(
         [
             grad_gain_one.reshape(-1, 128),
-            grad_gain_two.reshape(-1, 128),
-            jnp.broadcast_to(partial_loss, (4, 128)),
+            ffn_stats[0].reshape(-1, 128),
+            jnp.broadcast_to(jnp.sum(ffn_stats[1]), (4, 128)),
         ]
     )
     grads = (grad_lin, grad_ldown, grad_hout, grad_lout, grad_hqkv, grad_lqkv)

time: 589 us -> 542 us (0.920)
  matrix products: 90.5 us -> 55.6 us
  Pallas kernels: 398 us -> 382 us
  local copies, waits for them, and re-layouts: 52 us -> 59.4 us
    pallas_call x1, Pallas kernels: 25.7 us -> 2.16 us  [deal_rows(): pl.pallas_call(deal_kernel, out_shape=jax.ShapeDtypeStruct(rows.shape, ro...]
    dot_general x8 -> x4, matrix products: 18.6 us -> 5.31 us  [mul_back(): return jnp.einsum('...e,de->...d', left, right, preferred_element_type=F32)]
    dot_general x8 -> x4, matrix products: 20.6 us -> 9.79 us  [weight_grad(): return jnp.einsum('pd,pe->de', a, b, preferred_element_type=F32)]
    dot_general x8 -> x4, matrix products: 15.7 us -> 7.88 us  [mul(): return jnp.einsum('...d,de->...e', left, right, preferred_element_type=F32)]
    pallas_call x8 -> x5, Pallas kernels: 370 us -> 378 us  [call(): pl.pallas_call(kernel, out_shape=out_shape, in_specs=in_specs, out_specs=...]
    unnamed x165 -> x99, local copies, waits for them, and re-layouts: 16.8 us -> 15.8 us
where the time goes in v2:
time: 542 us; the launch traced here: 535 us
  Pallas kernels  382 us (70%)
  local copies, waits for them, and re-layouts  59.4 us (11%)
  matrix products  55.6 us (10%)
  other arithmetic  33 us (6%)
    pallas_call x5, Pallas kernels, call(): pl.pallas_call(kernel, out_shape=out_shape, in_specs=in_specs, out_specs=...  378 us
    unnamed x99, local copies, waits for them, and re-layouts  15.8 us

profile of v2, /device:TPU:0, one launch (start us, length us, event | category | flops | bytes accessed | tf_op | source)
XLA Modules:
  0.0 534.6 jit_solution(4660216601912771889)
XLA Ops:
  1.4 1.3 reduce_sum.166
  6.1 1.3 fusion.70.refs_1_
  8.4 1.6 select_reduce_fusion
  12.2 1.0 reshape.508.refs_8_
  13.2 1.4 fusion.81
  18.2 2.2 shard_map.256.refs_0_
  20.3 140.9 %shard_map.257 = (bf16[2,8,32,768]{3,2,1,0:T(8,128)(2,1)}, bf16[4,2,2,2,8,128]{5,4,3,2,1,0:T(8,128)(2,1)}, bf16[4,2,2,2,24,1536]{5,4,3,2,1,0:T(8,128)(2,1)}, bf1...) custom-call(bf16[16,32,768]{2,1,0:T(8,128)(2,1)} %shard_map.256.refs, ...), custom_call_target="tpu_custom_call" | custom-call | tf_op jit(solution)/shard_map/pallas_call | solution.py:72
  161.2 1.0 fusion.87
  163.0 1.4 fusion.13
  165.9 2.7 convolution_convert_fusion
  170.7 3.0 convolution_convert_fusion.1
  173.8 1.2 copy.104
  175.1 1.1 fusion.86
  176.2 22.1 %shard_map.258 = (bf16[2,128,1024]{2,1,0:T(8,128)(2,1)}, bf16[2,128,1024]{2,1,0:T(8,128)(2,1)}, bf16[2,4,64,1536]{3,2,1,0:T(8,128)(2,1)}) custom-call(bf16[2,128,1024]{2,1,0:T(8,128)(2,1)} %get-tuple-element.129.left, bf16[2,128,1024]{2,1,0:T(8,128)(2,1)} %get-tuple-element.128.right, bf16[2,64,1536]{2,1,0:T(8,128)(2,1)} %slice.94.kv), custom_call_target="tpu_custom_call" | custom-call | tf_op jit(solution)/shard_map/pallas_call | solution.py:72
  198.3 1.4 pad_maximum_fusion.1
  199.7 1.2 fusion.84
  200.8 1.5 copy.105
  202.3 1.4 copy.103
  203.7 1.5 fusion.85
  205.2 1.2 copy.109
  206.3 1.2 copy.107
  207.5 1.8 fusion.88
  213.0 1.7 fusion.89
  214.7 1.9 fusion
  216.6 1.3 copy-done
  217.9 2.7 fusion.20
  220.7 1.7 fusion.16
  222.5 67.6 %shard_map.259 = (bf16[768,2048]{1,0:T(8,128)(2,1)}, bf16[1024,768]{1,0:T(8,128)(2,1)}, bf16[768,1024]{1,0:T(8,128)(2,1)}, bf16[512,768]{1,0:T(8,128)(2,1)}, f32[512,768]{1,0:T(8,128)}, /*index=5*/f32[8,768]{1,0:T(8,128)}) custom-call(f32[512,768]{1,0:T(8,128)} %bitcast.231, bf16[2,64,256]{2,1,0:T(8,128)(2,1)} %copy.115.select, ...), custom_call_target="tpu_custom_call" | custom-call | tf_op jit(solution)/shard_map/pallas_call | solution.py:72
  290.1 1.5 slice_reduce_fusion
  292.3 1.7 fusion.41
  295.4 1.2 convolution_convert_fusion.5
  296.6 1.8 copy.143
  298.4 2.6 bitcast_convert_fusion.2
  301.1 1.3 fusion.19
  305.3 1.2 fusion.21
  307.4 2.8 concatenate.30
  310.1 2.0 copy.126
  312.2 2.8 concatenate.31
  315.0 2.1 copy.127
  317.1 2.7 pad_maximum_fusion.2.part
  319.9 1.0 copy-done.30
  321.0 1.4 convolution_convert_fusion.3
  322.4 1.5 bitcast_convert_fusion.3
  323.8 2.1 copy.121
  325.9 6.4 %fusion.3 = f32[2,8,64,512]{3,2,1,0:T(8,128)} fusion(bf16[2,256,8,64]{1,3,2,0:T(8,128)(2,1)} %bitcast.237, f32[2,8,256,512]{3,2,1,0:T(8,128)} %copy-done, f32[2,8,256]{2,1,0:T(8,128)S(1)} %log_add_fusion), kind=kOutput, calls=%fused_computation.16 | convolution fusion | flops 272629760 | bytes 11026432 | tf_op jit(solution)/shard_map/shqk,sqhd->skhd/dot_general | solution.py:984
  332.3 2.9 copy.123
  335.2 6.7 %multiply_reduce_fusion = (f32[2,8,256]{2,1,0:T(8,128)S(1)}, f32[2,8,256,512]{3,2,1,0:T(8,128)S(1)}) fusion(f32[2,8,256,512]{3,2,1,0:T(8,128)} %copy-done, f32[2,8,256]{2,1,0:T(8,128)S(1)} %log_add_fusion, bf16[2,256,8,64]{1,3,2,0:T(8,128)(2,1)} %bitcast.238, bf16[2,512,8,64]{1,3,2,0:T(8,128)(2,1)} %bitcast.239), kind=kOutput, calls=%fused_computation.1 | convolution fusion | flops 274722816 | bytes 18382848 | tf_op jit(solution)/shard_map/sqhd,skhd->shqk/dot_general | solution.py:967
  341.9 4.4 multiply_convert_fusion
  346.3 2.2 fusion.22
  348.5 2.2 convolution_multiply_fusion
  350.7 3.0 copy.122
  353.9 2.5 fusion.2
  356.4 1.1 fusion.83
  357.5 20.8 %shard_map.260 = (bf16[2,128,1024]{2,1,0:T(8,128)(2,1)}, bf16[2,128,1024]{2,1,0:T(8,128)(2,1)}, f32[2,64,1536]{2,1,0:T(8,128)}) custom-call(bf16[2,128,1024]{2,1,0:T(8,128)(2,1)} %get-tuple-element.123.left, bf16[2,128,1024]{2,1,0:T(8,128)(2,1)} %get-tuple-element.122.right, bf16[2,4,64,1536]{3,2,1,0:T(8,128)(2,1)} %pad_maximum_fusion.2.part), custom_call_target="tpu_custom_call" | custom-call | tf_op jit(solution)/shard_map/pallas_call | solution.py:72
  378.3 2.3 fusion.28
  381.5 1.3 fusion.43
  383.2 1.4 fusion.38
  384.6 2.8 bitcast_convert_fusion.1
  389.3 1.3 fusion.8
  390.6 2.9 bitcast_convert_fusion
  393.5 126.3 %shard_map.261 = (bf16[8,2,32,768]{3,2,1,0:T(8,128)(2,1)}, f32[16,128]{1,0:T(8,128)}, f32[24,2048]{1,0:T(8,128)}, f32[32,768]{1,0:T(8,128)}, f32[24,768]{1,0:T(8...) custom-call(bf16[2,8,32,768]{3,2,1,0:T(8,128)(2,1)} %bitcast.245, ...), custom_call_target="tpu_custom_call" | custom-call | tf_op jit(solution)/shard_map/pallas_call | solution.py:72
  519.8 1.2 slice.88
  523.6 2.5 shard_map.262
  527.0 1.3 copy.154
  (166 shorter events, 34.7 us)
Async XLA Ops:
  0.6 11.3 %copy-start.33 = (bf16[24,8192]{1,0:T(8,128)(2,1)S(1)}, bf16[24,8192]{1,0:T(8,128)(2,1)}, u32[]{:S(2)}) copy-start(bf16[24,8192]{1,0:T(8,128)(2,1)} %param.32) | copy-start | bytes 1179652
  14.6 150.1 %copy-start.21 = (pred[2,4,64,256]{2,3,0,1:T(32,128)(4,1)}, pred[2,4,64,256]{2,3,0,1:T(32,128)(4,1)S(1)}, u32[]{:S(2)}) copy-start(pred[2,4,64,256]{2,3,0,1:T(32,128)(4,1)S(1)} %get-tuple-element.157) | copy-start | bytes 393220
  161.2 3.2 copy-start.1
  164.7 0.9 copy-start.14
  165.9 2.7 copy-start.18
  173.7 1.3 copy-start.10
  176.2 22.1 %slice-start = ((bf16[2,256,1536]{2,1,0:T(8,128)(2,1)}), bf16[2,256,1024]{2,1,0:T(8,128)(2,1)S(1)}, s32[]{:S(2)}) async-start(bf16[2,256,1536]{2,1,0:T(8,128)(2,1)} %copy-done.10), calls=%async_computation | async-start | bytes 2097152 | tf_op jit(solution)/shard_map/slice | solution.py:1107
  207.5 2.4 copy-start.16
  209.9 1.3 copy-start.6
  210.7 1.6 copy-start.26
  210.7 1.2 copy-start.22
  211.8 1.0 copy-start.8
  211.8 1.1 copy-start.27
  214.7 3.2 copy-start
  214.7 3.2 copy-start.11
  217.9 2.8 copy-start.29
  220.7 1.8 copy-start.31
  290.1 3.9 copy-start.2
  294.0 1.3 copy-start.7
  294.4 0.7 copy-start.24
  298.4 2.7 copy-start.12
  301.1 1.3 copy-start.17
  303.2 1.1 copy-start.5
  304.3 1.0 copy-start.13
  317.1 2.8 copy-start.3
  319.8 1.1 copy-start.30
  319.9 2.4 copy-start.32
  346.3 2.2 copy-start.9
  350.7 3.0 copy-start.20
  378.3 2.4 copy-start.28
  378.3 3.2 copy-start.4
  378.3 3.2 copy-start.25
  381.5 1.7 copy-start.42
  383.1 1.4 copy-start.15
  384.6 2.9 copy-start.23
  389.3 1.4 copy-start.19
  519.8 6.3 %copy-start.35 = (bf16[8,24,1024]{2,1,0:T(8,128)(2,1)S(1)}, bf16[8,24,1024]{2,1,0:T(8,128)(2,1)}, u32[]{:S(2)}) copy-start(bf16[8,24,1024]{2,1,0:T(8,128)(2,1)} %get-tuple-element.74) | copy-start | bytes 1179652
  526.5 1.9 copy-start.38
  526.5 2.5 copy-start.41
  526.5 3.1 copy-start.36
  527.0 3.4 copy-start.40
  527.0 4.0 copy-start.37
  527.0 4.7 copy-start.39
  527.0 5.3 copy-start.34

commit v3 on v2

--- a/solution.py
+++ b/solution.py
@@ -311,86 +311,6 @@
 def line_peers():
     hi, lo, x, c = place()
     return [at(hi, lo, x, 1 - c), at(hi, lo, 1 - x, c), at(hi, lo, 1 - x, 1 - c)]
-
-
-def keys_kernel(left, right, kv, from_left, from_right, every, own, ls, lr, rs, rr, ss, sr):
-    hi, lo, x, c = place()
-    f = x * 2 + c
-    meet(line_peers())
-    finish = rim_exchange(left, right, from_left, from_right, ls, lr, rs, rr)
-    mine = keep(kv, every.at[:, f], own)
-    across = send(kv, every.at[:, f], ss.at[0], sr.at[0], at(hi, lo, 1 - x, c))
-    beside = send(kv, every.at[:, f], ss.at[1], sr.at[1], at(hi, lo, x, 1 - c))
-    across.wait()
-    other = every.at[:, (1 - x) * 2 + c]
-    relay = send(other, other, ss.at[2], sr.at[2], at(hi, lo, x, 1 - c))
-    mine.wait()
-    beside.wait()
-    relay.wait()
-    finish()
-
-
-def exchange_keys(left, right, kv):
-    group, cap, width = kv.shape
-    return call(
-        keys_kernel,
-        [
-            jax.ShapeDtypeStruct(left.shape, BF),
-            jax.ShapeDtypeStruct(right.shape, BF),
-            jax.ShapeDtypeStruct((group, 4, cap, width), BF),
-        ],
-        [left, right, kv],
-        [VM] * 3,
-        [VM] * 3,
-        [DMA, DMA, DMA, DMA, DMA, DMA((3,)), DMA((3,))],
-        2,
-    )
-
-
-def key_grads_kernel(left, right, part, from_left, from_right, total, got, far, ls, lr, rs, rr, ss, sr):
-    hi, lo, x, c = place()
-    meet(line_peers())
-    finish = rim_exchange(left, right, from_left, from_right, ls, lr, rs, rr)
-    beside = [
-        send(
-            part.at[:, b * 2 + 1 - c], got.at[b], ss.at[b], sr.at[b], at(hi, lo, x, 1 - c)
-        )
-        for b in (0, 1)
-    ]
-    for copy in beside:
-        copy.wait()
-    for b in (0, 1):
-        got[b] = (got[b].astype(F32) + part[:, b * 2 + c].astype(F32)).astype(BF)
-    across = send(got.at[1 - x], far, ss.at[2], sr.at[2], at(hi, lo, 1 - x, c))
-    across.wait()
-    total[...] = got[x].astype(F32) + far[...].astype(F32)
-    finish()
-
-
-def exchange_key_grads(left, right, part):
-    group, _, cap, width = part.shape
-    return call(
-        key_grads_kernel,
-        [
-            jax.ShapeDtypeStruct(left.shape, BF),
-            jax.ShapeDtypeStruct(right.shape, BF),
-            jax.ShapeDtypeStruct((group, cap, width), F32),
-        ],
-        [left, right, part],
-        [VM] * 3,
-        [VM] * 3,
-        [
-            pltpu.VMEM((2, group, cap, width), BF),
-            pltpu.VMEM((group, cap, width), BF),
-            DMA,
-            DMA,
-            DMA,
-            DMA,
-            DMA((3,)),
-            DMA((3,)),
-        ],
-        3,
-    )
 
 
 def dot(left, right):
@@ -540,17 +460,8 @@
     there, back = spread(every, 0)
 
     def light_up(r):
-        a = hn[r, :]
-
-        def inner(j):
-            k = pl.ds(pl.multiple_of(j.start + fl, 256), 256)
-            g = dot(a, w_in[:, j])
-            u = dot(a, w_in[:, k])
-            up_l[r, j] = g
-            up_l[r, k] = u
-            z[r, j] = (gelu_value(g) * u).astype(BF)
-
-        tiles(fl, 256, inner)
+        up_l[r, :] = dot(hn[r, :], w_in[...])
+        z[r, :] = (gelu_value(up_l[r, :fl]) * up_l[r, fl:]).astype(BF)
 
     tiles(tokens, 256, light_up)
     relay(every, 0, there, back)
@@ -566,12 +477,8 @@
         def up(i, carry):
             a = every[e, pl.ds(2 * i, 2)].reshape(2 * group * cap, D)
             r = pl.ds(pl.multiple_of(i * 256, 256), 256)
-            for j in range(0, fh, 256):
-                g = dot(a, w_hin[:, j : j + 256])
-                u = dot(a, w_hin[:, fh + j : fh + j + 256])
-                up_h[e, r, j : j + 256] = g
-                up_h[e, r, fh + j : fh + j + 256] = u
-                zh[e, r, j : j + 256] = (gelu_value(g) * u).astype(BF)
+            up_h[e, r, :] = dot(a, w_hin[...])
+            zh[e, r, :] = (gelu_value(up_h[e, r, :fh]) * up_h[e, r, fh:]).astype(BF)
             v = dot(zh[e, r, :], w_hdn[...]).astype(BF)
             part[e, pl.ds(2 * i, 2)] = v.reshape(2, group * cap, D)
             return carry
@@ -606,16 +513,10 @@
     there, back = spread(d_every, 1)
 
     def light_back(r):
-        d = dl[r, :]
-
-        def inner(j):
-            k = pl.ds(pl.multiple_of(j.start + fl, 256), 256)
-            dz = dot_back(d, w_dn[j, :])
-            value, slope = gelu_parts(up_l[r, j])
-            dup_l[r, j] = (dz * up_l[r, k] * slope).astype(BF)
-            dup_l[r, k] = (dz * value).astype(BF)
-
-        tiles(fl, 256, inner)
+        dz = dot_back(dl[r, :], w_dn[...])
+        value, slope = gelu_parts(up_l[r, :fl])
+        dup_l[r, :fl] = (dz * up_l[r, fl:] * slope).astype(BF)
+        dup_l[r, fl:] = (dz * value).astype(BF)
 
     tiles(tokens, 256, light_back)
     relay(d_every, 1, there, back)
@@ -623,7 +524,7 @@
     def light_grad(j):
         g_dn[j, :] = dot_grad(z[:, j], dl[...]).astype(BF)
 
-    tiles(fl, 256, light_grad)
+    tiles(fl, 512, light_grad)
     for copy in back:
         copy.wait()
 
@@ -631,13 +532,10 @@
         def run(i, carry):
             d = d_every[e, pl.ds(2 * i, 2)].reshape(2 * group * cap, D)
             r = pl.ds(pl.multiple_of(i * 256, 256), 256)
-            for j in range(0, fh, 256):
-                dz = dot_back(d, w_hdn[j : j + 256, :])
-                value, slope = gelu_parts(up_h[e, r, j : j + 256])
-                dup_h[e, r, j : j + 256] = (
-                    dz * up_h[e, r, fh + j : fh + j + 256] * slope
-                ).astype(BF)
-                dup_h[e, r, fh + j : fh + j + 256] = (dz * value).astype(BF)
+            dz = dot_back(d, w_hdn[...])
+            value, slope = gelu_parts(up_h[e, r, :fh])
+            dup_h[e, r, :fh] = (dz * up_h[e, r, fh:] * slope).astype(BF)
+            dup_h[e, r, fh:] = (dz * value).astype(BF)
             v = dot_back(dup_h[e, r, :], w_hin[...]).astype(BF)
             part[e, pl.ds(2 * i, 2)] = v.reshape(2, group * cap, D)
             return carry
@@ -652,7 +550,7 @@
     def light_in_grad(j):
         g_in[:, j] = dot_grad(hn[...], dup_l[:, j]).astype(BF)
 
-    tiles(2 * fl, 256, light_in_grad)
+    tiles(2 * fl, 1024, light_in_grad)
 
     def light_in_back(r):
         dhn[r, :] = dot_back(dup_l[r, :], w_in[...])
@@ -661,15 +559,15 @@
     every_rows = every[...].reshape(2 * rows_h, D)
 
     def heavy_grad(j):
-        g_hin[:, j] = dot_grad(every_rows, dup_h[:, :, j].reshape(2 * rows_h, 256)).astype(BF)
-
-    tiles(2 * fh, 256, heavy_grad)
+        g_hin[:, j] = dot_grad(every_rows, dup_h[:, :, j].reshape(2 * rows_h, 512)).astype(BF)
+
+    tiles(2 * fh, 512, heavy_grad)
     d_rows = d_every[...].reshape(2 * rows_h, D)
 
     def heavy_down_grad(j):
-        g_hdn[j, :] = dot_grad(zh[:, :, j].reshape(2 * rows_h, 256), d_rows).astype(BF)
-
-    tiles(fh, 256, heavy_down_grad)
+        g_hdn[j, :] = dot_grad(zh[:, :, j].reshape(2 * rows_h, 512), d_rows).astype(BF)
+
+    tiles(fh, 512, heavy_down_grad)
     d_high, d_low = halves(folded(near2, far2, there))
     for s in range(group):
         r = slice(s * width, (s + 1) * width)
@@ -739,6 +637,441 @@
     )
 
 
+def pair_masks(scale):
+    lane = lax.broadcasted_iota(jnp.int32, (1, 2 * DH), 1)
+    left = jnp.where(lane < DH, scale, 0.0).astype(BF)
+    right = jnp.where(lane < DH, 0.0, scale).astype(BF)
+    return left, right
+
+
+def both(value, masks):
+    return jnp.concatenate([value * masks[0], value * masks[1]], axis=0)
+
+
+def side(stacked):
+    rows = stacked.shape[0] // 2
+    return jnp.concatenate([stacked[:rows], stacked[rows:]], axis=1)
+
+
+def pair_forward(q, k, v, bias, ones, scaled):
+    scores = dot_back(both(q, scaled), k) + bias
+    top = jnp.max(scores, axis=-1, keepdims=True)
+    shifted = jnp.exp(scores - top)
+    total = jnp.sum(shifted, axis=-1, keepdims=True)
+    prob = (shifted / total).astype(BF)
+    return dot(side(prob), both(v, ones)).astype(BF), top + jnp.log(total)
+
+
+def pair_backward(q, k, v, bias, lse, d_out, ones, scaled):
+    q2 = both(q, scaled)
+    d2 = both(d_out, ones)
+    prob = jnp.exp(dot_back(q2, k) + bias - lse)
+    d_prob = dot_back(d2, v)
+    row = jnp.sum(prob * d_prob, axis=-1, keepdims=True)
+    d_scores = (prob * (d_prob - row)).astype(BF)
+    dq = dot(side(d_scores), both(k, scaled))
+    return dq, dot_grad(d_scores, q2), dot_grad(prob.astype(BF), d2)
+
+
+def reach_bias(key_bias):
+    shape = (WIN, 3 * WIN)
+    offset = lax.broadcasted_iota(jnp.int32, shape, 1) - lax.broadcasted_iota(jnp.int32, shape, 0) - WIN
+    near = (offset >= -WIN) & (offset <= WIN)
+    inner = jnp.where(offset == 0, 0.0, jnp.broadcast_to(key_bias, shape))
+    bias = jnp.where(near, inner, MASKED)
+    return jnp.concatenate([bias, bias], axis=0)
+
+
+def put_lse(lse, pair, column):
+    lane = lax.broadcasted_iota(jnp.int32, lse.shape, 1)
+    rows = lse.shape[0]
+    lse = jnp.where(lane == 2 * pair, column[:rows], lse)
+    return jnp.where(lane == 2 * pair + 1, column[rows:], lse)
+
+
+def get_lse(lse, pair):
+    return jnp.concatenate([lse[:, 2 * pair : 2 * pair + 1], lse[:, 2 * pair + 1 : 2 * pair + 2]], axis=0)
+
+
+def attend_kernel(
+    x,
+    gain,
+    select,
+    select_t,
+    key_bias,
+    heavy_bias,
+    w_lqkv,
+    w_hqkv,
+    w_lout,
+    w_hout,
+    hidden,
+    xn,
+    lq,
+    rim,
+    lo_out,
+    l_lse,
+    a_rows,
+    hq,
+    kvh,
+    ho,
+    h_lse,
+    ls,
+    lr,
+    rs,
+    rr,
+    ss,
+    sr,
+):
+    hi, lo, x_, c = place()
+    f = x_ * 2 + c
+    meet(line_peers())
+    tokens = x.shape[0]
+    group, cap, width = select.shape
+    wl, wh = HL * DH, HH * DH
+    ones, scaled = pair_masks(1.0), pair_masks(SCORE_SCALE)
+    across, partner = at(hi, lo, 1 - x_, c), at(hi, lo, x_, 1 - c)
+
+    def norm(r):
+        h = x[r, :].astype(F32)
+        inv = lax.rsqrt(jnp.mean(h * h, axis=-1, keepdims=True) + EPSILON)
+        xn[r, :] = (h * inv * gain[...]).astype(BF)
+
+    tiles(tokens, 128, norm)
+    for s in range(group):
+        rows = dot(select[s], xn[s * width : (s + 1) * width, :]).astype(BF)
+        a_rows[s * cap : (s + 1) * cap, :] = rows
+    kv = dot(a_rows[...], w_hqkv[:, wh:]).astype(BF)
+    for s in range(group):
+        kvh[s, f] = kv[s * cap : (s + 1) * cap]
+    mine = kvh.at[:, f]
+    first = send(mine, mine, ss.at[0], sr.at[0], across)
+    beside = send(mine, mine, ss.at[1], sr.at[1], partner)
+    for s in range(group):
+        rows = xn[s * width : (s + 1) * width, :]
+        rim[s, WIN : WIN + width, :] = dot(rows, w_lqkv[:, wl:]).astype(BF)
+    finish = rim_exchange(
+        rim.at[:, pl.ds(WIN, WIN)],
+        rim.at[:, pl.ds(width, WIN)],
+        rim.at[:, pl.ds(0, WIN)],
+        rim.at[:, pl.ds(width + WIN, WIN)],
+        ls,
+        lr,
+        rs,
+        rr,
+    )
+    hq[...] = dot(a_rows[...], w_hqkv[:, :wh]).astype(BF)
+    for s in range(group):
+        rows = slice(s * width, (s + 1) * width)
+        lq[rows, :] = dot(xn[rows, :], w_lqkv[:, :wl]).astype(BF)
+    first.wait()
+    other = kvh.at[:, (1 - x_) * 2 + c]
+    relay = send(other, other, ss.at[2], sr.at[2], partner)
+    finish()
+    blocks = width // WIN
+
+    def light(i, carry):
+        s, b = i // blocks, i % blocks
+        r = pl.ds(pl.multiple_of(i * WIN, WIN), WIN)
+        keys = pl.ds(pl.multiple_of(b * WIN, WIN), 3 * WIN)
+        bias = reach_bias(key_bias[i])
+        lse = jnp.zeros((WIN, 128), F32)
+        for pair in range(HL // 2):
+            at_k = slice(pair * 128, (pair + 1) * 128)
+            at_v = slice(wl + pair * 128, wl + (pair + 1) * 128)
+            o, column = pair_forward(
+                lq[r, at_k], rim[s, keys, at_k], rim[s, keys, at_v], bias, ones, scaled
+            )
+            lo_out[r, at_k] = o
+            lse = put_lse(lse, pair, column)
+        l_lse[r, :] = lse
+        return carry
+
+    lax.fori_loop(0, group * blocks, light, 0)
+    beside.wait()
+    relay.wait()
+    heavy_kv = kvh.reshape(group, 4 * cap, 2 * wh)
+
+    def heavy(s, carry):
+        r = pl.ds(pl.multiple_of(s * cap, cap), cap)
+        bias = heavy_bias[s]
+        bias = jnp.concatenate([bias, bias], axis=0)
+        lse = jnp.zeros((cap, 128), F32)
+        for pair in range(HH // 2):
+            at_k = slice(pair * 128, (pair + 1) * 128)
+            at_v = slice(wh + pair * 128, wh + (pair + 1) * 128)
+            o, column = pair_forward(
+                hq[r, at_k], heavy_kv[s, :, at_k], heavy_kv[s, :, at_v], bias, ones, scaled
+            )
+            ho[r, at_k] = o
+            lse = put_lse(lse, pair, column)
+        h_lse[r, :] = lse
+        return carry
+
+    lax.fori_loop(0, group, heavy, 0)
+    high, low = halves(dot(ho[...], w_hout[...]))
+    for s in range(group):
+        r = slice(s * width, (s + 1) * width)
+        q = slice(s * cap, (s + 1) * cap)
+        hidden[r, :] = (
+            x[r, :].astype(F32)
+            + dot(lo_out[r, :], w_lout[...])
+            + (dot(select_t[s], high[q]) + dot(select_t[s], low[q]))
+        )
+
+
+def attend(x, gain, select, select_t, key_bias, heavy_bias, w_lqkv, w_hqkv, w_lout, w_hout):
+    tokens = x.shape[0]
+    group, cap, width = select.shape
+    wl, wh = HL * DH, HH * DH
+    rows = group * cap
+    operands = [x, gain, select, select_t, key_bias, heavy_bias, w_lqkv, w_hqkv, w_lout, w_hout]
+    shapes = [
+        jax.ShapeDtypeStruct((tokens, D), F32),
+        jax.ShapeDtypeStruct((tokens, D), BF),
+        jax.ShapeDtypeStruct((tokens, wl), BF),
+        jax.ShapeDtypeStruct((group, width + 2 * WIN, 2 * wl), BF),
+        jax.ShapeDtypeStruct((tokens, wl), BF),
+        jax.ShapeDtypeStruct((tokens, 128), F32),
+        jax.ShapeDtypeStruct((rows, D), BF),
+        jax.ShapeDtypeStruct((rows, wh), BF),
+        jax.ShapeDtypeStruct((group, 4, cap, 2 * wh), BF),
+        jax.ShapeDtypeStruct((rows, wh), BF),
+        jax.ShapeDtypeStruct((rows, 128), F32),
+    ]
+    return call(
+        attend_kernel,
+        shapes,
+        operands,
+        [VM] * len(operands),
+        [VM] * len(shapes),
+        [DMA, DMA, DMA, DMA, DMA((3,)), DMA((3,))],
+        2,
+    )
+
+
+def attend_back_kernel(
+    d_hidden,
+    x,
+    gain,
+    select,
+    select_t,
+    key_bias,
+    heavy_bias,
+    w_lqkv,
+    w_hqkv,
+    w_lout,
+    w_hout,
+    xn,
+    lq,
+    rim,
+    lo_out,
+    l_lse,
+    a_rows,
+    hq,
+    kvh,
+    ho,
+    h_lse,
+    g_lqkv,
+    g_hqkv,
+    g_lout,
+    g_hout,
+    dx,
+    stats,
+    d_ho,
+    d_hproj,
+    part,
+    got,
+    far,
+    d_la,
+    d_lo,
+    d_rim,
+    edge,
+    edge_in,
+    d_lproj,
+    d_xn,
+    ls,
+    lr,
+    rs,
+    rr,
+    ss,
+    sr,
+):
+    hi, lo, x_, c = place()
+    meet(line_peers())
+    tokens = x.shape[0]
+    group, cap, width = select.shape
+    wl, wh = HL * DH, HH * DH
+    ones, scaled = pair_masks(1.0), pair_masks(SCORE_SCALE)
+    across, partner = at(hi, lo, 1 - x_, c), at(hi, lo, x_, 1 - c)
+    picked = []
+    for s in range(group):
+        high, low = halves(d_hidden[s * width : (s + 1) * width, :])
+        picked.append((dot(select[s], high) + dot(select[s], low)).astype(BF))
+    d_ha = jnp.concatenate(picked, axis=0)
+    d_ho[...] = dot_back(d_ha, w_hout[...]).astype(BF)
+    heavy_kv = kvh.reshape(group, 4 * cap, 2 * wh)
+    part_kv = part.reshape(group, 4 * cap, 2 * wh)
+
+    def heavy(s, carry):
+        r = pl.ds(pl.multiple_of(s * cap, cap), cap)
+        bias = heavy_bias[s]
+        bias = jnp.concatenate([bias, bias], axis=0)
+        lse = h_lse[r, :]
+        for pair in range(HH // 2):
+            at_k = slice(pair * 128, (pair + 1) * 128)
+            at_v = slice(wh + pair * 128, wh + (pair + 1) * 128)
+            dq, dk, dv = pair_backward(
+                hq[r, at_k],
+                heavy_kv[s, :, at_k],
+                heavy_kv[s, :, at_v],
+                bias,
+                get_lse(lse, pair),
+                d_ho[r, at_k],
+                ones,
+                scaled,
+            )
+            d_hproj[r, at_k] = dq.astype(BF)
+            part_kv[s, :, at_k] = dk.astype(BF)
+            part_kv[s, :, at_v] = dv.astype(BF)
+        return carry
+
+    lax.fori_loop(0, group, heavy, 0)
+    beside = [
+        send(part.at[:, b * 2 + 1 - c], got.at[b], ss.at[b], sr.at[b], partner) for b in (0, 1)
+    ]
+    g_hout[...] = dot_grad(ho[...], d_ha).astype(BF)
+
+    def light_out_back(r):
+        d = d_hidden[r, :].astype(BF)
+        d_la[r, :] = d
+        d_lo[r, :] = dot_back(d, w_lout[...]).astype(BF)
+
+    tiles(tokens, 256, light_out_back)
+    for copy in beside:
+        copy.wait()
+    for b in (0, 1):
+        got[b] = (got[b].astype(F32) + part[:, b * 2 + c].astype(F32)).astype(BF)
+    third = send(got.at[1 - x_], far, ss.at[2], sr.at[2], across)
+    d_rim[...] = jnp.zeros(d_rim.shape, F32)
+    blocks = width // WIN
+
+    def light(i, carry):
+        s, b = i // blocks, i % blocks
+        r = pl.ds(pl.multiple_of(i * WIN, WIN), WIN)
+        keys = pl.ds(pl.multiple_of(b * WIN, WIN), 3 * WIN)
+        bias = reach_bias(key_bias[i])
+        lse = l_lse[r, :]
+        for pair in range(HL // 2):
+            at_k = slice(pair * 128, (pair + 1) * 128)
+            at_v = slice(wl + pair * 128, wl + (pair + 1) * 128)
+            dq, dk, dv = pair_backward(
+                lq[r, at_k],
+                rim[s, keys, at_k],
+                rim[s, keys, at_v],
+                bias,
+                get_lse(lse, pair),
+                d_lo[r, at_k],
+                ones,
+                scaled,
+            )
+            d_lproj[r, at_k] = dq.astype(BF)
+            d_rim[s, keys, at_k] += dk
+            d_rim[s, keys, at_v] += dv
+        return carry
+
+    lax.fori_loop(0, group * blocks, light, 0)
+    edge[0] = d_rim[:, :WIN, :].astype(BF)
+    edge[1] = d_rim[:, WIN + width :, :].astype(BF)
+    finish = rim_exchange(
+        edge.at[0], edge.at[1], edge_in.at[0], edge_in.at[1], ls, lr, rs, rr
+    )
+    g_lout[...] = dot_grad(lo_out[...], d_la[...]).astype(BF)
+    third.wait()
+    total = (got[x_].astype(F32) + far[...].astype(F32)).astype(BF)
+    for s in range(group):
+        d_hproj[s * cap : (s + 1) * cap, wh:] = total[s]
+
+    def heavy_grad(j):
+        g_hqkv[:, j] = dot_grad(a_rows[...], d_hproj[:, j]).astype(BF)
+
+    tiles(3 * wh, 768, heavy_grad)
+    d_high, d_low = halves(dot_back(d_hproj[...], w_hqkv[...]))
+    finish()
+    for s in range(group):
+        d_rim[s, WIN : 2 * WIN, :] += edge_in[0, s].astype(F32)
+        d_rim[s, width : width + WIN, :] += edge_in[1, s].astype(F32)
+        d_lproj[s * width : (s + 1) * width, wl:] = d_rim[s, WIN : WIN + width, :].astype(BF)
+
+    def light_grad(j):
+        g_lqkv[:, j] = dot_grad(xn[...], d_lproj[:, j]).astype(BF)
+
+    tiles(3 * wl, 768, light_grad)
+    for s in range(group):
+        r = slice(s * width, (s + 1) * width)
+        q = slice(s * cap, (s + 1) * cap)
+        d_xn[r, :] = dot_back(d_lproj[r, :], w_lqkv[...]) + (
+            dot(select_t[s], d_high[q]) + dot(select_t[s], d_low[q])
+        )
+    stats[...] = jnp.zeros(stats.shape, F32)
+
+    def norm_back(r):
+        h = x[r, :].astype(F32)
+        inv = lax.rsqrt(jnp.mean(h * h, axis=-1, keepdims=True) + EPSILON)
+        d = d_xn[r, :]
+        dh = d * h
+        stats[0:1, :] += jnp.sum(dh * inv, axis=0, keepdims=True)
+        mean = jnp.mean(gain[...] * dh, axis=-1, keepdims=True)
+        dx[r, :] = (
+            d_hidden[r, :] + inv * gain[...] * d - h * (inv * inv * inv * mean)
+        ).astype(BF)
+
+    tiles(tokens, 128, norm_back)
+
+
+def attend_back(d_hidden, x, gain, select, select_t, key_bias, heavy_bias, weights, saved):
+    tokens = x.shape[0]
+    group, cap, width = select.shape
+    wl, wh = HL * DH, HH * DH
+    rows = group * cap
+    operands = [d_hidden, x, gain, select, select_t, key_bias, heavy_bias, *weights, *saved]
+    shapes = [
+        jax.ShapeDtypeStruct((D, 3 * wl), BF),
+        jax.ShapeDtypeStruct((D, 3 * wh), BF),
+        jax.ShapeDtypeStruct((wl, D), BF),
+        jax.ShapeDtypeStruct((wh, D), BF),
+        jax.ShapeDtypeStruct((tokens, D), BF),
+        jax.ShapeDtypeStruct((8, D), F32),
+    ]
+    return call(
+        attend_back_kernel,
+        shapes,
+        operands,
+        [VM] * len(operands),
+        [VM] * len(shapes),
+        [
+            pltpu.VMEM((rows, wh), BF),
+            pltpu.VMEM((rows, 3 * wh), BF),
+            pltpu.VMEM((group, 4, cap, 2 * wh), BF),
+            pltpu.VMEM((2, group, cap, 2 * wh), BF),
+            pltpu.VMEM((group, cap, 2 * wh), BF),
+            pltpu.VMEM((tokens, D), BF),
+            pltpu.VMEM((tokens, wl), BF),
+            pltpu.VMEM((group, width + 2 * WIN, 2 * wl), F32),
+            pltpu.VMEM((2, group, WIN, 2 * wl), BF),
+            pltpu.VMEM((2, group, WIN, 2 * wl), BF),
+            pltpu.VMEM((tokens, 3 * wl), BF),
+            pltpu.VMEM((tokens, D), F32),
+            DMA,
+            DMA,
+            DMA,
+            DMA,
+            DMA((3,)),
+            DMA((3,)),
+        ],
+        3,
+    )
+
+
 def scatter_kernel(dp, nw, *refs):
     nz = dp // 2
     dx, stats, gs, hin, hdn = refs[0], refs[1], refs[2 : 2 + nw], refs[2 + nw], refs[3 + nw]
@@ -927,92 +1260,6 @@
     )
 
 
-def rms_norm(value, gain):
-    return value * lax.rsqrt(jnp.mean(value * value, axis=-1, keepdims=True) + EPSILON) * gain
-
-
-def split_heads(rows, heads):
-    return rows.reshape(rows.shape[0], rows.shape[1], heads, -1)
-
-
-def head_scores(queries, key_rows, allowed, heads):
-    scores = (
-        jnp.einsum(
-            "sqhd,skhd->shqk",
-            split_heads(queries, heads),
-            split_heads(key_rows, heads),
-            preferred_element_type=F32,
-        )
-        * SCORE_SCALE
-    )
-    return jnp.where(allowed[:, None], scores, MASKED)
-
-
-def attend_forward(queries, key_rows, value_rows, allowed, heads):
-    scores = head_scores(queries, key_rows, allowed, heads)
-    row_max = jnp.max(scores, axis=-1, keepdims=True)
-    shifted = jnp.exp(scores - row_max)
-    row_sum = jnp.sum(shifted, axis=-1, keepdims=True)
-    attn_prob = (shifted / row_sum).astype(BF)
-    attended = jnp.einsum(
-        "shqk,skhd->sqhd", attn_prob, split_heads(value_rows, heads), preferred_element_type=F32
-    )
-    return (attended.reshape(queries.shape).astype(BF), row_max + jnp.log(row_sum))
-
-
-def attend_backward(queries, key_rows, value_rows, allowed, log_sum, d_attended, heads):
-    scores = head_scores(queries, key_rows, allowed, heads)
-    attn_prob = jnp.exp(scores - log_sum)
-    d_heads = split_heads(d_attended, heads)
-    d_prob = jnp.einsum(
-        "sqhd,skhd->shqk", d_heads, split_heads(value_rows, heads), preferred_element_type=F32
-    )
-    row_dot = jnp.sum(attn_prob * d_prob, axis=-1, keepdims=True)
-    d_scores = (attn_prob * (d_prob - row_dot)).astype(BF)
-    d_query = (
-        jnp.einsum(
-            "shqk,skhd->sqhd", d_scores, split_heads(key_rows, heads), preferred_element_type=F32
-        )
-        * SCORE_SCALE
-    )
-    d_key = (
-        jnp.einsum(
-            "shqk,sqhd->skhd", d_scores, split_heads(queries, heads), preferred_element_type=F32
-        )
-        * SCORE_SCALE
-    )
-    d_value = jnp.einsum(
-        "shqk,sqhd->skhd", attn_prob.astype(BF), d_heads, preferred_element_type=F32
-    )
-    return (
-        d_query.reshape(queries.shape),
-        d_key.reshape(key_rows.shape),
-        d_value.reshape(value_rows.shape),
-    )
-
-
-def mul(left, right):
-    return jnp.einsum("...d,de->...e", left, right, preferred_element_type=F32)
-
-
-def mul_back(left, right):
-    return jnp.einsum("...e,de->...d", left, right, preferred_element_type=F32)
-
-
-def weight_grad(left, right):
-    a = left.reshape(-1, left.shape[-1])
-    b = right.reshape(-1, right.shape[-1])
-    return jnp.einsum("pd,pe->de", a, b, preferred_element_type=F32)
-
-
-def pick(spec, hot, value):
-    high = value.astype(BF)
-    rest = (value - high.astype(F32)).astype(BF)
-    return jnp.einsum(spec, hot, high, preferred_element_type=F32) + jnp.einsum(
-        spec, hot, rest, preferred_element_type=F32
-    )
-
-
 def routing(routes, pieces, piece_len):
     places = jnp.arange(pieces * piece_len)
     routed = jnp.any(routes[:, None, :] == places[None, :, None], axis=-1)
@@ -1072,7 +1319,6 @@
         hin_src = hin_src.reshape(8, -1, 128)
     got = gather_all(dp, xin, [gains] + [packed(m) for m in matrices], hin_src, heavy_down)
     tokens = layer_input.shape[2] * dp
-    inputs = got[0].reshape(group, tokens, D).astype(F32)
     gain_rows = got[1].reshape(n, 8, 128)
     gain_one = gain_rows[:, 0, :gain_len].reshape(-1).astype(F32)
     gain_two = gain_rows[:, 1, :gain_len].reshape(-1).astype(F32)
@@ -1099,42 +1345,24 @@
     slot_score = jnp.sum(
         jnp.where(f_spot[:, :, None] == ffn_pick[:, None, :], score_pick[:, None, :], 0.0), axis=-1
     )
-    width_light = HL * DH
-    width_heavy = HH * DH
-    normed = rms_norm(inputs, gain_one).astype(BF)
-    light_proj = mul(normed, w_lqkv).astype(BF)
-    l_query = light_proj[..., :width_light]
-    own_pair = light_proj[..., width_light:]
-    a_rows = jnp.einsum("scp,spd->scd", a_select, normed, preferred_element_type=F32).astype(BF)
-    heavy_proj = mul(a_rows, w_hqkv).astype(BF)
-    h_query = heavy_proj[..., :width_heavy]
-    from_left, from_right, kv_every = exchange_keys(
-        own_pair[:, :WIN], own_pair[:, tokens - WIN :], heavy_proj[..., width_heavy:]
-    )
-    rim_pair = jnp.concatenate([from_left, own_pair, from_right], axis=1)
-    rim_keys = rim_pair[..., :width_light]
-    rim_values = rim_pair[..., width_light:]
     key_pos = piece * tokens - WIN + jnp.arange(tokens + 2 * WIN)
-    within_reach = (jnp.abs(positions[:, None] - key_pos[None, :]) <= WIN) & (key_pos >= 0)[None, :]
-    live_key = key_pos[None, :] < seq_lengths[:, None]
-    light_allowed = within_reach[None] & (
-        live_key[:, None, :] | (positions[:, None] == key_pos[None, :])[None]
-    )
-    l_att, l_lse = attend_forward(l_query, rim_keys, rim_values, light_allowed, HL)
-    light_branch = mul(l_att, w_lout)
-    kv_every = kv_every.reshape(group, pieces * CAP, 2 * width_heavy)
+    live_key = (key_pos >= 0)[None, :] & (key_pos[None, :] < seq_lengths[:, None])
+    key_line = jnp.where(live_key, 0.0, MASKED)
+    key_bias = jnp.stack(
+        [key_line[:, b : b + 3 * WIN] for b in range(0, tokens, WIN)], axis=1
+    ).reshape(-1, 1, 3 * WIN)
     all_spots = a_spots.reshape(group, pieces * CAP)
     heavy_allowed = ((all_spots >= 0) & (all_spots < seq_lengths[:, None]))[:, None, :] | (
         a_spot[:, :, None] == all_spots[:, None, :]
     )
-    hv_keys = kv_every[..., :width_heavy]
-    hv_values = kv_every[..., width_heavy:]
-    h_att, h_lse = attend_forward(h_query, hv_keys, hv_values, heavy_allowed, HH)
-    heavy_branch = mul(h_att, w_hout)
-    hidden = inputs + light_branch + pick("scp,scd->spd", a_select, heavy_branch)
+    heavy_bias = jnp.where(heavy_allowed, 0.0, MASKED)
+    flat_x = got[0].reshape(-1, D)
+    masks = (a_select, a_select.swapaxes(1, 2), key_bias, heavy_bias)
+    attn_weights = (w_lqkv, w_hqkv, w_lout, w_hout)
+    hidden, *saved = attend(flat_x, gain_one.reshape(1, D), *masks, *attn_weights)
     weight_mask = valid_mask.reshape(-1, 1).astype(F32)
     grad_lin, grad_ldown, grad_hin, grad_hdown, d_hidden, ffn_stats = feed_forward(
-        hidden.reshape(-1, D),
+        hidden,
         f_select,
         f_select.swapaxes(1, 2),
         slot_score.reshape(-1, 1),
@@ -1147,48 +1375,13 @@
         w_hin,
         w_hdown,
     )
-    d_hidden = d_hidden.reshape(group, tokens, D)
-    d_heavy_attn = pick("scp,spd->scd", a_select, d_hidden).astype(BF)
-    grad_hout = weight_grad(h_att, d_heavy_attn)
-    d_h_att = mul_back(d_heavy_attn, w_hout).astype(BF)
-    dq_heavy, dk_heavy, dv_heavy = attend_backward(
-        h_query, hv_keys, hv_values, heavy_allowed, h_lse, d_h_att, HH
-    )
-    kv_part = jnp.concatenate([dk_heavy, dv_heavy], axis=-1).astype(BF)
-    d_light_attn = d_hidden.astype(BF)
-    grad_lout = weight_grad(l_att, d_light_attn)
-    d_l_att = mul_back(d_light_attn, w_lout).astype(BF)
-    dq_light, dk_light, dv_light = attend_backward(
-        l_query, rim_keys, rim_values, light_allowed, l_lse, d_l_att, HL
-    )
-    rim_grads = jnp.concatenate([dk_light, dv_light], axis=-1)
-    back_left, back_right, kv_grads = exchange_key_grads(
-        rim_grads[:, :WIN].astype(BF),
-        rim_grads[:, tokens + WIN :].astype(BF),
-        kv_part.reshape(group, pieces, CAP, 2 * width_heavy),
-    )
-    d_h_proj = jnp.concatenate([dq_heavy.astype(BF), kv_grads.astype(BF)], axis=-1)
-    grad_hqkv = weight_grad(a_rows, d_h_proj)
-    d_a_rows = mul_back(d_h_proj, w_hqkv)
-    own_grads = rim_grads[:, WIN : WIN + tokens]
-    own_grads = jnp.concatenate(
-        [
-            own_grads[:, :WIN] + back_left.astype(F32),
-            own_grads[:, WIN : tokens - WIN],
-            own_grads[:, tokens - WIN :] + back_right.astype(F32),
-        ],
-        axis=1,
-    )
-    d_l_proj = jnp.concatenate([dq_light.astype(BF), own_grads.astype(BF)], axis=-1)
-    grad_lqkv = weight_grad(normed, d_l_proj)
-    d_normed = pick("scp,scd->spd", a_select, d_a_rows) + mul_back(d_l_proj, w_lqkv)
-    _, first_pull = jax.vjp(rms_norm, inputs, gain_one)
-    d_inputs_norm, grad_gain_one = first_pull(d_normed)
-    d_inputs = d_hidden + d_inputs_norm
+    grad_lqkv, grad_hqkv, grad_lout, grad_hout, d_inputs, attn_stats = attend_back(
+        d_hidden, flat_x, gain_one.reshape(1, D), *masks, attn_weights, saved
+    )
     rows = tokens // dp
     stats = jnp.concatenate(
         [
-            grad_gain_one.reshape(-1, 128),
+            attn_stats[0].reshape(-1, 128),
             ffn_stats[0].reshape(-1, 128),
             jnp.broadcast_to(jnp.sum(ffn_stats[1]), (4, 128)),
         ]
@@ -1201,7 +1394,7 @@
     hin_tile = hin_src.shape[1:]
     done = scatter_all(
         dp,
-        d_inputs.astype(BF).reshape(group, dp, rows, D),
+        d_inputs.reshape(group, dp, rows, D),
         stats,
         sent,
         grad_hin.astype(BF).reshape((nz, 8) + hin_tile),

time: 542 us -> 449 us (0.83)
  matrix products: 55.6 us -> 0.3 us
  local copies, waits for them, and re-layouts: 59.4 us -> 21.4 us
  Pallas kernels: 382 us -> 407 us
  other arithmetic: 33 us -> 13.4 us
    dot_general x31 -> x0, matrix products: 55.3 us -> none  [the longest x4 9.79 us: weight_grad(): return jnp.einsum('pd,pe->de', a, b, preferred_element_type=F32)]
    pallas_call x5, Pallas kernels: 378 us -> 403 us  [call(): pl.pallas_call(kernel, out_shape=out_shape, in_specs=in_specs, out_specs=...]
    slice x14 -> x1, local copies, waits for them, and re-layouts: 12.1 us -> 0.75 us  [local(): attn_stats[0].reshape(-1, 128)]
    concatenate x5 -> x1, local copies, waits for them, and re-layouts: 9.74 us -> 0.07 us  [local(): jnp.concatenate([attn_stats[0].reshape(-1, 128), ffn_stats[0].reshape(-1,...]
    reshape x4 -> x1, local copies, waits for them, and re-layouts: 8.67 us -> 0.61 us  [local(): key_bias = jnp.stack([key_line[:, b:b + 3 * WIN] for b in range(0, tokens...]
    unnamed x99 -> x29, local copies, waits for them, and re-layouts: 15.8 us -> 8.84 us
    convert_element_type x7 -> x0, other arithmetic: 6.87 us -> none  [the longest x2 4.91 us: attend_backward(): d_scores = (attn_prob * (d_prob - row_dot)).astype(BF)]
where the time goes in v3:
time: 449 us; the launch traced here: 446 us
  Pallas kernels  407 us (91%)
  local copies, waits for them, and re-layouts  21.4 us (5%)
  other arithmetic  13.4 us (3%)
    pallas_call x5, Pallas kernels, call(): pl.pallas_call(kernel, out_shape=out_shape, in_specs=in_specs, out_specs=...  403 us

profile of v3, /device:TPU:0, one launch (start us, length us, event | category | flops | bytes accessed | tf_op | source)
XLA Modules:
  0.0 445.8 jit_solution(1804716158161494826)
XLA Ops:
  0.7 0.7 dynamic_slice.23
  1.4 1.3 reduce_sum.88
  3.3 0.8 select_reduce_fusion.6
  4.2 0.1 iota_compare_fusion.7
  4.3 0.8 select_reduce_fusion.3
  5.0 0.1 and_select_fusion
  5.1 0.8 select_reduce_fusion.4
  5.9 0.1 fusion.21
  6.0 1.2 fusion.18.refs_1_
  7.3 0.6 reshape.288.key_bias
  7.9 0.4 fusion
  8.2 0.4 fusion.2
  8.6 0.2 fusion.5
  8.8 0.2 fusion.7
  8.9 1.6 select_reduce_fusion
  10.5 0.9 copy.85
  11.3 1.1 copy.81
  12.4 0.2 copy.92
  12.6 1.0 reshape.285.refs_8_
  13.6 1.4 fusion.24
  15.0 0.2 select_reduce_fusion.2
  15.2 0.1 select_n.74
  15.3 0.7 fusion.11
  16.0 0.7 fusion.9
  16.7 0.7 copy.66.select
  17.4 0.1 fusion.19
  17.5 0.8 reshape.321.score
  18.3 0.7 copy.70.select
  19.0 0.7 or_select_fusion.heavy_bias
  19.7 0.9 copy.83
  20.6 2.2 shard_map.256.refs_0_
  22.8 140.9 %shard_map.257 = (bf16[2,8,32,768]{3,2,1,0:T(8,128)(2,1)}, bf16[4,2,2,2,8,128]{5,4,3,2,1,0:T(8,128)(2,1)}, bf16[4,2,2,2,24,1536]{5,4,3,2,1,0:T(8,128)(2,1)}, bf1...) custom-call(bf16[16,32,768]{2,1,0:T(8,128)(2,1)} %shard_map.256.refs, ...), custom_call_target="tpu_custom_call" | custom-call | tf_op jit(solution)/shard_map/pallas_call | solution.py:72
  163.7 0.9 fusion.26
  164.6 0.7 reshape.313.gain
  165.3 0.7 reshape.310.gain
  166.0 27.7 %shard_map.258 = (f32[512,768]{1,0:T(8,128)}, bf16[512,768]{1,0:T(8,128)(2,1)}, bf16[512,512]{1,0:T(8,128)(2,1)}, bf16[2,512,1024]{2,1,0:T(8,128)(2,1)}, bf16[51...) custom-call(bf16[512,768]{1,0:T(8,128)(2,1)} %bitcast.92, ...), custom_call_target="tpu_custom_call" | custom-call | tf_op jit(solution)/shard_map/pallas_call | solution.py:72
  193.6 72.6 %shard_map.259 = (bf16[768,2048]{1,0:T(8,128)(2,1)}, bf16[1024,768]{1,0:T(8,128)(2,1)}, bf16[768,1024]{1,0:T(8,128)(2,1)}, bf16[512,768]{1,0:T(8,128)(2,1)}, f32[512,768]{1,0:T(8,128)}, /*index=5*/f32[8,768]{1,0:T(8,128)}) custom-call(f32[512,768]{1,0:T(8,128)} %get-tuple-element.61.hidden, bf16[2,64,256]{2,1,0:T(8,128)(2,1)} %copy.70.select, ...), custom_call_target="tpu_custom_call" | custom-call | tf_op jit(solution)/shard_map/pallas_call | solution.py:72
  266.2 35.7 %shard_map.260 = (bf16[768,1536]{1,0:T(8,128)(2,1)}, bf16[768,2304]{1,0:T(8,128)(2,1)}, bf16[512,768]{1,0:T(8,128)(2,1)}, bf16[768,768]{1,0:T(8,128)(2,1)}, bf16[512,768]{1,0:T(8,128)(2,1)}, /*index=5*/f32[8,768]{1,0:T(8,128)}) custom-call(f32[512,768]{1,0:T(8,128)} %get-tuple-element.66.d_hidden, bf16[512,768]{1,0:T(8,128)(2,1)} %bitcast.93, ...), custom_call_target="tpu_custom_call" | custom-call | tf_op jit(solution)/shard_map/pallas_call | solution.py:72
  301.9 0.8 slice_reduce_fusion.2
  302.7 1.4 slice_reduce_fusion
  304.1 0.6 broadcast_in_dim.165
  304.8 0.1 pad.7.clone
  304.9 0.7 maximum_maximum_fusion.refs_1_
  305.5 125.9 %shard_map.261 = (bf16[8,2,32,768]{3,2,1,0:T(8,128)(2,1)}, f32[16,128]{1,0:T(8,128)}, f32[24,2048]{1,0:T(8,128)}, f32[32,768]{1,0:T(8,128)}, f32[24,768]{1,0:T(8...) custom-call(bf16[2,8,32,768]{3,2,1,0:T(8,128)(2,1)} %bitcast.112, ...), custom_call_target="tpu_custom_call" | custom-call | tf_op jit(solution)/shard_map/pallas_call | solution.py:72
  431.4 0.0 copy-start.1
  431.4 1.2 slice.37
  433.3 0.8 slice_bitcast_fusion
  434.1 0.6 dynamic_slice.29
  434.7 0.6 dynamic_slice.28
  435.2 2.5 shard_map.262
  437.7 0.0 copy-done.1
  437.7 0.3 reshape.319
  438.1 0.0 copy-start.4
  438.1 0.5 copy.75
  438.6 1.3 copy.91
  439.9 0.0 copy-done.4
  440.0 0.7 copy.100
  440.6 0.6 copy.101
  441.2 0.7 copy.102
  441.9 0.6 copy.103
  442.6 0.7 copy.104
  443.2 0.6 copy.105
  443.9 0.0 copy-done
  443.9 0.7 copy.106
  (26 shorter events, 0.1 us)
Async XLA Ops:
  431.4 6.3 %copy-start.1 = (bf16[8,24,1024]{2,1,0:T(8,128)(2,1)S(1)}, bf16[8,24,1024]{2,1,0:T(8,128)(2,1)}, u32[]{:S(2)}) copy-start(bf16[8,24,1024]{2,1,0:T(8,128)(2,1)} %get-tuple-element.96) | copy-start | bytes 1179652
  438.1 1.9 copy-start.4
  438.1 2.5 copy-start.7
  438.1 3.1 copy-start.2
  438.6 3.4 copy-start.6
  438.6 4.0 copy-start.3
  438.6 4.7 %copy-start.5 = (f32[32,768]{1,0:T(8,128)S(1)}, f32[32,768]{1,0:T(8,128)}, u32[]{:S(2)}) copy-start(f32[32,768]{1,0:T(8,128)} %get-tuple-element.181) | copy-start | bytes 294916
  438.6 5.3 %copy-start = (f32[128,768]{1,0:T(8,128)S(1)}, f32[128,768]{1,0:T(8,128)}, u32[]{:S(2)}) copy-start(f32[128,768]{1,0:T(8,128)} %get-tuple-element.183) | copy-start | bytes 1179652

commit v4 on v3

--- a/solution.py
+++ b/solution.py
@@ -128,127 +128,211 @@
     return gathered.reshape(-1, rows, columns).reshape(-1, columns)
 
 
-def gather_kernel(dp, nw, *refs):
-    nz = dp // 2
-    xin, ws, hin, hdn = refs[0], refs[1 : 1 + nw], refs[1 + nw], refs[2 + nw]
-    outs = refs[3 + nw :]
-    xo, wos, hin_o, hdn_o = outs[0], outs[1 : 1 + nw], outs[1 + nw], outs[2 + nw]
-    loc, xs, xr, zs, zr, ps, pr, cs, cr, hs, hr = outs[3 + nw :]
+def plane_others():
     hi, lo, x, c = place()
-    d = hi * 2 + lo
-    f = x * 2 + c
-    plane = (lo * 2 + x) * 2 + c
-    group = xin.shape[0] // dp
-    dp_peers = [(lax.rem(d + k, dp), f) for k in range(1, dp)]
-    rest = [(a, b, e) for a in (0, 1) for b in (0, 1) for e in (0, 1) if a or b or e]
-    flat8 = []
-    for a, b, e in rest:
-        l2 = 1 - lo if a else lo
-        x2 = 1 - x if b else x
-        c2 = 1 - c if e else c
-        flat8.append((l2, x2, c2))
-    meet(dp_peers + [at(hi, *p) for (a, b, e), p in zip(rest, flat8) if b or e])
-    locals_ = [keep(ws[w], wos[w].at[hi, lo, x, c], loc.at[w]) for w in range(nw)]
-    locals_.append(keep(xin.at[pl.ds(d * group, group)], xo.at[:, d], loc.at[nw]))
-    locals_.append(keep(hin.at[plane], hin_o.at[hi, plane], loc.at[nw + 1]))
-    locals_.append(keep(hdn, hdn_o.at[hi], loc.at[nw + 2]))
-    x_sends = []
-    for k, peer in enumerate(dp_peers):
-        x_sends.append(
-            send(xin.at[pl.ds(peer[0] * group, group)], xo.at[:, d], xs.at[k], xr.at[k], peer)
-        )
-    z_peers = [at(lax.rem(hi + k, nz), lo, x, c) for k in range(1, nz)]
-    z_sends = [
-        [
-            send(ws[w], wos[w].at[hi, lo, x, c], zs.at[w, k], zr.at[w, k], peer)
-            for k, peer in enumerate(z_peers)
+    others = []
+    for a in (0, 1):
+        for b in (0, 1):
+            for e in (0, 1):
+                if a or b or e:
+                    others.append(
+                        (1 - lo if a else lo, 1 - x if b else x, 1 - c if e else c, b or e)
+                    )
+    return others
+
+
+class Gather:
+    def __init__(self, dp, xin, ws, hin, hdn, xo, wos, hin_o, hdn_o, sems):
+        self.dp, self.nz = dp, dp // 2
+        self.xin, self.ws, self.hin, self.hdn = xin, ws, hin, hdn
+        self.xo, self.wos, self.hin_o, self.hdn_o = xo, wos, hin_o, hdn_o
+        self.loc, self.xs, self.xr, self.zs, self.zr = sems[:5]
+        self.ps, self.pr, self.cs, self.cr, self.hs, self.hr = sems[5:]
+        self.hi, self.lo, self.x, self.c = place()
+        hi, lo, x, c = place()
+        self.d = hi * 2 + lo
+        self.home = (lo * 2 + x) * 2 + c
+        self.rows_to = [(lax.rem(self.d + k, dp), x * 2 + c) for k in range(1, dp)]
+        self.z_to = [at(lax.rem(hi + k, self.nz), lo, x, c) for k in range(1, self.nz)]
+        self.others = plane_others()
+        nw = len(ws)
+        self.kept, self.z, self.p, self.f, self.k = ([None] * nw for _ in range(5))
+
+    def shard(self, w, z, lo, x):
+        full, rows = self.wos[w], self.ws[w].shape[0]
+        if len(full.shape) == 6:
+            return full.at[z, lo, x, self.c]
+        return full.at[z, lo, x, pl.ds(pl.multiple_of(self.c * rows, 8), rows)]
+
+    def meet(self):
+        peers = self.rows_to + [at(self.hi, *q[:3]) for q in self.others if q[3]]
+        meet(peers)
+
+    def rows(self):
+        group = self.xin.shape[0] // self.dp
+        nw = len(self.ws)
+        spot = self.xo.at[:, self.d]
+        self.own = keep(self.xin.at[pl.ds(self.d * group, group)], spot, self.loc.at[nw])
+        self.moved = [
+            send(self.xin.at[pl.ds(to[0] * group, group)], spot, self.xs.at[k], self.xr.at[k], to)
+            for k, to in enumerate(self.rows_to)
         ]
-        for w in range(nw)
-    ]
-    h_sends = []
-    for k, (l2, x2, c2) in enumerate(flat8):
-        h_sends.append(
+
+    def rows_ready(self):
+        self.own.wait()
+        for copy in self.moved:
+            copy.wait()
+
+    def line(self, w):
+        spot = self.shard(w, self.hi, self.lo, self.x)
+        self.kept[w] = keep(self.ws[w], spot, self.loc.at[w])
+        self.z[w] = [
+            send(self.ws[w], spot, self.zs.at[w, k], self.zr.at[w, k], to)
+            for k, to in enumerate(self.z_to)
+        ]
+
+    def onward(self, part, w, k, to, sems):
+        return send(part, part, sems[0].at[w, k], sems[1].at[w, k], to)
+
+    def plane(self, w):
+        self.kept[w].wait()
+        for copy in self.z[w]:
+            copy.wait()
+        hi, lo, x, c = self.hi, self.lo, self.x, self.c
+        column = self.shard(w, slice(None), lo, x)
+        plane = (self.ps, self.pr)
+        self.p[w] = [
+            self.onward(column, w, 0, at(hi, lo, 1 - x, c), plane),
+            self.onward(column, w, 1, at(hi, 1 - lo, x, c), plane),
+        ]
+        self.k[w] = [self.onward(column, w, 0, at(hi, lo, x, 1 - c), (self.cs, self.cr))]
+
+    def cross(self, w):
+        hi, lo, x, c = self.hi, self.lo, self.x, self.c
+        plane, core, half = (self.ps, self.pr), (self.cs, self.cr), self.nz // 2
+        partner = at(hi, lo, x, 1 - c)
+        self.p[w][1].wait()
+        part = self.shard(w, pl.ds(0, half), 1 - lo, x)
+        first = self.onward(part, w, 2, at(hi, lo, 1 - x, c), plane)
+        self.p[w][0].wait()
+        part = self.shard(w, pl.ds(half, self.nz - half), lo, 1 - x)
+        self.f[w] = [first, self.onward(part, w, 3, at(hi, 1 - lo, x, c), plane)]
+        for k, part in ((1, (1 - lo, x)), (2, (lo, 1 - x))):
+            self.k[w].append(
+                self.onward(self.shard(w, slice(None), *part), w, k, partner, core)
+            )
+
+    def core(self, w):
+        for copy in self.f[w]:
+            copy.wait()
+        part = self.shard(w, slice(None), 1 - self.lo, 1 - self.x)
+        partner = at(self.hi, self.lo, self.x, 1 - self.c)
+        self.k[w].append(self.onward(part, w, 3, partner, (self.cs, self.cr)))
+
+    def ready(self, w):
+        for copy in self.k[w]:
+            copy.wait()
+
+    def heavy_plane(self):
+        nw, hi = len(self.ws), self.hi
+        spot = self.hin_o.at[hi, self.home]
+        self.h_own = [
+            keep(self.hin.at[self.home], spot, self.loc.at[nw + 1]),
+            keep(self.hdn, self.hdn_o.at[hi], self.loc.at[nw + 2]),
+        ]
+        self.h_near = [
             send(
-                hin.at[(l2 * 2 + x2) * 2 + c2],
-                hin_o.at[hi, plane],
-                hs.at[0, k],
-                hr.at[0, k],
-                at(hi, l2, x2, c2),
+                self.hin.at[(q[0] * 2 + q[1]) * 2 + q[2]],
+                spot,
+                self.hs.at[0, k],
+                self.hr.at[0, k],
+                at(hi, *q[:3]),
             )
-        )
-    quad = quad_peers()
-    partner = at(hi, lo, x, 1 - c)
-    p_sends, c_sends = [], []
-
-    def forward_plane(w):
-        locals_[w].wait()
-        for copy in z_sends[w]:
+            for k, q in enumerate(self.others)
+        ]
+
+    def heavy_line(self):
+        for copy in self.h_own + self.h_near:
             copy.wait()
-        column = wos[w].at[:, lo, x, c]
-        p_sends.append(
-            [
-                send(column, column, ps.at[w, k], pr.at[w, k], at(hi, l2, x2, c))
-                for k, (l2, x2) in enumerate(quad)
-            ]
-        )
-        c_sends.append([send(column, column, cs.at[w, 0], cr.at[w, 0], partner)])
-
-    def forward_core(w):
-        for k, (l2, x2) in enumerate(quad):
-            p_sends[w][k].wait()
-            column = wos[w].at[:, l2, x2, c]
-            c_sends[w].append(send(column, column, cs.at[w, k + 1], cr.at[w, k + 1], partner))
-
-    for w in range(nw):
-        forward_plane(w)
-        if w >= 1:
-            forward_core(w - 1)
-    for copy in h_sends:
-        copy.wait()
-    locals_[nw + 1].wait()
-    late = []
-    for k, peer in enumerate(z_peers):
-        late.append(send(hin_o.at[hi], hin_o.at[hi], hs.at[1, k], hr.at[1, k], peer))
-        late.append(send(hdn, hdn_o.at[hi], hs.at[2, k], hr.at[2, k], peer))
-    forward_core(nw - 1)
-    locals_[nw].wait()
-    locals_[nw + 2].wait()
-    for copy in x_sends + late:
-        copy.wait()
-    for copies in c_sends:
-        for copy in copies:
+        part = self.hin_o.at[self.hi]
+        self.h_far = []
+        for k, to in enumerate(self.z_to):
+            self.h_far.append(send(part, part, self.hs.at[1, k], self.hr.at[1, k], to))
+            self.h_far.append(
+                send(self.hdn, self.hdn_o.at[self.hi], self.hs.at[2, k], self.hr.at[2, k], to)
+            )
+
+    def heavy_ready(self):
+        for copy in self.h_far:
             copy.wait()
 
 
-def gather_all(dp, xin, weights, hin, hdn):
-    nz = dp // 2
-    nw = len(weights)
-    seqs, rows, _ = xin.shape
-    shapes = [jax.ShapeDtypeStruct((seqs // dp, dp, rows, D), BF)]
-    shapes += [jax.ShapeDtypeStruct((nz, 2, 2, 2) + w.shape, BF) for w in weights]
-    shapes.append(jax.ShapeDtypeStruct((nz,) + hin.shape, BF))
-    shapes.append(jax.ShapeDtypeStruct((nz,) + hdn.shape, BF))
-    most = max(7, nz)
-    scratch = [
+def gather_sems(dp, nw):
+    nz, most = dp // 2, max(7, dp // 2)
+    return [
         DMA((nw + 3,)),
         DMA((dp,)),
         DMA((dp,)),
         DMA((nw, nz)),
         DMA((nw, nz)),
-        DMA((nw, 3)),
-        DMA((nw, 3)),
+        DMA((nw, 4)),
+        DMA((nw, 4)),
         DMA((nw, 4)),
         DMA((nw, 4)),
         DMA((3, most)),
         DMA((3, most)),
     ]
+
+
+def gather_kernel(dp, nw, *refs):
+    ins, outs, sems = refs[: 3 + nw], refs[3 + nw : 6 + 2 * nw], refs[6 + 2 * nw :]
+    g = Gather(
+        dp, ins[0], ins[1:-2], ins[-2], ins[-1], outs[0], outs[1:-2], outs[-2], outs[-1], sems
+    )
+    g.meet()
+    g.rows()
+    for w in range(nw):
+        g.line(w)
+    g.heavy_plane()
+    for w in range(nw):
+        g.plane(w)
+        if w == 1:
+            g.heavy_line()
+        if w >= 1:
+            g.cross(w - 1)
+        if w >= 2:
+            g.core(w - 2)
+    g.cross(nw - 1)
+    for w in range(nw - 2, nw):
+        g.core(w)
+    g.rows_ready()
+    for w in range(nw):
+        g.ready(w)
+    g.heavy_ready()
+
+
+def gather_shapes(dp, xin, weights, hin, hdn, paired):
+    nz = dp // 2
+    seqs, rows, _ = xin.shape
+    shapes = [jax.ShapeDtypeStruct((seqs // dp, dp, rows, D), BF)]
+    if paired:
+        shapes += [jax.ShapeDtypeStruct((nz, 2, 2, 2 * w.shape[0], w.shape[1]), BF) for w in weights]
+    else:
+        shapes += [jax.ShapeDtypeStruct((nz, 2, 2, 2) + w.shape, BF) for w in weights]
+    shapes.append(jax.ShapeDtypeStruct((nz,) + hin.shape, BF))
+    shapes.append(jax.ShapeDtypeStruct((nz,) + hdn.shape, BF))
+    return shapes
+
+
+def gather_all(dp, xin, weights, hin, hdn):
+    nw = len(weights)
     return call(
         functools.partial(gather_kernel, dp, nw),
-        shapes,
+        gather_shapes(dp, xin, weights, hin, hdn, False),
         [xin, *weights, hin, hdn],
         [ANY] * (3 + nw),
         [ANY] * (3 + nw),
-        scratch,
+        gather_sems(dp, nw),
         1,
     )
 
@@ -450,7 +534,7 @@
     def norm(r):
         h = hidden[r, :]
         inv = lax.rsqrt(jnp.mean(h * h, axis=-1, keepdims=True) + EPSILON)
-        hn[r, :] = (h * inv * gain[...]).astype(BF)
+        hn[r, :] = (h * inv * gain[1:2, :]).astype(BF)
 
     tiles(tokens, 128, norm)
     for s in range(group):
@@ -580,8 +664,8 @@
         d = dhn[r, :]
         dh = d * h
         stats[0:1, :] += jnp.sum(dh * inv, axis=0, keepdims=True)
-        mean = jnp.mean(gain[...] * dh, axis=-1, keepdims=True)
-        d_hidden[r, :] = out[r, :] + inv * gain[...] * d - h * (inv * inv * inv * mean)
+        mean = jnp.mean(gain[1:2, :] * dh, axis=-1, keepdims=True)
+        d_hidden[r, :] = out[r, :] + inv * gain[1:2, :] * d - h * (inv * inv * inv * mean)
 
     tiles(tokens, 128, norm_back)
 
@@ -693,7 +777,8 @@
     return jnp.concatenate([lse[:, 2 * pair : 2 * pair + 1], lse[:, 2 * pair + 1 : 2 * pair + 2]], axis=0)
 
 
-def attend_kernel(
+def attend_body(
+    stages,
     x,
     gain,
     select,
@@ -724,7 +809,6 @@
 ):
     hi, lo, x_, c = place()
     f = x_ * 2 + c
-    meet(line_peers())
     tokens = x.shape[0]
     group, cap, width = select.shape
     wl, wh = HL * DH, HH * DH
@@ -734,18 +818,20 @@
     def norm(r):
         h = x[r, :].astype(F32)
         inv = lax.rsqrt(jnp.mean(h * h, axis=-1, keepdims=True) + EPSILON)
-        xn[r, :] = (h * inv * gain[...]).astype(BF)
+        xn[r, :] = (h * inv * gain[0:1, :]).astype(BF)
 
     tiles(tokens, 128, norm)
     for s in range(group):
         rows = dot(select[s], xn[s * width : (s + 1) * width, :]).astype(BF)
         a_rows[s * cap : (s + 1) * cap, :] = rows
+    stages[0]()
     kv = dot(a_rows[...], w_hqkv[:, wh:]).astype(BF)
     for s in range(group):
         kvh[s, f] = kv[s * cap : (s + 1) * cap]
     mine = kvh.at[:, f]
     first = send(mine, mine, ss.at[0], sr.at[0], across)
     beside = send(mine, mine, ss.at[1], sr.at[1], partner)
+    stages[1]()
     for s in range(group):
         rows = xn[s * width : (s + 1) * width, :]
         rim[s, WIN : WIN + width, :] = dot(rows, w_lqkv[:, wl:]).astype(BF)
@@ -763,6 +849,7 @@
     for s in range(group):
         rows = slice(s * width, (s + 1) * width)
         lq[rows, :] = dot(xn[rows, :], w_lqkv[:, :wl]).astype(BF)
+    stages[2]()
     first.wait()
     other = kvh.at[:, (1 - x_) * 2 + c]
     relay = send(other, other, ss.at[2], sr.at[2], partner)
@@ -786,7 +873,10 @@
         l_lse[r, :] = lse
         return carry
 
-    lax.fori_loop(0, group * blocks, light, 0)
+    lax.fori_loop(0, group * blocks // 2, light, 0)
+    stages[3]()
+    lax.fori_loop(group * blocks // 2, group * blocks, light, 0)
+    stages[4]()
     beside.wait()
     relay.wait()
     heavy_kv = kvh.reshape(group, 4 * cap, 2 * wh)
@@ -808,6 +898,7 @@
         return carry
 
     lax.fori_loop(0, group, heavy, 0)
+    stages[5]()
     high, low = halves(dot(ho[...], w_hout[...]))
     for s in range(group):
         r = slice(s * width, (s + 1) * width)
@@ -819,13 +910,16 @@
         )
 
 
-def attend(x, gain, select, select_t, key_bias, heavy_bias, w_lqkv, w_hqkv, w_lout, w_hout):
-    tokens = x.shape[0]
+def attend_kernel(*refs):
+    meet(line_peers())
+    attend_body([lambda: None] * 6, *refs)
+
+
+def attend_shapes(tokens, select):
     group, cap, width = select.shape
     wl, wh = HL * DH, HH * DH
     rows = group * cap
-    operands = [x, gain, select, select_t, key_bias, heavy_bias, w_lqkv, w_hqkv, w_lout, w_hout]
-    shapes = [
+    return [
         jax.ShapeDtypeStruct((tokens, D), F32),
         jax.ShapeDtypeStruct((tokens, D), BF),
         jax.ShapeDtypeStruct((tokens, wl), BF),
@@ -838,14 +932,116 @@
         jax.ShapeDtypeStruct((rows, wh), BF),
         jax.ShapeDtypeStruct((rows, 128), F32),
     ]
+
+
+ATTEND_SEMS = [DMA, DMA, DMA, DMA, DMA((3,)), DMA((3,))]
+
+
+def attend(x, gain, select, select_t, key_bias, heavy_bias, w_lqkv, w_hqkv, w_lout, w_hout):
+    operands = [x, gain, select, select_t, key_bias, heavy_bias, w_lqkv, w_hqkv, w_lout, w_hout]
+    shapes = attend_shapes(x.shape[0], select)
     return call(
         attend_kernel,
         shapes,
         operands,
         [VM] * len(operands),
         [VM] * len(shapes),
-        [DMA, DMA, DMA, DMA, DMA((3,)), DMA((3,))],
+        ATTEND_SEMS,
         2,
+    )
+
+
+def gather_attend_kernel(dp, nw, *refs):
+    n_in, n_out = 7 + nw, 3 + nw + 12
+    ins, outs, rest = refs[:n_in], refs[n_in : n_in + n_out], refs[n_in + n_out :]
+    xin, ws, hin, hdn = ins[0], ins[1 : 1 + nw], ins[1 + nw], ins[2 + nw]
+    masks = ins[3 + nw :]
+    xo, wos, hin_o, hdn_o = outs[0], outs[1 : 1 + nw], outs[1 + nw], outs[2 + nw]
+    gain, saved = outs[3 + nw], outs[4 + nw :]
+    g = Gather(dp, xin, ws, hin, hdn, xo, wos, hin_o, hdn_o, rest[:11])
+    g.meet()
+    g.rows()
+    for w in (0, 1, 2):
+        g.line(w)
+    g.heavy_plane()
+    for w in (0, 1, 2):
+        g.plane(w)
+    for w in (3, 4, 5, 6):
+        g.line(w)
+    g.heavy_line()
+    g.cross(0)
+    g.core(0)
+    g.cross(1)
+    g.cross(2)
+    g.ready(0)
+    total = jnp.zeros(gain.shape, F32)
+    for z in range(dp // 2):
+        for l2, x2 in ((0, 0), (0, 1), (1, 0), (1, 1)):
+            pair = wos[0][z, l2, x2].astype(F32)
+            total += pair[:8] + pair[8:]
+    gain[...] = total
+    g.rows_ready()
+
+    def heavy_projection():
+        g.core(1)
+        g.core(2)
+        g.ready(2)
+
+    def keys_travel():
+        g.plane(3)
+        g.plane(4)
+
+    def half_way():
+        g.cross(3)
+        g.cross(4)
+        g.plane(5)
+
+    def light_done():
+        g.core(3)
+        g.core(4)
+        g.cross(5)
+        g.plane(6)
+
+    def heavy_done():
+        g.ready(3)
+        g.ready(4)
+        g.core(5)
+        g.cross(6)
+
+    full = [wos[w].reshape(-1, wos[w].shape[-1]) for w in range(nw)]
+    stages = [heavy_projection, lambda: g.ready(1), keys_travel, half_way, light_done, heavy_done]
+    attend_body(
+        stages,
+        xo.reshape(-1, D),
+        gain,
+        *masks,
+        full[1],
+        full[2],
+        full[3],
+        full[4],
+        *saved,
+        *rest[11:],
+    )
+    g.core(6)
+    g.ready(5)
+    g.ready(6)
+    g.heavy_ready()
+
+
+def gather_attend(dp, xin, weights, hin, hdn, masks):
+    nw = len(weights)
+    shapes = gather_shapes(dp, xin, weights, hin, hdn, True)
+    tokens = shapes[0].shape[0] * dp * xin.shape[1]
+    shapes.append(jax.ShapeDtypeStruct((8, D), F32))
+    shapes += attend_shapes(tokens, masks[0])
+    return call(
+        functools.partial(gather_attend_kernel, dp, nw),
+        shapes,
+        [xin, *weights, hin, hdn, *masks],
+        [ANY] * (3 + nw) + [VM] * 4,
+        [VM] * 6 + [ANY] * 4 + [VM] * 12,
+        gather_sems(dp, nw) + ATTEND_SEMS,
+        1,
     )
 
 
@@ -1020,9 +1216,9 @@
         d = d_xn[r, :]
         dh = d * h
         stats[0:1, :] += jnp.sum(dh * inv, axis=0, keepdims=True)
-        mean = jnp.mean(gain[...] * dh, axis=-1, keepdims=True)
+        mean = jnp.mean(gain[0:1, :] * dh, axis=-1, keepdims=True)
         dx[r, :] = (
-            d_hidden[r, :] + inv * gain[...] * d - h * (inv * inv * inv * mean)
+            d_hidden[r, :] + inv * gain[0:1, :] * d - h * (inv * inv * inv * mean)
         ).astype(BF)
 
     tiles(tokens, 128, norm_back)
@@ -1305,9 +1501,12 @@
     gain_len = gain_attn.shape[0]
     hidden_units = heavy_in.shape[1] // 2 // n
     xin = deal_rows(dealing, layer_input[:, 0])
-    gains = jnp.pad(
-        jnp.stack([gain_attn, gain_ffn]), ((0, 6), (0, 128 - gain_len))
-    )
+    mine = data_index * pieces + piece
+    owned = jnp.arange(D)[None, :] // gain_len == mine
+    spread_out = jnp.broadcast_to(
+        jnp.stack([gain_attn, gain_ffn])[:, None, :], (2, D // gain_len, gain_len)
+    ).reshape(2, D)
+    gains = jnp.pad(jnp.where(owned, spread_out, 0.0).astype(BF), ((0, 6), (0, 0)))
     matrices = (light_qkv, heavy_qkv, light_out, heavy_out, light_in, light_down)
     hin_rows = heavy_in.shape[0]
     hin_src = (
@@ -1317,16 +1516,7 @@
     )
     if hin_rows % 8:
         hin_src = hin_src.reshape(8, -1, 128)
-    got = gather_all(dp, xin, [gains] + [packed(m) for m in matrices], hin_src, heavy_down)
     tokens = layer_input.shape[2] * dp
-    gain_rows = got[1].reshape(n, 8, 128)
-    gain_one = gain_rows[:, 0, :gain_len].reshape(-1).astype(F32)
-    gain_two = gain_rows[:, 1, :gain_len].reshape(-1).astype(F32)
-    w_lqkv, w_hqkv, w_lout, w_hout, w_lin, w_ldown = (
-        unpacked(full, *m.shape) for full, m in zip(got[2:8], matrices)
-    )
-    w_hin = unpacked(got[8], hin_rows, 2 * nz * hidden_units)
-    w_hdown = got[9].reshape(-1, D)
     chosen = lax.dynamic_slice_in_dim(dealing, data_index * group, group)
     one = (chosen[:, None] == jnp.arange(seqs)[None, :])
     seq_lengths = jnp.sum(jnp.where(one, lengths[None, :], 0), axis=1)
@@ -1356,17 +1546,32 @@
         a_spot[:, :, None] == all_spots[:, None, :]
     )
     heavy_bias = jnp.where(heavy_allowed, 0.0, MASKED)
+    masks = (a_select, a_select.swapaxes(1, 2), key_bias, heavy_bias)
+    sources = (xin, [gains] + [packed(m) for m in matrices], hin_src, heavy_down)
+    merged = all(m.shape[0] % 8 == 0 for m in (*matrices, heavy_in, heavy_down, layer_input[0, 0]))
+    if merged:
+        got = gather_attend(dp, *sources, masks)
+    else:
+        got = gather_all(dp, *sources)
     flat_x = got[0].reshape(-1, D)
-    masks = (a_select, a_select.swapaxes(1, 2), key_bias, heavy_bias)
+    w_lqkv, w_hqkv, w_lout, w_hout, w_lin, w_ldown = (
+        unpacked(full, *m.shape) for full, m in zip(got[2:8], matrices)
+    )
+    w_hin = unpacked(got[8], hin_rows, 2 * nz * hidden_units)
+    w_hdown = got[9].reshape(-1, D)
     attn_weights = (w_lqkv, w_hqkv, w_lout, w_hout)
-    hidden, *saved = attend(flat_x, gain_one.reshape(1, D), *masks, *attn_weights)
+    if merged:
+        gain, hidden, *saved = got[10:]
+    else:
+        gain = jnp.sum(got[1].reshape(n, 8, D).astype(F32), axis=0)
+        hidden, *saved = attend(flat_x, gain, *masks, *attn_weights)
     weight_mask = valid_mask.reshape(-1, 1).astype(F32)
     grad_lin, grad_ldown, grad_hin, grad_hdown, d_hidden, ffn_stats = feed_forward(
         hidden,
         f_select,
         f_select.swapaxes(1, 2),
         slot_score.reshape(-1, 1),
-        gain_two.reshape(1, D),
+        gain,
         teacher.reshape(-1, D),
         weight_mask,
         2.0 * weight_mask / (D * token_count),
@@ -1376,7 +1581,7 @@
         w_hdown,
     )
     grad_lqkv, grad_hqkv, grad_lout, grad_hout, d_inputs, attn_stats = attend_back(
-        d_hidden, flat_x, gain_one.reshape(1, D), *masks, attn_weights, saved
+        d_hidden, flat_x, gain, *masks, attn_weights, saved
     )
     rows = tokens // dp
     stats = jnp.concatenate(
@@ -1402,7 +1607,6 @@
     )
     d_layer = undeal_rows(dealing, done[0].reshape(seqs, rows, D))[:, None]
     summed = done[1]
-    mine = data_index * pieces + piece
     loss_value = summed[12, 0] / (D * token_count)
     own_one = lax.dynamic_slice_in_dim(summed[:6].reshape(-1), mine * gain_len, gain_len)
     own_two = lax.dynamic_slice_in_dim(summed[6:12].reshape(-1), mine * gain_len, gain_len)

time: 449 us -> 386 us (0.86)
  Pallas kernels: 407 us -> 349 us
    pallas_call x5 -> x4, Pallas kernels: 403 us -> 344 us  [call(): pl.pallas_call(kernel, out_shape=out_shape, in_specs=in_specs, out_specs=...]
where the time goes in v4:
time: 386 us; the launch traced here: 385 us
  Pallas kernels  349 us (90%)
  local copies, waits for them, and re-layouts  19.8 us (5%)
  other arithmetic  12.8 us (3%)
    pallas_call x4, Pallas kernels, call(): pl.pallas_call(kernel, out_shape=out_shape, in_specs=in_specs, out_specs=...  344 us
    unnamed x29, local copies, waits for them, and re-layouts  8.83 us

profile of v4, /device:TPU:0, one launch (start us, length us, event | category | flops | bytes accessed | tf_op | source)
XLA Modules:
  0.0 385.2 jit_solution(15506197057901348099)
XLA Ops:
  0.7 0.7 dynamic_slice.23
  1.4 1.3 reduce_sum.88
  3.3 0.8 select_reduce_fusion.6
  4.2 0.1 iota_compare_fusion.5
  4.2 0.7 pad_maximum_fusion.1
  5.0 0.8 select_reduce_fusion.3
  5.7 0.1 and_select_fusion
  5.8 0.8 select_reduce_fusion.4
  6.6 0.1 fusion.19
  6.7 0.6 reshape.286.refs_12_.key_bias
  7.4 0.4 fusion
  7.7 0.4 fusion.2
  8.1 0.2 fusion.5
  8.2 0.2 fusion.7
  8.4 1.6 select_reduce_fusion
  10.0 0.1 reshape.283
  10.1 0.6 pad.4.refs_1_
  10.7 0.9 copy.77
  11.6 1.1 copy.73
  12.6 0.2 copy.82
  12.8 1.0 reshape.285.refs_8_
  13.8 1.4 fusion.22
  15.3 0.2 select_reduce_fusion.2
  15.5 0.1 select_n.90
  15.5 0.7 fusion.11
  16.2 0.7 fusion.9
  16.9 0.7 copy.61.refs_10_.select
  17.7 0.1 fusion.17
  17.7 0.8 reshape.318.score
  18.5 0.7 copy.64.select
  19.2 0.7 or_select_fusion.refs_13_.heavy_bias
  20.0 0.9 copy.75
  20.8 2.2 shard_map.256.refs_0_
  23.0 124.6 %shard_map.257 = (bf16[2,8,32,768]{3,2,1,0:T(8,128)(2,1)}, bf16[4,2,2,16,768]{4,3,2,1,0:T(8,128)(2,1)}, bf16[4,2,2,48,1536]{4,3,2,1,0:T(8,128)(2,1)}, bf16[4,2,2...) custom-call(bf16[16,32,768]{2,1,0:T(8,128)(2,1)} %shard_map.256.refs, ...), custom_call_target="tpu_custom_call" | custom-call | tf_op jit(solution)/shard_map/pallas_call | solution.py:72
  147.6 67.7 %shard_map.258 = (bf16[768,2048]{1,0:T(8,128)(2,1)}, bf16[1024,768]{1,0:T(8,128)(2,1)}, bf16[768,1024]{1,0:T(8,128)(2,1)}, bf16[512,768]{1,0:T(8,128)(2,1)}, f32[512,768]{1,0:T(8,128)}, /*index=5*/f32[8,768]{1,0:T(8,128)}) custom-call(f32[512,768]{1,0:T(8,128)} %get-tuple-element.55.hidden, bf16[2,64,256]{2,1,0:T(8,128)(2,1)} %copy.64.select, ...), custom_call_target="tpu_custom_call" | custom-call | tf_op jit(solution)/shard_map/pallas_call | solution.py:72
  215.3 35.7 %shard_map.259 = (bf16[768,1536]{1,0:T(8,128)(2,1)}, bf16[768,2304]{1,0:T(8,128)(2,1)}, bf16[512,768]{1,0:T(8,128)(2,1)}, bf16[768,768]{1,0:T(8,128)(2,1)}, bf16[512,768]{1,0:T(8,128)(2,1)}, /*index=5*/f32[8,768]{1,0:T(8,128)}) custom-call(f32[512,768]{1,0:T(8,128)} %get-tuple-element.61.d_hidden, bf16[512,768]{1,0:T(8,128)(2,1)} %bitcast.106, ...), custom_call_target="tpu_custom_call" | custom-call | tf_op jit(solution)/shard_map/pallas_call | solution.py:72
  251.0 0.8 slice_reduce_fusion.2
  251.8 1.4 slice_reduce_fusion
  253.2 0.6 broadcast_in_dim.187
  253.8 0.1 pad.7.clone
  253.9 0.7 maximum_maximum_fusion.refs_1_
  254.6 116.2 %shard_map.260 = (bf16[8,2,32,768]{3,2,1,0:T(8,128)(2,1)}, f32[16,128]{1,0:T(8,128)}, f32[24,2048]{1,0:T(8,128)}, f32[32,768]{1,0:T(8,128)}, f32[24,768]{1,0:T(8...) custom-call(bf16[2,8,32,768]{3,2,1,0:T(8,128)(2,1)} %bitcast.100, ...), custom_call_target="tpu_custom_call" | custom-call | tf_op jit(solution)/shard_map/pallas_call | solution.py:72
  370.8 0.0 copy-start.1
  370.8 1.2 slice.29
  372.7 0.8 slice_bitcast_fusion
  373.5 0.6 dynamic_slice.29
  374.1 0.6 dynamic_slice.28
  374.7 2.5 shard_map.261
  377.1 0.0 copy-done.1
  377.1 0.3 reshape.316
  377.5 0.0 copy-start.4
  377.5 0.5 copy.69
  378.0 1.3 copy.81
  379.4 0.0 copy-done.4
  379.4 0.7 copy.90
  380.0 0.6 copy.91
  380.7 0.7 copy.92
  381.3 0.6 copy.93
  382.0 0.0 copy-done.3
  382.0 0.7 copy.94
  382.7 0.0 copy-done.5
  382.7 0.6 copy.95
  383.3 0.0 copy-done
  383.3 0.7 copy.96
  (26 shorter events, 0.1 us)
Async XLA Ops:
  370.8 6.3 %copy-start.1 = (bf16[8,24,1024]{2,1,0:T(8,128)(2,1)S(1)}, bf16[8,24,1024]{2,1,0:T(8,128)(2,1)}, u32[]{:S(2)}) copy-start(bf16[8,24,1024]{2,1,0:T(8,128)(2,1)} %get-tuple-element.96) | copy-start | bytes 1179652
  377.5 1.9 copy-start.4
  377.5 2.5 copy-start.7
  377.5 3.1 copy-start.2
  378.0 3.4 copy-start.6
  378.0 4.0 %copy-start.3 = (f32[24,2048]{1,0:T(8,128)S(1)}, f32[24,2048]{1,0:T(8,128)}, u32[]{:S(2)}) copy-start(f32[24,2048]{1,0:T(8,128)} %get-tuple-element.176) | copy-start | bytes 589828
  378.0 4.7 %copy-start.5 = (f32[32,768]{1,0:T(8,128)S(1)}, f32[32,768]{1,0:T(8,128)}, u32[]{:S(2)}) copy-start(f32[32,768]{1,0:T(8,128)} %get-tuple-element.177) | copy-start | bytes 294916
  378.0 5.3 %copy-start = (f32[128,768]{1,0:T(8,128)S(1)}, f32[128,768]{1,0:T(8,128)}, u32[]{:S(2)}) copy-start(f32[128,768]{1,0:T(8,128)} %get-tuple-element.179) | copy-start | bytes 1179652

commit v5 on v4

--- a/solution.py
+++ b/solution.py
@@ -142,7 +142,7 @@
 
 
 class Gather:
-    def __init__(self, dp, xin, ws, hin, hdn, xo, wos, hin_o, hdn_o, sems):
+    def __init__(self, dp, xin, ws, hin, hdn, xo, wos, hin_o, hdn_o, sems, halves=None):
         self.dp, self.nz = dp, dp // 2
         self.xin, self.ws, self.hin, self.hdn = xin, ws, hin, hdn
         self.xo, self.wos, self.hin_o, self.hdn_o = xo, wos, hin_o, hdn_o
@@ -158,11 +158,33 @@
         nw = len(ws)
         self.kept, self.z, self.p, self.f, self.k = ([None] * nw for _ in range(5))
 
+        self.halves = halves
+
+    def lanes(self, w, c):
+        half = self.ws[w].shape[1] // 2
+        return pl.ds(pl.multiple_of(c * half, 128), half)
+
     def shard(self, w, z, lo, x):
-        full, rows = self.wos[w], self.ws[w].shape[0]
-        if len(full.shape) == 6:
-            return full.at[z, lo, x, self.c]
-        return full.at[z, lo, x, pl.ds(pl.multiple_of(self.c * rows, 8), rows)]
+        if self.halves is None:
+            return self.wos[w].at[z, lo, x, self.c]
+        return self.wos[w].at[z, lo, x, :, self.lanes(w, self.c)]
+
+    def swap(self, w):
+        mine, mate, _, sems = self.halves
+        partner = at(self.hi, self.lo, self.x, 1 - self.c)
+        self.kept[w] = keep(self.ws[w].at[:, self.lanes(w, self.c)], mine[w], sems[0].at[w])
+        out = self.ws[w].at[:, self.lanes(w, 1 - self.c)]
+        self.z[w] = send(out, mate[w], sems[1].at[w], sems[2].at[w], partner)
+
+    def join(self, w):
+        mine, mate, base, _ = self.halves
+        self.kept[w].wait()
+        self.z[w].wait()
+        a, b = mine[w][...].astype(F32), mate[w][...].astype(F32)
+        first = self.c == 0
+        rows = [jnp.where(first, a, b), jnp.where(first, b, a)]
+        base[w][...] = jnp.concatenate(rows, axis=0).astype(BF)
+        self.line(w)
 
     def meet(self):
         peers = self.rows_to + [at(self.hi, *q[:3]) for q in self.others if q[3]]
@@ -185,9 +207,10 @@
 
     def line(self, w):
         spot = self.shard(w, self.hi, self.lo, self.x)
-        self.kept[w] = keep(self.ws[w], spot, self.loc.at[w])
+        own = self.ws[w] if self.halves is None else self.halves[2][w]
+        self.kept[w] = keep(own, spot, self.loc.at[w])
         self.z[w] = [
-            send(self.ws[w], spot, self.zs.at[w, k], self.zr.at[w, k], to)
+            send(own, spot, self.zs.at[w, k], self.zr.at[w, k], to)
             for k, to in enumerate(self.z_to)
         ]
 
@@ -958,16 +981,20 @@
     masks = ins[3 + nw :]
     xo, wos, hin_o, hdn_o = outs[0], outs[1 : 1 + nw], outs[1 + nw], outs[2 + nw]
     gain, saved = outs[3 + nw], outs[4 + nw :]
-    g = Gather(dp, xin, ws, hin, hdn, xo, wos, hin_o, hdn_o, rest[:11])
+    parts, rest = rest[: 3 * nw + 3], rest[3 * nw + 3 :]
+    halves = (parts[:nw], parts[nw : 2 * nw], parts[2 * nw : 3 * nw], parts[3 * nw :])
+    g = Gather(dp, xin, ws, hin, hdn, xo, wos, hin_o, hdn_o, rest[:11], halves)
     g.meet()
+    for w in range(nw):
+        g.swap(w)
     g.rows()
     for w in (0, 1, 2):
-        g.line(w)
+        g.join(w)
     g.heavy_plane()
     for w in (0, 1, 2):
         g.plane(w)
     for w in (3, 4, 5, 6):
-        g.line(w)
+        g.join(w)
     g.heavy_line()
     g.cross(0)
     g.core(0)
@@ -1040,12 +1067,17 @@
         [xin, *weights, hin, hdn, *masks],
         [ANY] * (3 + nw) + [VM] * 4,
         [VM] * 6 + [ANY] * 4 + [VM] * 12,
-        gather_sems(dp, nw) + ATTEND_SEMS,
+        [pltpu.VMEM((w.shape[0], w.shape[1] // 2), BF) for w in weights] * 2
+        + [pltpu.VMEM((2 * w.shape[0], w.shape[1] // 2), BF) for w in weights]
+        + [DMA((nw,))] * 3
+        + gather_sems(dp, nw)
+        + ATTEND_SEMS,
         1,
     )
 
 
-def attend_back_kernel(
+def attend_back_body(
+    stages,
     d_hidden,
     x,
     gain,
@@ -1084,7 +1116,6 @@
     edge,
     edge_in,
     d_lproj,
-    d_xn,
     ls,
     lr,
     rs,
@@ -1093,7 +1124,6 @@
     sr,
 ):
     hi, lo, x_, c = place()
-    meet(line_peers())
     tokens = x.shape[0]
     group, cap, width = select.shape
     wl, wh = HL * DH, HH * DH
@@ -1136,6 +1166,7 @@
         send(part.at[:, b * 2 + 1 - c], got.at[b], ss.at[b], sr.at[b], partner) for b in (0, 1)
     ]
     g_hout[...] = dot_grad(ho[...], d_ha).astype(BF)
+    stages[0]()
 
     def light_out_back(r):
         d = d_hidden[r, :].astype(BF)
@@ -1143,11 +1174,14 @@
         d_lo[r, :] = dot_back(d, w_lout[...]).astype(BF)
 
     tiles(tokens, 256, light_out_back)
+    g_lout[...] = dot_grad(lo_out[...], d_la[...]).astype(BF)
+    stages[1]()
     for copy in beside:
         copy.wait()
     for b in (0, 1):
         got[b] = (got[b].astype(F32) + part[:, b * 2 + c].astype(F32)).astype(BF)
     third = send(got.at[1 - x_], far, ss.at[2], sr.at[2], across)
+    stages[2]()
     d_rim[...] = jnp.zeros(d_rim.shape, F32)
     blocks = width // WIN
 
@@ -1175,13 +1209,15 @@
             d_rim[s, keys, at_v] += dv
         return carry
 
-    lax.fori_loop(0, group * blocks, light, 0)
+    lax.fori_loop(0, group * blocks // 2, light, 0)
+    stages[3]()
+    lax.fori_loop(group * blocks // 2, group * blocks, light, 0)
     edge[0] = d_rim[:, :WIN, :].astype(BF)
     edge[1] = d_rim[:, WIN + width :, :].astype(BF)
     finish = rim_exchange(
         edge.at[0], edge.at[1], edge_in.at[0], edge_in.at[1], ls, lr, rs, rr
     )
-    g_lout[...] = dot_grad(lo_out[...], d_la[...]).astype(BF)
+    stages[4]()
     third.wait()
     total = (got[x_].astype(F32) + far[...].astype(F32)).astype(BF)
     for s in range(group):
@@ -1191,6 +1227,7 @@
         g_hqkv[:, j] = dot_grad(a_rows[...], d_hproj[:, j]).astype(BF)
 
     tiles(3 * wh, 768, heavy_grad)
+    stages[5]()
     d_high, d_low = halves(dot_back(d_hproj[...], w_hqkv[...]))
     finish()
     for s in range(group):
@@ -1202,33 +1239,52 @@
         g_lqkv[:, j] = dot_grad(xn[...], d_lproj[:, j]).astype(BF)
 
     tiles(3 * wl, 768, light_grad)
+    stages[6]()
+    stats[...] = jnp.zeros(stats.shape, F32)
     for s in range(group):
         r = slice(s * width, (s + 1) * width)
         q = slice(s * cap, (s + 1) * cap)
-        d_xn[r, :] = dot_back(d_lproj[r, :], w_lqkv[...]) + (
+        d = dot_back(d_lproj[r, :], w_lqkv[...]) + (
             dot(select_t[s], d_high[q]) + dot(select_t[s], d_low[q])
         )
-    stats[...] = jnp.zeros(stats.shape, F32)
-
-    def norm_back(r):
         h = x[r, :].astype(F32)
         inv = lax.rsqrt(jnp.mean(h * h, axis=-1, keepdims=True) + EPSILON)
-        d = d_xn[r, :]
         dh = d * h
         stats[0:1, :] += jnp.sum(dh * inv, axis=0, keepdims=True)
         mean = jnp.mean(gain[0:1, :] * dh, axis=-1, keepdims=True)
         dx[r, :] = (
             d_hidden[r, :] + inv * gain[0:1, :] * d - h * (inv * inv * inv * mean)
         ).astype(BF)
-
-    tiles(tokens, 128, norm_back)
-
-
-def attend_back(d_hidden, x, gain, select, select_t, key_bias, heavy_bias, weights, saved):
-    tokens = x.shape[0]
+    stages[7]()
+
+
+def attend_back_kernel(*refs):
+    meet(line_peers())
+    attend_back_body([lambda: None] * 8, *refs)
+
+
+def attend_back_scratch(tokens, select):
     group, cap, width = select.shape
     wl, wh = HL * DH, HH * DH
     rows = group * cap
+    return [
+        pltpu.VMEM((rows, wh), BF),
+        pltpu.VMEM((rows, 3 * wh), BF),
+        pltpu.VMEM((group, 4, cap, 2 * wh), BF),
+        pltpu.VMEM((2, group, cap, 2 * wh), BF),
+        pltpu.VMEM((group, cap, 2 * wh), BF),
+        pltpu.VMEM((tokens, D), BF),
+        pltpu.VMEM((tokens, wl), BF),
+        pltpu.VMEM((group, width + 2 * WIN, 2 * wl), F32),
+        pltpu.VMEM((2, group, WIN, 2 * wl), BF),
+        pltpu.VMEM((2, group, WIN, 2 * wl), BF),
+        pltpu.VMEM((tokens, 3 * wl), BF),
+    ] + ATTEND_SEMS
+
+
+def attend_back(d_hidden, x, gain, select, select_t, key_bias, heavy_bias, weights, saved):
+    tokens = x.shape[0]
+    wl, wh = HL * DH, HH * DH
     operands = [d_hidden, x, gain, select, select_t, key_bias, heavy_bias, *weights, *saved]
     shapes = [
         jax.ShapeDtypeStruct((D, 3 * wl), BF),
@@ -1244,26 +1300,7 @@
         operands,
         [VM] * len(operands),
         [VM] * len(shapes),
-        [
-            pltpu.VMEM((rows, wh), BF),
-            pltpu.VMEM((rows, 3 * wh), BF),
-            pltpu.VMEM((group, 4, cap, 2 * wh), BF),
-            pltpu.VMEM((2, group, cap, 2 * wh), BF),
-            pltpu.VMEM((group, cap, 2 * wh), BF),
-            pltpu.VMEM((tokens, D), BF),
-            pltpu.VMEM((tokens, wl), BF),
-            pltpu.VMEM((group, width + 2 * WIN, 2 * wl), F32),
-            pltpu.VMEM((2, group, WIN, 2 * wl), BF),
-            pltpu.VMEM((2, group, WIN, 2 * wl), BF),
-            pltpu.VMEM((tokens, 3 * wl), BF),
-            pltpu.VMEM((tokens, D), F32),
-            DMA,
-            DMA,
-            DMA,
-            DMA,
-            DMA((3,)),
-            DMA((3,)),
-        ],
+        attend_back_scratch(tokens, select),
         3,
     )
 
@@ -1456,6 +1493,328 @@
     )
 
 
+class Scatter:
+    def __init__(self, nz, shards, gs, near, one, two, end, sems):
+        self.nz, self.shards, self.gs = nz, shards, gs
+        self.near, self.one, self.two, self.end = near, one, two, end
+        self.cs, self.cr, self.ps, self.pr, self.zs, self.zr = sems
+        self.hi, self.lo, self.x, self.c = hi, lo, x, c = place()
+        self.partner = at(hi, lo, x, 1 - c)
+        self.by_x, self.by_y = at(hi, lo, 1 - x, c), at(hi, 1 - lo, x, c)
+        self.z_index = [lax.rem(hi + k, nz) for k in range(1, nz)]
+        self.copies = {}
+
+    def lanes(self, w, c):
+        half = self.shards[w][1] // 2
+        return pl.ds(pl.multiple_of(c * half, 128), half)
+
+    def core(self, w):
+        out = self.gs[w].at[:, :, :, :, self.lanes(w, 1 - self.c)]
+        self.copies[w, 0] = [send(out, self.near[w], self.cs.at[w], self.cr.at[w], self.partner)]
+
+    def wait(self, w, stage):
+        for copy in self.copies[w, stage]:
+            copy.wait()
+
+    def plane(self, w):
+        g, own = self.gs[w], self.lanes(w, self.c)
+        self.add_plane(w, lambda z, a, b: g[z, a, b, :, own])
+
+    def own_plane(self, w, kept):
+        self.add_plane(w, lambda z, a, b: kept[z, a, b])
+
+    def add_plane(self, w, own):
+        self.wait(w, 0)
+        near = self.near[w]
+        lo, x, half = self.lo, self.x, self.nz // 2
+
+        def body(i, carry):
+            z, a, b = i // 4, (i // 2) % 2, i % 2
+            near[z, a, b] = (near[z, a, b].astype(F32) + own(z, a, b).astype(F32)).astype(BF)
+            return carry
+
+        lax.fori_loop(0, self.nz * 4, body, 0)
+        low, high = pl.ds(0, half), pl.ds(half, self.nz - half)
+        self.copies[w, 1] = [
+            send(near.at[low, :, 1 - x], self.one[w].at[low], self.ps.at[w, 0], self.pr.at[w, 0], self.by_x),
+            send(near.at[high, 1 - lo], self.one[w].at[high], self.ps.at[w, 1], self.pr.at[w, 1], self.by_y),
+        ]
+
+    def cross(self, w):
+        self.wait(w, 1)
+        near, one, lo, x, half = self.near[w], self.one[w], self.lo, self.x, self.nz // 2
+
+        def low_body(i, carry):
+            z, a = i // 2, i % 2
+            near[z, a, x] = (near[z, a, x].astype(F32) + one[z, a].astype(F32)).astype(BF)
+            return carry
+
+        def high_body(i, carry):
+            z, b = half + i // 2, i % 2
+            near[z, lo, b] = (near[z, lo, b].astype(F32) + one[z, b].astype(F32)).astype(BF)
+            return carry
+
+        lax.fori_loop(0, half * 2, low_body, 0)
+        lax.fori_loop(0, (self.nz - half) * 2, high_body, 0)
+        low, high = pl.ds(0, half), pl.ds(half, self.nz - half)
+        two = self.two[w]
+        self.copies[w, 2] = [
+            send(near.at[low, 1 - lo, x], two.at[low], self.ps.at[w, 2], self.pr.at[w, 2], self.by_y),
+            send(near.at[high, lo, 1 - x], two.at[high], self.ps.at[w, 3], self.pr.at[w, 3], self.by_x),
+        ]
+
+    def line(self, w):
+        self.wait(w, 2)
+        near, part, lo, x = self.near[w], self.two[w], self.lo, self.x
+
+        def body(z, carry):
+            part[z] = (near[z, lo, x].astype(F32) + part[z].astype(F32)).astype(BF)
+            return carry
+
+        lax.fori_loop(0, self.nz, body, 0)
+        self.copies[w, 3] = [
+            send(
+                part.at[z],
+                self.end[w].at[k],
+                self.zs.at[w, k],
+                self.zr.at[w, k],
+                at(z, lo, x, self.c),
+            )
+            for k, z in enumerate(self.z_index)
+        ]
+
+    def last(self, w, fin, out, sems):
+        self.wait(w, 3)
+        value = self.two[w][self.hi].astype(F32)
+        for k in range(self.nz - 1):
+            value += self.end[w][k].astype(F32)
+        fin[...] = value
+        count = self.shards[w][0]
+        own = pl.ds(pl.multiple_of(self.c * count, 8), count)
+        mate = pl.ds(pl.multiple_of((1 - self.c) * count, 8), count)
+        spot = out.at[:, self.lanes(w, self.c)]
+        return [
+            keep(fin.at[own], spot, sems[0].at[w]),
+            send(fin.at[mate], spot, sems[1].at[w], sems[2].at[w], self.partner),
+        ]
+
+
+def back_scatter_kernel(dp, shards, *refs):
+    nz, nw = dp // 2, len(shards)
+    n_ops = 7 + 4 + 10
+    ops, (g_lin, g_ldn, hin, hdn, ffn_stats) = refs[:n_ops], refs[n_ops : n_ops + 5]
+    outs, rest = refs[n_ops + 5 : n_ops + 9 + nw], refs[n_ops + 9 + nw :]
+    dxo, total, gos, hin_o, hdn_o = outs[0], outs[1], outs[2 : 2 + nw], outs[2 + nw], outs[3 + nw]
+    full, rest = rest[:4], rest[4:]
+    own_lin, own_ldn, stats, rest = rest[0], rest[1], rest[2], rest[3:]
+    back, rest = rest[:17], rest[17:]
+    dx = back[5]
+    near, one, two, end, fin = (rest[k * nw : (k + 1) * nw] for k in range(5))
+    hin_own, hdn_own, hin_r, hdn_r, acc, sc, sp, sz, acc2 = rest[5 * nw : 5 * nw + 9]
+    own, xs, xr, cs, cr, ps, pr, zs, zr, hs, hr, ts, tr, *fsem = rest[5 * nw + 9 :]
+    hi, lo, x, c = place()
+    d = hi * 2 + lo
+    plane = (lo * 2 + x) * 2 + c
+    others = plane_others()
+    rows_to = [(lax.rem(d + k, dp), x * 2 + c) for k in range(1, dp)]
+    z_index = [lax.rem(hi + k, nz) for k in range(1, nz)]
+    z_to = [at(z, lo, x, c) for z in z_index]
+    quad = quad_peers()
+    g_views = [g_lin, g_ldn]
+    for k, w in enumerate((2, 3, 4, 5)):
+        rows, columns = shards[w]
+        g_views.append(full[k].reshape(nz, 2, 2, 2 * rows, columns))
+    t = Scatter(nz, shards, g_views, near, one, two, end, (cs, cr, ps, pr, zs, zr))
+    meet(rows_to + [at(hi, *q[:3]) for q in others if q[3]])
+    h_sends = []
+    for k, z in enumerate(z_index):
+        h_sends.append(send(hin.at[z], hin_r.at[k], hs.at[1, k], hr.at[1, k], z_to[k]))
+        h_sends.append(send(hdn.at[z], hdn_r.at[k], hs.at[2, k], hr.at[2, k], z_to[k]))
+    t.core(0)
+    t.core(1)
+    kept = [
+        keep(g_lin.at[:, :, :, :, t.lanes(0, c)], own_lin, own.at[0]),
+        keep(g_ldn.at[:, :, :, :, t.lanes(1, c)], own_ldn, own.at[1]),
+        keep(hin.at[hi], hin_own, own.at[2]),
+        keep(hdn.at[hi], hdn_own, own.at[3]),
+    ]
+    late = []
+
+    def first_plane():
+        kept[0].wait()
+        kept[1].wait()
+        t.own_plane(0, own_lin)
+        t.own_plane(1, own_ldn)
+        t.core(2)
+
+    def out_core():
+        t.core(3)
+
+    def before_light():
+        t.cross(0)
+        t.cross(1)
+
+    def half_way():
+        t.line(0)
+        t.line(1)
+        t.plane(2)
+        t.plane(3)
+
+    def rims_left():
+        t.cross(2)
+        t.cross(3)
+
+    def heavy_grad_done():
+        t.core(4)
+        t.line(2)
+        t.line(3)
+
+    def light_grad_done():
+        t.core(5)
+        t.plane(4)
+
+    def rows_done():
+        rows = dx.reshape(dxo.shape[1], dp, dxo.shape[2], D)
+        late.append(keep(rows.at[:, d], dxo.at[d], own.at[4]))
+        for k, to in enumerate(rows_to):
+            late.append(send(rows.at[:, to[0]], dxo.at[d], xs.at[k], xr.at[k], to))
+
+    stages = [
+        first_plane,
+        out_core,
+        before_light,
+        half_way,
+        rims_left,
+        heavy_grad_done,
+        light_grad_done,
+        rows_done,
+    ]
+    attend_back_body(
+        stages, *ops, full[3], full[2], full[1], full[0], dx, stats, *back
+    )
+    partner = at(hi, lo, x, 1 - c)
+    for k in range(6):
+        lanes = slice(k * 128, (k + 1) * 128)
+        acc[k : k + 1, :] = stats[0:1, lanes]
+        acc[6 + k : 7 + k, :] = ffn_stats[0:1, lanes]
+    loss = jnp.sum(ffn_stats[1:2, :], axis=-1, keepdims=True)
+    acc[12:16, :] = jnp.broadcast_to(loss, (4, 128))
+    t_c = send(acc, sc, ts.at[0], tr.at[0], partner)
+    t.plane(5)
+    t.cross(4)
+    t_c.wait()
+    acc2[...] = acc[...] + sc[...]
+    t_p = [
+        send(acc2, sp.at[k], ts.at[1 + k], tr.at[1 + k], at(hi, l2, x2, c))
+        for k, (l2, x2) in enumerate(quad)
+    ]
+    for copy in h_sends + kept[2:]:
+        copy.wait()
+
+    def body(i, carry):
+        value = hin_own[i].astype(F32)
+        for k in range(nz - 1):
+            value += hin_r[k, i].astype(F32)
+        hin_own[i] = value.astype(BF)
+        return carry
+
+    lax.fori_loop(0, 8, body, 0)
+    hin_o[plane] = hin_own[plane]
+    late += [
+        send(
+            hin_own.at[(q[0] * 2 + q[1]) * 2 + q[2]],
+            hin_o.at[plane],
+            hs.at[0, k],
+            hr.at[0, k],
+            at(hi, *q[:3]),
+        )
+        for k, q in enumerate(others)
+    ]
+    value = hdn_own[...].astype(F32)
+    for k in range(nz - 1):
+        value += hdn_r[k].astype(F32)
+    hdn_o[...] = value
+    t.cross(5)
+    t.line(4)
+    for copy in t_p:
+        copy.wait()
+    acc[...] = acc2[...] + sp[0] + sp[1] + sp[2]
+    t_z = [send(acc, sz.at[k], ts.at[4 + k], tr.at[4 + k], z_to[k]) for k in range(nz - 1)]
+    t.line(5)
+    for w in range(nw):
+        late += t.last(w, fin[w], gos[w], fsem)
+    for copy in t_z:
+        copy.wait()
+    value = acc[...]
+    for k in range(nz - 1):
+        value += sz[k]
+    total[...] = value
+    for copy in late:
+        copy.wait()
+
+
+def back_scatter(dp, rows, d_hidden, x, gain, masks, weights, saved, ffn_grads, ffn_stats, shards, hin, hdn):
+    nz, nw = dp // 2, len(shards)
+    tokens = x.shape[0]
+    group = masks[0].shape[0]
+    most = max(7, nz)
+    stat_shape = (16, 128)
+    paired = [
+        g.reshape(nz, 2, 2, 2 * s[0], s[1]) for g, s in zip(ffn_grads, shards)
+    ]
+    operands = [d_hidden, x, gain, *masks, *weights, *saved, *paired, hin, hdn, ffn_stats]
+    shapes = [jax.ShapeDtypeStruct((dp, group, rows, D), BF), jax.ShapeDtypeStruct(stat_shape, F32)]
+    shapes += [jax.ShapeDtypeStruct(s, F32) for s in shards]
+    shapes.append(jax.ShapeDtypeStruct(hin.shape[1:], BF))
+    shapes.append(jax.ShapeDtypeStruct(hdn.shape[1:], F32))
+    scratch = [pltpu.VMEM((s[0] * 8 * nz, s[1]), BF) for s in shards[2:]]
+    split = [(2 * s[0], s[1] // 2) for s in shards]
+    scratch += [pltpu.VMEM((nz, 2, 2) + s, BF) for s in split[:2]]
+    scratch += [pltpu.VMEM((8, D), F32)]
+    scratch += attend_back_scratch(tokens, masks[0])
+    scratch += [pltpu.VMEM((nz, 2, 2) + s, BF) for s in split]
+    scratch += [pltpu.VMEM((nz, 2) + s, BF) for s in split]
+    scratch += [pltpu.VMEM((nz,) + s, BF) for s in split]
+    scratch += [pltpu.VMEM((nz - 1,) + s, BF) for s in split]
+    scratch += [pltpu.VMEM(s, F32) for s in split]
+    scratch += [
+        pltpu.VMEM(hin.shape[1:], BF),
+        pltpu.VMEM(hdn.shape[1:], BF),
+        pltpu.VMEM((nz - 1,) + hin.shape[1:], BF),
+        pltpu.VMEM((nz - 1,) + hdn.shape[1:], BF),
+        pltpu.VMEM(stat_shape, F32),
+        pltpu.VMEM(stat_shape, F32),
+        pltpu.VMEM((3,) + stat_shape, F32),
+        pltpu.VMEM((nz - 1,) + stat_shape, F32),
+        pltpu.VMEM(stat_shape, F32),
+        DMA((5,)),
+        DMA((dp,)),
+        DMA((dp,)),
+        DMA((nw,)),
+        DMA((nw,)),
+        DMA((nw, 4)),
+        DMA((nw, 4)),
+        DMA((nw, nz)),
+        DMA((nw, nz)),
+        DMA((3, most)),
+        DMA((3, most)),
+        DMA((4 + nz,)),
+        DMA((4 + nz,)),
+        DMA((nw,)),
+        DMA((nw,)),
+        DMA((nw,)),
+    ]
+    return call(
+        functools.partial(back_scatter_kernel, dp, shards),
+        shapes,
+        operands,
+        [VM] * (len(operands) - 5) + [ANY] * 4 + [VM],
+        [VM] * len(shapes),
+        scratch,
+        6,
+    )
+
+
 def routing(routes, pieces, piece_len):
     places = jnp.arange(pieces * piece_len)
     routed = jnp.any(routes[:, None, :] == places[None, :, None], axis=-1)
@@ -1548,7 +1907,9 @@
     heavy_bias = jnp.where(heavy_allowed, 0.0, MASKED)
     masks = (a_select, a_select.swapaxes(1, 2), key_bias, heavy_bias)
     sources = (xin, [gains] + [packed(m) for m in matrices], hin_src, heavy_down)
-    merged = all(m.shape[0] % 8 == 0 for m in (*matrices, heavy_in, heavy_down, layer_input[0, 0]))
+    merged = layer_input.shape[2] % 16 == 0 and all(
+        m.shape[0] % 8 == 0 and m.shape[1] % 256 == 0 for m in (*matrices, heavy_in, heavy_down)
+    )
     if merged:
         got = gather_attend(dp, *sources, masks)
     else:
@@ -1580,31 +1941,42 @@
         w_hin,
         w_hdown,
     )
-    grad_lqkv, grad_hqkv, grad_lout, grad_hout, d_inputs, attn_stats = attend_back(
-        d_hidden, flat_x, gain, *masks, attn_weights, saved
-    )
     rows = tokens // dp
-    stats = jnp.concatenate(
-        [
-            attn_stats[0].reshape(-1, 128),
-            ffn_stats[0].reshape(-1, 128),
-            jnp.broadcast_to(jnp.sum(ffn_stats[1]), (4, 128)),
-        ]
-    )
-    grads = (grad_lin, grad_ldown, grad_hout, grad_lout, grad_hqkv, grad_lqkv)
     shards = (light_in, light_down, heavy_out, light_out, heavy_qkv, light_qkv)
-    sent = [
-        packed_full(grad.astype(BF), shard.shape, nz) for grad, shard in zip(grads, shards)
-    ]
-    hin_tile = hin_src.shape[1:]
-    done = scatter_all(
-        dp,
-        d_inputs.reshape(group, dp, rows, D),
-        stats,
-        sent,
-        grad_hin.astype(BF).reshape((nz, 8) + hin_tile),
-        grad_hdown.astype(BF).reshape(nz, -1, D),
-    )
+    hin_part = grad_hin.reshape((nz, 8) + hin_src.shape[1:])
+    hdn_part = grad_hdown.reshape(nz, -1, D)
+    if merged:
+        done = back_scatter(
+            dp,
+            rows,
+            d_hidden,
+            flat_x,
+            gain,
+            masks,
+            attn_weights,
+            saved,
+            (grad_lin, grad_ldown),
+            ffn_stats,
+            tuple(shard.shape for shard in shards),
+            hin_part,
+            hdn_part,
+        )
+    else:
+        grad_lqkv, grad_hqkv, grad_lout, grad_hout, d_inputs, attn_stats = attend_back(
+            d_hidden, flat_x, gain, *masks, attn_weights, saved
+        )
+        stats = jnp.concatenate(
+            [
+                attn_stats[0].reshape(-1, 128),
+                ffn_stats[0].reshape(-1, 128),
+                jnp.broadcast_to(jnp.sum(ffn_stats[1]), (4, 128)),
+            ]
+        )
+        grads = (grad_lin, grad_ldown, grad_hout, grad_lout, grad_hqkv, grad_lqkv)
+        sent = [packed_full(grad, shard.shape, nz) for grad, shard in zip(grads, shards)]
+        done = scatter_all(
+            dp, d_inputs.reshape(group, dp, rows, D), stats, sent, hin_part, hdn_part
+        )
     d_layer = undeal_rows(dealing, done[0].reshape(seqs, rows, D))[:, None]
     summed = done[1]
     loss_value = summed[12, 0] / (D * token_count)

time: 386 us -> 350 us (0.907)
  Pallas kernels: 349 us -> 312 us
    pallas_call x4 -> x3, Pallas kernels: 344 us -> 308 us  [call(): pl.pallas_call(kernel, out_shape=out_shape, in_specs=in_specs, out_specs=...]
where the time goes in v5:
time: 350 us; the launch traced here: 345 us
  Pallas kernels  312 us (89%)
  local copies, waits for them, and re-layouts  18.4 us (5%)
  other arithmetic  10.7 us (3%)
  between operations  3.78 us (1%)
    pallas_call x3, Pallas kernels, call(): pl.pallas_call(kernel, out_shape=out_shape, in_specs=in_specs, out_specs=...  308 us
    unnamed x29, local copies, waits for them, and re-layouts  8.84 us

profile of v5, /device:TPU:0, one launch (start us, length us, event | category | flops | bytes accessed | tf_op | source)
XLA Modules:
  0.0 345.3 jit_solution(9023351978042249160)
XLA Ops:
  0.7 0.7 dynamic_slice.23
  1.4 1.3 reduce_sum.79
  3.3 0.8 select_reduce_fusion.6
  4.2 0.1 iota_compare_fusion.5
  4.2 0.7 pad_maximum_fusion.1
  5.0 0.8 select_reduce_fusion.3
  5.7 0.1 and_select_fusion
  5.8 0.8 select_reduce_fusion.4
  6.6 0.1 fusion.19
  6.7 0.6 reshape.271.refs_12_.refs_5_
  7.4 0.4 fusion
  7.7 0.4 fusion.2
  8.1 0.2 fusion.5
  8.2 0.2 fusion.7
  8.4 1.6 select_reduce_fusion
  10.0 0.1 reshape.268
  10.1 0.6 pad.4.refs_1_
  10.7 0.9 copy.77
  11.6 1.1 copy.73
  12.6 0.2 copy.82
  12.8 1.0 reshape.270.refs_8_
  13.8 1.4 fusion.22
  15.3 0.2 select_reduce_fusion.2
  15.5 0.1 select_n.90
  15.5 0.7 fusion.11
  16.2 0.7 fusion.9
  16.9 0.7 copy.61.refs_10_.refs_3_
  17.7 0.1 fusion.17
  17.7 0.8 reshape.298.score
  18.5 0.7 copy.64.select
  19.2 0.7 or_select_fusion.refs_13_.refs_6_
  20.0 0.9 copy.75
  20.8 2.2 shard_map.256.refs_0_
  23.0 124.5 %shard_map.257 = (bf16[2,8,32,768]{3,2,1,0:T(8,128)(2,1)}, bf16[4,2,2,16,768]{4,3,2,1,0:T(8,128)(2,1)}, bf16[4,2,2,48,1536]{4,3,2,1,0:T(8,128)(2,1)}, bf16[4,2,2...) custom-call(bf16[16,32,768]{2,1,0:T(8,128)(2,1)} %shard_map.256.refs, ...), custom_call_target="tpu_custom_call" | custom-call | tf_op jit(solution)/shard_map/pallas_call | solution.py:72
  147.5 67.6 %shard_map.258 = (bf16[768,2048]{1,0:T(8,128)(2,1)}, bf16[1024,768]{1,0:T(8,128)(2,1)}, bf16[768,1024]{1,0:T(8,128)(2,1)}, bf16[512,768]{1,0:T(8,128)(2,1)}, f32[512,768]{1,0:T(8,128)}, /*index=5*/f32[8,768]{1,0:T(8,128)}) custom-call(f32[512,768]{1,0:T(8,128)} %get-tuple-element.49.hidden, bf16[2,64,256]{2,1,0:T(8,128)(2,1)} %copy.64.select, ...), custom_call_target="tpu_custom_call" | custom-call | tf_op jit(solution)/shard_map/pallas_call | solution.py:72
  215.1 115.4 %shard_map.259 = (bf16[8,2,32,768]{3,2,1,0:T(8,128)(2,1)}, f32[16,128]{1,0:T(8,128)}, f32[24,2048]{1,0:T(8,128)}, f32[32,768]{1,0:T(8,128)}, f32[24,768]{1,0:T(8...) custom-call(f32[512,768]{1,0:T(8,128)} %get-tuple-element.55.refs_0_, ...), custom_call_target="tpu_custom_call" | custom-call | tf_op jit(solution)/shard_map/pallas_call | solution.py:72
  330.5 0.0 copy-start.1
  330.5 1.2 slice.17
  332.4 0.8 slice_bitcast_fusion
  333.2 0.6 dynamic_slice.29
  333.8 0.6 dynamic_slice.28
  334.4 2.5 shard_map.260
  336.8 0.0 copy-done.1
  336.8 0.3 reshape.296
  337.2 0.0 copy-start.4
  337.2 0.0 copy-start.7
  337.2 0.0 copy-start.2
  337.2 0.5 copy.69
  337.7 0.0 copy-start.6
  337.7 0.0 copy-start.3
  337.7 0.0 copy-start.5
  337.7 0.0 copy-start
  337.7 1.3 copy.81
  339.1 0.0 copy-done.4
  339.1 0.7 copy.90
  339.7 0.0 copy-done.7
  339.7 0.6 copy.91
  340.4 0.0 copy-done.2
  340.4 0.7 copy.92
  341.0 0.0 copy-done.6
  341.0 0.6 copy.93
  341.7 0.7 copy.94
  342.4 0.6 copy.95
  343.0 0.7 copy.96
  (20 shorter events, 0.1 us)
Async XLA Ops:
  330.5 6.3 %copy-start.1 = (bf16[8,24,1024]{2,1,0:T(8,128)(2,1)S(1)}, bf16[8,24,1024]{2,1,0:T(8,128)(2,1)}, u32[]{:S(2)}) copy-start(bf16[8,24,1024]{2,1,0:T(8,128)(2,1)} %get-tuple-element.84) | copy-start | bytes 1179652
  337.2 1.9 copy-start.4
  337.2 2.5 copy-start.7
  337.2 3.1 copy-start.2
  337.7 3.4 copy-start.6
  337.7 4.0 %copy-start.3 = (f32[24,2048]{1,0:T(8,128)S(1)}, f32[24,2048]{1,0:T(8,128)}, u32[]{:S(2)}) copy-start(f32[24,2048]{1,0:T(8,128)} %get-tuple-element.162) | copy-start | bytes 589828
  337.7 4.7 %copy-start.5 = (f32[32,768]{1,0:T(8,128)S(1)}, f32[32,768]{1,0:T(8,128)}, u32[]{:S(2)}) copy-start(f32[32,768]{1,0:T(8,128)} %get-tuple-element.163) | copy-start | bytes 294916
  337.7 5.3 %copy-start = (f32[128,768]{1,0:T(8,128)S(1)}, f32[128,768]{1,0:T(8,128)}, u32[]{:S(2)}) copy-start(f32[128,768]{1,0:T(8,128)} %get-tuple-element.165) | copy-start | bytes 1179652

commit v6 on v5

--- a/solution.py
+++ b/solution.py
@@ -115,6 +115,79 @@
         out_specs=VM,
         compiler_params=pltpu.CompilerParams(vmem_limit_bytes=VMEM_BYTES),
     )(dealing, rows)
+
+
+def prepare_kernel(deal_ref, x_ref, heavy_ref, one_ref, two_ref, xin, hin, gains):
+    def body(i, carry):
+        xin[i] = x_ref[deal_ref[i]]
+        return carry
+
+    lax.fori_loop(0, xin.shape[0], body, 0)
+    count = one_ref.shape[1]
+    units = D // count
+    step = heavy_ref.shape[1] // 2 // units
+    for j in range(8):
+        for k in range(units // 8):
+            for g in (0, 1):
+                start = g * heavy_ref.shape[1] // 2 + (k * 8 + j) * step
+                spot = (g * (units // 8) + k) * step
+                hin[j, :, spot : spot + step] = heavy_ref[:, start : start + step]
+    mine = lax.axis_index("dp") * 4 + lax.axis_index("fsdp")
+    row = lax.broadcasted_iota(jnp.int32, (count, D), 0)
+    lane = lax.broadcasted_iota(jnp.int32, (count, D), 1)
+    hot = jnp.where(lane == row + mine * count, 1.0, 0.0).astype(BF)
+    lines = [jnp.broadcast_to(ref[...], (8, count)) for ref in (one_ref, two_ref)]
+    one, two = (jnp.dot(line, hot, preferred_element_type=F32) for line in lines)
+    kind = lax.broadcasted_iota(jnp.int32, (8, D), 0)
+    gains[...] = jnp.where(kind == 0, one, jnp.where(kind == 1, two, 0.0)).astype(BF)
+
+
+def prepare(dealing, rows, heavy_in, gain_one, gain_two):
+    count = gain_one.shape[0]
+    columns = heavy_in.shape[1] // 8
+    return pl.pallas_call(
+        prepare_kernel,
+        out_shape=[
+            jax.ShapeDtypeStruct(rows.shape, BF),
+            jax.ShapeDtypeStruct((8, heavy_in.shape[0], columns), BF),
+            jax.ShapeDtypeStruct((8, D), BF),
+        ],
+        in_specs=[pl.BlockSpec(memory_space=pltpu.SMEM), VM, VM, VM, VM],
+        out_specs=[VM] * 3,
+        compiler_params=pltpu.CompilerParams(vmem_limit_bytes=VMEM_BYTES),
+    )(dealing, rows, heavy_in, gain_one.reshape(1, count), gain_two.reshape(1, count))
+
+
+def finish_kernel(units, deal_ref, x_ref, hin, *refs):
+    count = (len(refs) - 2) // 2
+    ins, (rows, heavy), outs = refs[:count], refs[count : count + 2], refs[count + 2 :]
+
+    def body(i, carry):
+        rows[deal_ref[i]] = x_ref[i].astype(F32)
+        return carry
+
+    lax.fori_loop(0, x_ref.shape[0], body, 0)
+    step = heavy.shape[1] // 2 // units
+    for j in range(8):
+        for k in range(units // 8):
+            for g in (0, 1):
+                start = g * heavy.shape[1] // 2 + (k * 8 + j) * step
+                spot = (g * (units // 8) + k) * step
+                heavy[:, start : start + step] = hin[j, :, spot : spot + step].astype(F32)
+    for source, out in zip(ins, outs):
+        out[...] = source[...]
+
+
+def finish_all(units, dealing, rows, hin, grads, heavy_shape):
+    shapes = [jax.ShapeDtypeStruct(rows.shape, F32), jax.ShapeDtypeStruct(heavy_shape, F32)]
+    shapes += [jax.ShapeDtypeStruct(g.shape, F32) for g in grads]
+    return pl.pallas_call(
+        functools.partial(finish_kernel, units),
+        out_shape=shapes,
+        in_specs=[pl.BlockSpec(memory_space=pltpu.SMEM)] + [VM] * (2 + len(grads)),
+        out_specs=[VM] * len(shapes),
+        compiler_params=pltpu.CompilerParams(vmem_limit_bytes=VMEM_BYTES),
+    )(dealing, rows, hin, *grads)
 
 
 def packed(matrix):
@@ -571,6 +644,13 @@
         z[r, :] = (gelu_value(up_l[r, :fl]) * up_l[r, fl:]).astype(BF)
 
     tiles(tokens, 256, light_up)
+
+    def light_slopes(r):
+        value, slope = gelu_parts(up_l[r, :fl])
+        up_l[r, :fl] = up_l[r, fl:] * slope
+        up_l[r, fl:] = value
+
+    tiles(tokens, 64, light_slopes)
     relay(every, 0, there, back)
 
     def light_down(r):
@@ -596,6 +676,14 @@
     first = send(part.at[1 - c], near, es.at[0], er.at[0], partner)
     heavy(c)
     there = fold(near, far, 0, first)
+    for e in (0, 1):
+
+        def heavy_slopes(r, e=e):
+            value, slope = gelu_parts(up_h[e, r, :fh])
+            up_h[e, r, :fh] = up_h[e, r, fh:] * slope
+            up_h[e, r, fh:] = value
+
+        tiles(rows_h, 128, heavy_slopes)
     hf = folded(near, far, there) * score[...]
     hf_high, hf_low = halves(hf)
     for s in range(group):
@@ -621,11 +709,14 @@
 
     def light_back(r):
         dz = dot_back(dl[r, :], w_dn[...])
-        value, slope = gelu_parts(up_l[r, :fl])
-        dup_l[r, :fl] = (dz * up_l[r, fl:] * slope).astype(BF)
-        dup_l[r, fl:] = (dz * value).astype(BF)
+        dup_l[r, :fl] = (dz * up_l[r, :fl]).astype(BF)
+        dup_l[r, fl:] = (dz * up_l[r, fl:]).astype(BF)
 
     tiles(tokens, 256, light_back)
+    def light_in_back(r):
+        dhn[r, :] = dot_back(dup_l[r, :], w_in[...])
+
+    tiles(tokens, 256, light_in_back)
     relay(d_every, 1, there, back)
 
     def light_grad(j):
@@ -640,9 +731,8 @@
             d = d_every[e, pl.ds(2 * i, 2)].reshape(2 * group * cap, D)
             r = pl.ds(pl.multiple_of(i * 256, 256), 256)
             dz = dot_back(d, w_hdn[...])
-            value, slope = gelu_parts(up_h[e, r, :fh])
-            dup_h[e, r, :fh] = (dz * up_h[e, r, fh:] * slope).astype(BF)
-            dup_h[e, r, fh:] = (dz * value).astype(BF)
+            dup_h[e, r, :fh] = (dz * up_h[e, r, :fh]).astype(BF)
+            dup_h[e, r, fh:] = (dz * up_h[e, r, fh:]).astype(BF)
             v = dot_back(dup_h[e, r, :], w_hin[...]).astype(BF)
             part[e, pl.ds(2 * i, 2)] = v.reshape(2, group * cap, D)
             return carry
@@ -659,10 +749,6 @@
 
     tiles(2 * fl, 1024, light_in_grad)
 
-    def light_in_back(r):
-        dhn[r, :] = dot_back(dup_l[r, :], w_in[...])
-
-    tiles(tokens, 256, light_in_back)
     every_rows = every[...].reshape(2 * rows_h, D)
 
     def heavy_grad(j):
@@ -974,32 +1060,118 @@
     )
 
 
+def route_part(deal, lengths, routes_a, routes_f, scores, tables):
+    sel_a, selt_a, key_bias, heavy_bias, sel_f, selt_f, score, mask, scale = tables
+    hi, lo, x, c = place()
+    group, cap, width = sel_a.shape
+    seqs = deal.shape[1]
+    here = ((x * 2 + c) * width).astype(F32)
+
+    def line(shape, dim):
+        return lax.broadcasted_iota(jnp.int32, shape, dim).astype(F32)
+
+    lane = lax.broadcasted_iota(jnp.int32, (1, seqs), 1)
+    before = jnp.where(line((width, width), 0) > line((width, width), 1), 1.0, 0.0).astype(BF)
+    length_row = lengths[...].astype(F32)
+    count = jnp.sum(length_row, axis=1, keepdims=True)
+    column = line((width, 1), 0)
+    row = line((1, width), 1)
+    ones = jnp.ones((8, routes_a.shape[1]), BF)
+
+    def columns_of(routes, base):
+        held = jnp.where(routes == column + base, 1.0, 0.0)
+        rank = jnp.sum(dot(before, held.astype(BF)), axis=1, keepdims=True)
+        there = jnp.sum(held, axis=1, keepdims=True)
+        hot_t = jnp.where(rank == line((width, cap), 1), 1.0, 0.0) * there
+        return held, rank, hot_t
+
+    def rows_of(held):
+        there = dot_back(ones, held.astype(BF))
+        rank = dot_back(there.astype(BF), before)
+        return jnp.where(rank[:1] == line((cap, width), 0), 1.0, 0.0) * there[:1]
+
+    for s in range(group):
+        place_here = lane == (hi * 2 + lo) * group + s
+        which = jnp.sum(jnp.where(place_here, deal[...].astype(F32), 0.0), axis=1, keepdims=True)
+        one = line((seqs, 1), 0) == which
+        length = jnp.sum(
+            jnp.where(line((1, seqs), 1) == which, length_row, 0.0), axis=1, keepdims=True
+        )
+        ra, rf, sf = (
+            jnp.sum(jnp.where(one, ref[...].astype(F32), 0.0), axis=0, keepdims=True)
+            for ref in (routes_a, routes_f, scores)
+        )
+        held, rank, hot_t = columns_of(ra, here)
+        hot = rows_of(held)
+        sel_a[s] = hot.astype(BF)
+        selt_a[s] = hot_t.astype(BF)
+        own_spot = jnp.sum(hot * (row + here + 1.0), axis=1, keepdims=True) - 1.0
+        for q in range(4):
+            base = float(q * width)
+            _, _, other_t = columns_of(ra, base)
+            spot = jnp.sum(other_t * (column + base + 1.0), axis=0, keepdims=True) - 1.0
+            live = jnp.where((spot >= 0.0) & (spot < length), 1.0, 0.0)
+            same = jnp.where(own_spot == spot, 1.0, 0.0)
+            heavy_bias[s, :, q * cap : (q + 1) * cap] = jnp.where(live + same > 0.0, 0.0, MASKED)
+        for b in range(width // WIN):
+            key = line((1, 3 * WIN), 1) + (here + float((b - 1) * WIN))
+            live = (key >= 0.0) & (key < length)
+            key_bias[s * (width // WIN) + b] = jnp.where(live, 0.0, MASKED)
+        valid = jnp.where(column + here < length, 1.0, 0.0)
+        mask[s * width : (s + 1) * width, :] = valid
+        scale[s * width : (s + 1) * width, :] = 2.0 * valid / (D * count)
+        held, rank, hot_t = columns_of(rf, here)
+        sel_f[s] = rows_of(held).astype(BF)
+        selt_f[s] = hot_t.astype(BF)
+        slot = jnp.sum(held * rank, axis=0, keepdims=True)
+        owned = jnp.sum(held, axis=0, keepdims=True)
+        hits = jnp.where(slot == line((cap, slot.shape[1]), 0), 1.0, 0.0)
+        score[s * cap : (s + 1) * cap, :] = jnp.sum(hits * (owned * sf), axis=1, keepdims=True)
+
+
+def route_shapes(group, width, tokens):
+    return [
+        jax.ShapeDtypeStruct((group, CAP, width), BF),
+        jax.ShapeDtypeStruct((group, width, CAP), BF),
+        jax.ShapeDtypeStruct((tokens // WIN, 1, 3 * WIN), F32),
+        jax.ShapeDtypeStruct((group, CAP, 4 * CAP), F32),
+        jax.ShapeDtypeStruct((group, CAP, width), BF),
+        jax.ShapeDtypeStruct((group, width, CAP), BF),
+        jax.ShapeDtypeStruct((group * CAP, 1), F32),
+        jax.ShapeDtypeStruct((tokens, 1), F32),
+        jax.ShapeDtypeStruct((tokens, 1), F32),
+    ]
+
+
 def gather_attend_kernel(dp, nw, *refs):
-    n_in, n_out = 7 + nw, 3 + nw + 12
+    n_in, n_out = 8 + nw, 3 + nw + 21
     ins, outs, rest = refs[:n_in], refs[n_in : n_in + n_out], refs[n_in + n_out :]
     xin, ws, hin, hdn = ins[0], ins[1 : 1 + nw], ins[1 + nw], ins[2 + nw]
-    masks = ins[3 + nw :]
+    integers = ins[3 + nw :]
     xo, wos, hin_o, hdn_o = outs[0], outs[1 : 1 + nw], outs[1 + nw], outs[2 + nw]
-    gain, saved = outs[3 + nw], outs[4 + nw :]
+    gain, tables, saved = outs[3 + nw], outs[4 + nw : 13 + nw], outs[13 + nw :]
     parts, rest = rest[: 3 * nw + 3], rest[3 * nw + 3 :]
     halves = (parts[:nw], parts[nw : 2 * nw], parts[2 * nw : 3 * nw], parts[3 * nw :])
     g = Gather(dp, xin, ws, hin, hdn, xo, wos, hin_o, hdn_o, rest[:11], halves)
     g.meet()
     for w in range(nw):
         g.swap(w)
-    g.rows()
     for w in (0, 1, 2):
         g.join(w)
-    g.heavy_plane()
     for w in (0, 1, 2):
         g.plane(w)
+    g.rows()
     for w in (3, 4, 5, 6):
         g.join(w)
-    g.heavy_line()
+    g.heavy_plane()
+    route_part(*integers, tables)
     g.cross(0)
     g.core(0)
     g.cross(1)
     g.cross(2)
+    g.heavy_line()
+    g.plane(3)
+    g.plane(4)
     g.ready(0)
     total = jnp.zeros(gain.shape, F32)
     for z in range(dp // 2):
@@ -1014,34 +1186,36 @@
         g.core(2)
         g.ready(2)
 
+    def light_projection():
+        g.plane(5)
+        g.plane(6)
+        g.ready(1)
+
     def keys_travel():
-        g.plane(3)
-        g.plane(4)
-
-    def half_way():
         g.cross(3)
         g.cross(4)
-        g.plane(5)
-
-    def light_done():
+
+    def half_way():
         g.core(3)
         g.core(4)
+
+    def light_done():
         g.cross(5)
-        g.plane(6)
+        g.cross(6)
 
     def heavy_done():
+        g.core(5)
+        g.core(6)
         g.ready(3)
         g.ready(4)
-        g.core(5)
-        g.cross(6)
 
     full = [wos[w].reshape(-1, wos[w].shape[-1]) for w in range(nw)]
-    stages = [heavy_projection, lambda: g.ready(1), keys_travel, half_way, light_done, heavy_done]
+    stages = [heavy_projection, light_projection, keys_travel, half_way, light_done, heavy_done]
     attend_body(
         stages,
         xo.reshape(-1, D),
         gain,
-        *masks,
+        *tables[:4],
         full[1],
         full[2],
         full[3],
@@ -1049,24 +1223,25 @@
         *saved,
         *rest[11:],
     )
-    g.core(6)
     g.ready(5)
     g.ready(6)
     g.heavy_ready()
 
 
-def gather_attend(dp, xin, weights, hin, hdn, masks):
+def gather_attend(dp, xin, weights, hin, hdn, integers):
     nw = len(weights)
     shapes = gather_shapes(dp, xin, weights, hin, hdn, True)
-    tokens = shapes[0].shape[0] * dp * xin.shape[1]
+    group, width = shapes[0].shape[0], dp * xin.shape[1]
+    tables = route_shapes(group, width, group * width)
     shapes.append(jax.ShapeDtypeStruct((8, D), F32))
-    shapes += attend_shapes(tokens, masks[0])
+    shapes += tables
+    shapes += attend_shapes(group * width, tables[0])
     return call(
         functools.partial(gather_attend_kernel, dp, nw),
         shapes,
-        [xin, *weights, hin, hdn, *masks],
-        [ANY] * (3 + nw) + [VM] * 4,
-        [VM] * 6 + [ANY] * 4 + [VM] * 12,
+        [xin, *weights, hin, hdn, *integers],
+        [ANY] * (3 + nw) + [VM] * 5,
+        [VM] * 6 + [ANY] * 4 + [VM] * 21,
         [pltpu.VMEM((w.shape[0], w.shape[1] // 2), BF) for w in weights] * 2
         + [pltpu.VMEM((2 * w.shape[0], w.shape[1] // 2), BF) for w in weights]
         + [DMA((nw,))] * 3
@@ -1210,6 +1385,15 @@
         return carry
 
     lax.fori_loop(0, group * blocks // 2, light, 0)
+    third.wait()
+    total = (got[x_].astype(F32) + far[...].astype(F32)).astype(BF)
+    for s in range(group):
+        d_hproj[s * cap : (s + 1) * cap, wh:] = total[s]
+
+    def heavy_grad(j):
+        g_hqkv[:, j] = dot_grad(a_rows[...], d_hproj[:, j]).astype(BF)
+
+    tiles(3 * wh, 768, heavy_grad)
     stages[3]()
     lax.fori_loop(group * blocks // 2, group * blocks, light, 0)
     edge[0] = d_rim[:, :WIN, :].astype(BF)
@@ -1218,16 +1402,6 @@
         edge.at[0], edge.at[1], edge_in.at[0], edge_in.at[1], ls, lr, rs, rr
     )
     stages[4]()
-    third.wait()
-    total = (got[x_].astype(F32) + far[...].astype(F32)).astype(BF)
-    for s in range(group):
-        d_hproj[s * cap : (s + 1) * cap, wh:] = total[s]
-
-    def heavy_grad(j):
-        g_hqkv[:, j] = dot_grad(a_rows[...], d_hproj[:, j]).astype(BF)
-
-    tiles(3 * wh, 768, heavy_grad)
-    stages[5]()
     d_high, d_low = halves(dot_back(d_hproj[...], w_hqkv[...]))
     finish()
     for s in range(group):
@@ -1239,7 +1413,7 @@
         g_lqkv[:, j] = dot_grad(xn[...], d_lproj[:, j]).astype(BF)
 
     tiles(3 * wl, 768, light_grad)
-    stages[6]()
+    stages[5]()
     stats[...] = jnp.zeros(stats.shape, F32)
     for s in range(group):
         r = slice(s * width, (s + 1) * width)
@@ -1255,12 +1429,12 @@
         dx[r, :] = (
             d_hidden[r, :] + inv * gain[0:1, :] * d - h * (inv * inv * inv * mean)
         ).astype(BF)
-    stages[7]()
+    stages[6]()
 
 
 def attend_back_kernel(*refs):
     meet(line_peers())
-    attend_back_body([lambda: None] * 8, *refs)
+    attend_back_body([lambda: None] * 7, *refs)
 
 
 def attend_back_scratch(tokens, select):
@@ -1653,25 +1827,23 @@
     def before_light():
         t.cross(0)
         t.cross(1)
+        t.plane(2)
 
     def half_way():
+        t.core(4)
+        t.plane(3)
         t.line(0)
         t.line(1)
-        t.plane(2)
-        t.plane(3)
 
     def rims_left():
+        t.plane(4)
         t.cross(2)
         t.cross(3)
 
-    def heavy_grad_done():
-        t.core(4)
+    def light_grad_done():
+        t.core(5)
         t.line(2)
         t.line(3)
-
-    def light_grad_done():
-        t.core(5)
-        t.plane(4)
 
     def rows_done():
         rows = dx.reshape(dxo.shape[1], dp, dxo.shape[2], D)
@@ -1685,7 +1857,6 @@
         before_light,
         half_way,
         rims_left,
-        heavy_grad_done,
         light_grad_done,
         rows_done,
     ]
@@ -1702,6 +1873,7 @@
     t_c = send(acc, sc, ts.at[0], tr.at[0], partner)
     t.plane(5)
     t.cross(4)
+    t.line(4)
     t_c.wait()
     acc2[...] = acc[...] + sc[...]
     t_p = [
@@ -1735,7 +1907,6 @@
         value += hdn_r[k].astype(F32)
     hdn_o[...] = value
     t.cross(5)
-    t.line(4)
     for copy in t_p:
         copy.wait()
     acc[...] = acc2[...] + sp[0] + sp[1] + sp[2]
@@ -1859,61 +2030,35 @@
     group = seqs // dp
     gain_len = gain_attn.shape[0]
     hidden_units = heavy_in.shape[1] // 2 // n
-    xin = deal_rows(dealing, layer_input[:, 0])
     mine = data_index * pieces + piece
-    owned = jnp.arange(D)[None, :] // gain_len == mine
-    spread_out = jnp.broadcast_to(
-        jnp.stack([gain_attn, gain_ffn])[:, None, :], (2, D // gain_len, gain_len)
-    ).reshape(2, D)
-    gains = jnp.pad(jnp.where(owned, spread_out, 0.0).astype(BF), ((0, 6), (0, 0)))
+    tokens = layer_input.shape[2] * dp
     matrices = (light_qkv, heavy_qkv, light_out, heavy_out, light_in, light_down)
     hin_rows = heavy_in.shape[0]
-    hin_src = (
-        heavy_in.reshape(hin_rows, 2, nz, 8, hidden_units)
-        .transpose(3, 0, 1, 2, 4)
-        .reshape(8, hin_rows, 2 * nz * hidden_units)
-    )
-    if hin_rows % 8:
-        hin_src = hin_src.reshape(8, -1, 128)
-    tokens = layer_input.shape[2] * dp
-    chosen = lax.dynamic_slice_in_dim(dealing, data_index * group, group)
-    one = (chosen[:, None] == jnp.arange(seqs)[None, :])
-    seq_lengths = jnp.sum(jnp.where(one, lengths[None, :], 0), axis=1)
-    attn_pick = jnp.sum(jnp.where(one[:, :, None], attn_routes[None], 0), axis=1)
-    ffn_pick = jnp.sum(jnp.where(one[:, :, None], ffn_routes[None], 0), axis=1)
-    score_pick = jnp.sum(jnp.where(one[:, :, None], ffn_scores[None], 0.0), axis=1)
     token_count = jnp.sum(lengths).astype(F32)
-    positions = piece * tokens + jnp.arange(tokens)
-    valid_mask = positions[None, :] < seq_lengths[:, None]
-    a_hot, a_spots = routing(attn_pick, pieces, tokens)
-    f_hot, f_spots = routing(ffn_pick, pieces, tokens)
-    a_select = lax.dynamic_index_in_dim(a_hot, piece, 1, False).astype(BF)
-    f_select = lax.dynamic_index_in_dim(f_hot, piece, 1, False).astype(BF)
-    a_spot = lax.dynamic_index_in_dim(a_spots, piece, 1, False)
-    f_spot = lax.dynamic_index_in_dim(f_spots, piece, 1, False)
-    slot_score = jnp.sum(
-        jnp.where(f_spot[:, :, None] == ffn_pick[:, None, :], score_pick[:, None, :], 0.0), axis=-1
-    )
-    key_pos = piece * tokens - WIN + jnp.arange(tokens + 2 * WIN)
-    live_key = (key_pos >= 0)[None, :] & (key_pos[None, :] < seq_lengths[:, None])
-    key_line = jnp.where(live_key, 0.0, MASKED)
-    key_bias = jnp.stack(
-        [key_line[:, b : b + 3 * WIN] for b in range(0, tokens, WIN)], axis=1
-    ).reshape(-1, 1, 3 * WIN)
-    all_spots = a_spots.reshape(group, pieces * CAP)
-    heavy_allowed = ((all_spots >= 0) & (all_spots < seq_lengths[:, None]))[:, None, :] | (
-        a_spot[:, :, None] == all_spots[:, None, :]
-    )
-    heavy_bias = jnp.where(heavy_allowed, 0.0, MASKED)
-    masks = (a_select, a_select.swapaxes(1, 2), key_bias, heavy_bias)
-    sources = (xin, [gains] + [packed(m) for m in matrices], hin_src, heavy_down)
-    merged = layer_input.shape[2] % 16 == 0 and all(
-        m.shape[0] % 8 == 0 and m.shape[1] % 256 == 0 for m in (*matrices, heavy_in, heavy_down)
+    merged = (
+        layer_input.shape[2] % 16 == 0
+        and hidden_units % 128 == 0
+        and all(m.shape[0] % 8 == 0 and m.shape[1] % 256 == 0 for m in (*matrices, heavy_down))
     )
     if merged:
-        got = gather_attend(dp, *sources, masks)
+        xin, hin_src, gains = prepare(dealing, layer_input[:, 0], heavy_in, gain_attn, gain_ffn)
+        integers = (dealing.reshape(1, -1), lengths.reshape(1, -1), attn_routes, ffn_routes, ffn_scores)
+        got = gather_attend(dp, xin, [gains, *matrices], hin_src, heavy_down, integers)
     else:
-        got = gather_all(dp, *sources)
+        xin = deal_rows(dealing, layer_input[:, 0])
+        owned = jnp.arange(D)[None, :] // gain_len == mine
+        spread_out = jnp.broadcast_to(
+            jnp.stack([gain_attn, gain_ffn])[:, None, :], (2, D // gain_len, gain_len)
+        ).reshape(2, D)
+        gains = jnp.pad(jnp.where(owned, spread_out, 0.0).astype(BF), ((0, 6), (0, 0)))
+        hin_src = (
+            heavy_in.reshape(hin_rows, 2, nz, 8, hidden_units)
+            .transpose(3, 0, 1, 2, 4)
+            .reshape(8, hin_rows, 2 * nz * hidden_units)
+        )
+        if hin_rows % 8:
+            hin_src = hin_src.reshape(8, -1, 128)
+        got = gather_all(dp, xin, [gains] + [packed(m) for m in matrices], hin_src, heavy_down)
     flat_x = got[0].reshape(-1, D)
     w_lqkv, w_hqkv, w_lout, w_hout, w_lin, w_ldown = (
         unpacked(full, *m.shape) for full, m in zip(got[2:8], matrices)
@@ -1922,20 +2067,24 @@
     w_hdown = got[9].reshape(-1, D)
     attn_weights = (w_lqkv, w_hqkv, w_lout, w_hout)
     if merged:
-        gain, hidden, *saved = got[10:]
+        gain, tables, (hidden, *saved) = got[10], got[11:20], got[20:]
+        masks, ffn_masks = tables[:4], tables[4:]
     else:
         gain = jnp.sum(got[1].reshape(n, 8, D).astype(F32), axis=0)
+        masks, ffn_masks = integer_tables(
+            dealing, lengths, attn_routes, ffn_routes, ffn_scores, group, pieces, tokens
+        )
         hidden, *saved = attend(flat_x, gain, *masks, *attn_weights)
-    weight_mask = valid_mask.reshape(-1, 1).astype(F32)
+    f_select, f_select_t, slot_score, weight_mask, weight_scale = ffn_masks
     grad_lin, grad_ldown, grad_hin, grad_hdown, d_hidden, ffn_stats = feed_forward(
         hidden,
         f_select,
-        f_select.swapaxes(1, 2),
-        slot_score.reshape(-1, 1),
+        f_select_t,
+        slot_score,
         gain,
         teacher.reshape(-1, D),
         weight_mask,
-        2.0 * weight_mask / (D * token_count),
+        weight_scale,
         w_lin,
         w_ldown,
         w_hin,
@@ -1977,24 +2126,30 @@
         done = scatter_all(
             dp, d_inputs.reshape(group, dp, rows, D), stats, sent, hin_part, hdn_part
         )
-    d_layer = undeal_rows(dealing, done[0].reshape(seqs, rows, D))[:, None]
     summed = done[1]
     loss_value = summed[12, 0] / (D * token_count)
     own_one = lax.dynamic_slice_in_dim(summed[:6].reshape(-1), mine * gain_len, gain_len)
     own_two = lax.dynamic_slice_in_dim(summed[6:12].reshape(-1), mine * gain_len, gain_len)
-    g_lin, g_ldown, g_hout, g_lout, g_hqkv, g_lqkv = (
-        full.reshape(shard.shape) for full, shard in zip(done[2:8], shards)
-    )
-    g_hin = (
-        done[8]
-        .astype(F32)
-        .reshape(8, hin_rows, 2, nz, hidden_units)
-        .transpose(1, 2, 3, 0, 4)
-        .reshape(heavy_in.shape)
-    )
+    back_rows = done[0].reshape(seqs, rows, D)
+    if merged:
+        d_layer, g_hin, *owned = finish_all(
+            n, dealing, back_rows, done[8], [*done[2:8], done[9]], heavy_in.shape
+        )
+    else:
+        d_layer = undeal_rows(dealing, back_rows)
+        owned = [full.reshape(shard.shape) for full, shard in zip(done[2:8], shards)]
+        owned.append(done[9].reshape(heavy_down.shape))
+        g_hin = (
+            done[8]
+            .astype(F32)
+            .reshape(8, hin_rows, 2, nz, hidden_units)
+            .transpose(1, 2, 3, 0, 4)
+            .reshape(heavy_in.shape)
+        )
+    g_lin, g_ldown, g_hout, g_lout, g_hqkv, g_lqkv, g_hdown = owned
     return (
         loss_value,
-        d_layer,
+        d_layer[:, None],
         own_one,
         own_two,
         g_lqkv,
@@ -2004,8 +2159,53 @@
         g_lin,
         g_ldown,
         g_hin,
-        done[9].reshape(heavy_down.shape),
+        g_hdown,
     )
+
+
+def integer_tables(dealing, lengths, attn_routes, ffn_routes, ffn_scores, group, pieces, tokens):
+    seqs = dealing.shape[0]
+    data_index = lax.axis_index("dp")
+    piece = lax.axis_index("fsdp")
+    chosen = lax.dynamic_slice_in_dim(dealing, data_index * group, group)
+    one = chosen[:, None] == jnp.arange(seqs)[None, :]
+    seq_lengths = jnp.sum(jnp.where(one, lengths[None, :], 0), axis=1)
+    attn_pick = jnp.sum(jnp.where(one[:, :, None], attn_routes[None], 0), axis=1)
+    ffn_pick = jnp.sum(jnp.where(one[:, :, None], ffn_routes[None], 0), axis=1)
+    score_pick = jnp.sum(jnp.where(one[:, :, None], ffn_scores[None], 0.0), axis=1)
+    token_count = jnp.sum(lengths).astype(F32)
+    positions = piece * tokens + jnp.arange(tokens)
+    valid_mask = positions[None, :] < seq_lengths[:, None]
+    a_hot, a_spots = routing(attn_pick, pieces, tokens)
+    f_hot, f_spots = routing(ffn_pick, pieces, tokens)
+    a_select = lax.dynamic_index_in_dim(a_hot, piece, 1, False).astype(BF)
+    f_select = lax.dynamic_index_in_dim(f_hot, piece, 1, False).astype(BF)
+    a_spot = lax.dynamic_index_in_dim(a_spots, piece, 1, False)
+    f_spot = lax.dynamic_index_in_dim(f_spots, piece, 1, False)
+    slot_score = jnp.sum(
+        jnp.where(f_spot[:, :, None] == ffn_pick[:, None, :], score_pick[:, None, :], 0.0), axis=-1
+    )
+    key_pos = piece * tokens - WIN + jnp.arange(tokens + 2 * WIN)
+    live_key = (key_pos >= 0)[None, :] & (key_pos[None, :] < seq_lengths[:, None])
+    key_line = jnp.where(live_key, 0.0, MASKED)
+    key_bias = jnp.stack(
+        [key_line[:, b : b + 3 * WIN] for b in range(0, tokens, WIN)], axis=1
+    ).reshape(-1, 1, 3 * WIN)
+    all_spots = a_spots.reshape(group, pieces * CAP)
+    heavy_allowed = ((all_spots >= 0) & (all_spots < seq_lengths[:, None]))[:, None, :] | (
+        a_spot[:, :, None] == all_spots[:, None, :]
+    )
+    heavy_bias = jnp.where(heavy_allowed, 0.0, MASKED)
+    weight_mask = valid_mask.reshape(-1, 1).astype(F32)
+    masks = (a_select, a_select.swapaxes(1, 2), key_bias, heavy_bias)
+    ffn_masks = (
+        f_select,
+        f_select.swapaxes(1, 2),
+        slot_score.reshape(-1, 1),
+        weight_mask,
+        2.0 * weight_mask / (D * token_count),
+    )
+    return masks, ffn_masks
 
 
 def packed_full(grad, shard_shape, nz):

time: 350 us -> 332 us (0.949); the launches traced: 345 us -> 331 us
  local copies, waits for them, and re-layouts: 18.4 us -> 1.7 us
  Pallas kernels: 312 us -> 326 us
  other arithmetic: 10.7 us -> 0.62 us
    pallas_call x3, Pallas kernels: 308 us -> 320 us  [call(): pl.pallas_call(kernel, out_shape=out_shape, in_specs=in_specs, out_specs=...]
    unnamed x29 -> x4, local copies, waits for them, and re-layouts: 8.84 us -> 0.01 us
    reduce_sum x5 -> x0, other arithmetic: 4.14 us -> none  [the longest x1 1.55 us: routing(): jnp.sum(jnp.where(hot, places.reshape(1, pieces, 1, piece_len), 0), axis=-1)]
where the time goes in v6:
time: 332 us; the launch traced here: 331 us
  Pallas kernels  326 us (98%)
    pallas_call x3, Pallas kernels, call(): pl.pallas_call(kernel, out_shape=out_shape, in_specs=in_specs, out_specs=...  320 us

profile of v6, /device:TPU:0, one launch (start us, length us, event | category | flops | bytes accessed | tf_op | source)
XLA Modules:
  0.0 331.3 jit_solution(1282168872716332732)
XLA Ops:
  0.6 2.4 shard_map.256
  3.1 128.0 %shard_map.257 = (bf16[2,8,32,768]{3,2,1,0:T(8,128)(2,1)}, bf16[4,2,2,16,768]{4,3,2,1,0:T(8,128)(2,1)}, bf16[4,2,2,48,1536]{4,3,2,1,0:T(8,128)(2,1)}, bf16[4,2,2...) custom-call(bf16[16,32,768]{2,1,0:T(8,128)(2,1)} %get-tuple-element., ...), custom_call_target="tpu_custom_call" | custom-call | tf_op jit(solution)/shard_map/pallas_call | solution.py:72
  131.1 66.9 %shard_map.258 = (bf16[768,2048]{1,0:T(8,128)(2,1)}, bf16[1024,768]{1,0:T(8,128)(2,1)}, bf16[768,1024]{1,0:T(8,128)(2,1)}, bf16[512,768]{1,0:T(8,128)(2,1)}, f32[512,768]{1,0:T(8,128)}, /*index=5*/f32[8,768]{1,0:T(8,128)}) custom-call(f32[512,768]{1,0:T(8,128)} %get-tuple-element.73.hidden, bf16[2,64,256]{2,1,0:T(8,128)(2,1)} %get-tuple-element.74.select, ...), custom_call_target="tpu_custom_call" | custom-call | tf_op jit(solution)/shard_map/pallas_call | solution.py:72
  198.0 124.9 %shard_map.259 = (bf16[8,2,32,768]{3,2,1,0:T(8,128)(2,1)}, f32[16,128]{1,0:T(8,128)}, f32[24,2048]{1,0:T(8,128)}, f32[32,768]{1,0:T(8,128)}, f32[24,768]{1,0:T(8...) custom-call(f32[512,768]{1,0:T(8,128)} %get-tuple-element.84.refs_0_, ...), custom_call_target="tpu_custom_call" | custom-call | tf_op jit(solution)/shard_map/pallas_call | solution.py:72
  323.0 0.0 copy-start
  323.0 0.0 copy-start.1
  323.0 3.6 %shard_map.260 = (f32[16,32,768]{2,1,0:T(8,128)}, f32[24,8192]{1,0:T(8,128)}, f32[24,2048]{1,0:T(8,128)}, f32[32,768]{1,0:T(8,128)}, f32[24,768]{1,0:T(8,128)}, ...) custom-call(s32[16]{0:T(128)} %deal_ref.3, bf16[16,32,768]{2,1,0:T(8,128)(2,1)} %bitcast.41, ...), custom_call_target="tpu_custom_call" | custom-call | tf_op jit(solution)/shard_map/pallas_call | solution.py:184
  326.6 0.0 copy-done
  326.6 0.6 dynamic_slice.6
  327.2 0.6 dynamic_slice.7
  327.8 0.5 slice.9
  328.3 0.0 copy-done.1
  328.3 0.6 reduce_sum.9
  (1 shorter events, 0.0 us)
Async XLA Ops:
  323.0 3.6 %copy-start = (f32[16,128]{1,0:T(8,128)S(1)}, f32[16,128]{1,0:T(8,128)}, u32[]{:S(2)}) copy-start(f32[16,128]{1,0:T(8,128)} %get-tuple-element.109) | copy-start | bytes 24580
  323.0 5.3 %copy-start.1 = (s32[16]{0:T(128)S(1)}, s32[16]{0:T(128)}, u32[]{:S(2)}) copy-start(s32[16]{0:T(128)} %param.19) | copy-start | bytes 196

commit v7 on v6

--- a/solution.py
+++ b/solution.py
@@ -215,10 +215,10 @@
 
 
 class Gather:
-    def __init__(self, dp, xin, ws, hin, hdn, xo, wos, hin_o, hdn_o, sems, halves=None):
+    def __init__(self, dp, xin, ws, hin, xo, wos, hin_o, sems, halves=None):
         self.dp, self.nz = dp, dp // 2
-        self.xin, self.ws, self.hin, self.hdn = xin, ws, hin, hdn
-        self.xo, self.wos, self.hin_o, self.hdn_o = xo, wos, hin_o, hdn_o
+        self.xin, self.ws, self.hin = xin, ws, hin
+        self.xo, self.wos, self.hin_o = xo, wos, hin_o
         self.loc, self.xs, self.xr, self.zs, self.zr = sems[:5]
         self.ps, self.pr, self.cs, self.cr, self.hs, self.hr = sems[5:]
         self.hi, self.lo, self.x, self.c = place()
@@ -334,7 +334,6 @@
         spot = self.hin_o.at[hi, self.home]
         self.h_own = [
             keep(self.hin.at[self.home], spot, self.loc.at[nw + 1]),
-            keep(self.hdn, self.hdn_o.at[hi], self.loc.at[nw + 2]),
         ]
         self.h_near = [
             send(
@@ -354,9 +353,6 @@
         self.h_far = []
         for k, to in enumerate(self.z_to):
             self.h_far.append(send(part, part, self.hs.at[1, k], self.hr.at[1, k], to))
-            self.h_far.append(
-                send(self.hdn, self.hdn_o.at[self.hi], self.hs.at[2, k], self.hr.at[2, k], to)
-            )
 
     def heavy_ready(self):
         for copy in self.h_far:
@@ -366,7 +362,7 @@
 def gather_sems(dp, nw):
     nz, most = dp // 2, max(7, dp // 2)
     return [
-        DMA((nw + 3,)),
+        DMA((nw + 2,)),
         DMA((dp,)),
         DMA((dp,)),
         DMA((nw, nz)),
@@ -375,16 +371,14 @@
         DMA((nw, 4)),
         DMA((nw, 4)),
         DMA((nw, 4)),
-        DMA((3, most)),
-        DMA((3, most)),
+        DMA((2, most)),
+        DMA((2, most)),
     ]
 
 
 def gather_kernel(dp, nw, *refs):
-    ins, outs, sems = refs[: 3 + nw], refs[3 + nw : 6 + 2 * nw], refs[6 + 2 * nw :]
-    g = Gather(
-        dp, ins[0], ins[1:-2], ins[-2], ins[-1], outs[0], outs[1:-2], outs[-2], outs[-1], sems
-    )
+    ins, outs, sems = refs[: 2 + nw], refs[2 + nw : 4 + 2 * nw], refs[4 + 2 * nw :]
+    g = Gather(dp, ins[0], ins[1:-1], ins[-1], outs[0], outs[1:-1], outs[-1], sems)
     g.meet()
     g.rows()
     for w in range(nw):
@@ -407,7 +401,7 @@
     g.heavy_ready()
 
 
-def gather_shapes(dp, xin, weights, hin, hdn, paired):
+def gather_shapes(dp, xin, weights, hin, paired):
     nz = dp // 2
     seqs, rows, _ = xin.shape
     shapes = [jax.ShapeDtypeStruct((seqs // dp, dp, rows, D), BF)]
@@ -416,18 +410,17 @@
     else:
         shapes += [jax.ShapeDtypeStruct((nz, 2, 2, 2) + w.shape, BF) for w in weights]
     shapes.append(jax.ShapeDtypeStruct((nz,) + hin.shape, BF))
-    shapes.append(jax.ShapeDtypeStruct((nz,) + hdn.shape, BF))
     return shapes
 
 
-def gather_all(dp, xin, weights, hin, hdn):
+def gather_all(dp, xin, weights, hin):
     nw = len(weights)
     return call(
         functools.partial(gather_kernel, dp, nw),
-        gather_shapes(dp, xin, weights, hin, hdn, False),
-        [xin, *weights, hin, hdn],
-        [ANY] * (3 + nw),
-        [ANY] * (3 + nw),
+        gather_shapes(dp, xin, weights, hin, False),
+        [xin, *weights, hin],
+        [ANY] * (2 + nw),
+        [ANY] * (2 + nw),
         gather_sems(dp, nw),
         1,
     )
@@ -535,6 +528,7 @@
 
 
 def ffn_kernel(
+    nz,
     hidden,
     select,
     select_t,
@@ -546,13 +540,16 @@
     w_in,
     w_dn,
     w_hin,
-    w_hdn,
+    hdn,
     g_in,
     g_dn,
     g_hin,
-    g_hdn,
+    hdn_o,
     d_hidden,
     stats,
+    w_line,
+    g_line,
+    g_in_line,
     hn,
     every,
     d_every,
@@ -563,8 +560,6 @@
     part,
     near,
     far,
-    near2,
-    far2,
     out,
     dl,
     dup_l,
@@ -578,6 +573,9 @@
     qr,
     es,
     er,
+    zs,
+    zr,
+    own,
 ):
     hi, lo, x, c = place()
     quad = quad_peers()
@@ -587,44 +585,55 @@
     tokens = hidden.shape[0]
     group, cap, width = select.shape
     fl = z.shape[1]
-    fh = zh.shape[2]
-    rows_h = part.shape[1] * part.shape[2]
-    meet([at(hi, l2, x2, c) for l2, x2 in quad] + [partner])
-
-    def spread(buffer, i):
-        spot = buffer.at[c, home]
+    fh = zh.shape[3]
+    block = 4 * cap
+    z_index = [lax.rem(hi + k, nz) for k in range(1, nz)]
+    z_to = [at(k, lo, x, c) for k in z_index]
+    meet([at(hi, l2, x2, c) for l2, x2 in quad] + [partner] + z_to)
+    hdn_own = keep(hdn, w_line.at[hi], own)
+    hdn_far = [send(hdn, w_line.at[hi], zs.at[0, k], zr.at[0, k], to) for k, to in enumerate(z_to)]
+    w_hdn = w_line.reshape(-1, D)
+
+    def span(s):
+        return slice(s * width, (s + 1) * width)
+
+    def slots(s):
+        return slice(s * cap, (s + 1) * cap)
+
+    def spread(buffer, s, i):
+        spot = buffer.at[s, c, home]
         there = [
             send(spot, spot, ps.at[i, k], pr.at[i, k], at(hi, l2, x2, c))
             for k, (l2, x2) in enumerate(quad)
         ]
         return there, [send(spot, spot, cs.at[i, 3], cr.at[i, 3], partner)]
 
-    def relay(buffer, i, there, back):
+    def relay(buffer, s, i, there, back):
         for k, q in enumerate(spots):
             there[k].wait()
-            other = buffer.at[c, q]
+            other = buffer.at[s, c, q]
             back.append(send(other, other, cs.at[i, k], cr.at[i, k], partner))
 
-    def fold(near_ref, far_ref, i, copy):
+    def fold(s, i, copy):
         copy.wait()
         there = []
         for k, q in enumerate(spots):
-            near_ref[q] = (near_ref[q].astype(F32) + part[c, q].astype(F32)).astype(BF)
+            near[i, q] = (near[i, q].astype(F32) + part[s, c, q].astype(F32)).astype(BF)
             l2, x2 = quad[k]
             there.append(
-                send(near_ref.at[q], far_ref.at[k], qs.at[i, k], qr.at[i, k], at(hi, l2, x2, c))
+                send(near.at[i, q], far.at[i, k], qs.at[i, k], qr.at[i, k], at(hi, l2, x2, c))
             )
         return there
 
-    def folded(near_ref, far_ref, there):
+    def folded(s, i, there):
         for copy in there:
             copy.wait()
         return (
-            near_ref[home].astype(F32)
-            + part[c, home].astype(F32)
-            + far_ref[0].astype(F32)
-            + far_ref[1].astype(F32)
-            + far_ref[2].astype(F32)
+            near[i, home].astype(F32)
+            + part[s, c, home].astype(F32)
+            + far[i, 0].astype(F32)
+            + far[i, 1].astype(F32)
+            + far[i, 2].astype(F32)
         )
 
     def norm(r):
@@ -632,199 +641,199 @@
         inv = lax.rsqrt(jnp.mean(h * h, axis=-1, keepdims=True) + EPSILON)
         hn[r, :] = (h * inv * gain[1:2, :]).astype(BF)
 
+    seqs = range(group)
+    moves = {}
     tiles(tokens, 128, norm)
-    for s in range(group):
-        every[c, home, s * cap : (s + 1) * cap, :] = dot(
-            select[s], hn[s * width : (s + 1) * width, :]
-        ).astype(BF)
-    there, back = spread(every, 0)
+    for s in seqs:
+        every[s, c, home] = dot(select[s], hn[span(s), :]).astype(BF)
+        moves[s] = spread(every, s, s)
 
     def light_up(r):
         up_l[r, :] = dot(hn[r, :], w_in[...])
         z[r, :] = (gelu_value(up_l[r, :fl]) * up_l[r, fl:]).astype(BF)
 
-    tiles(tokens, 256, light_up)
+    tiles(tokens, width, light_up)
+    for s in seqs:
+        relay(every, s, s, *moves[s])
+
+    def light_down(r):
+        out[r, :] = hidden[r, :] + dot(z[r, :], w_dn[...])
+
+    tiles(tokens, width, light_down)
 
     def light_slopes(r):
         value, slope = gelu_parts(up_l[r, :fl])
         up_l[r, :fl] = up_l[r, fl:] * slope
         up_l[r, fl:] = value
 
+    def heavy(s, e):
+        up_h[s, e] = dot(every[s, e].reshape(block, D), w_hin[...])
+        zh[s, e] = (gelu_value(up_h[s, e, :, :fh]) * up_h[s, e, :, fh:]).astype(BF)
+        part[s, e] = dot(zh[s, e], w_hdn[...]).astype(BF).reshape(4, cap, D)
+
+    hdn_own.wait()
+    for copy in hdn_far:
+        copy.wait()
+    sums = {}
+    for s in seqs:
+        for copy in moves[s][1]:
+            copy.wait()
+        heavy(s, 1 - c)
+        first = send(part.at[s, 1 - c], near.at[s], es.at[s], er.at[s], partner)
+        heavy(s, c)
+        sums[s] = fold(s, s, first)
     tiles(tokens, 64, light_slopes)
-    relay(every, 0, there, back)
-
-    def light_down(r):
-        out[r, :] = hidden[r, :] + dot(z[r, :], w_dn[...])
-
-    tiles(tokens, 256, light_down)
-    for copy in back:
-        copy.wait()
-
-    def heavy(e):
-        def up(i, carry):
-            a = every[e, pl.ds(2 * i, 2)].reshape(2 * group * cap, D)
-            r = pl.ds(pl.multiple_of(i * 256, 256), 256)
-            up_h[e, r, :] = dot(a, w_hin[...])
-            zh[e, r, :] = (gelu_value(up_h[e, r, :fh]) * up_h[e, r, fh:]).astype(BF)
-            v = dot(zh[e, r, :], w_hdn[...]).astype(BF)
-            part[e, pl.ds(2 * i, 2)] = v.reshape(2, group * cap, D)
-            return carry
-
-        lax.fori_loop(0, 2, up, 0)
-
-    heavy(1 - c)
-    first = send(part.at[1 - c], near, es.at[0], er.at[0], partner)
-    heavy(c)
-    there = fold(near, far, 0, first)
-    for e in (0, 1):
-
-        def heavy_slopes(r, e=e):
-            value, slope = gelu_parts(up_h[e, r, :fh])
-            up_h[e, r, :fh] = up_h[e, r, fh:] * slope
-            up_h[e, r, fh:] = value
-
-        tiles(rows_h, 128, heavy_slopes)
-    hf = folded(near, far, there) * score[...]
-    hf_high, hf_low = halves(hf)
-    for s in range(group):
-        r = slice(s * width, (s + 1) * width)
-        q = slice(s * cap, (s + 1) * cap)
-        out[r, :] += dot(select_t[s], hf_high[q]) + dot(select_t[s], hf_low[q])
+    for s in seqs:
+        for e in (0, 1):
+
+            def heavy_slopes(r, s=s, e=e):
+                value, slope = gelu_parts(up_h[s, e, r, :fh])
+                up_h[s, e, r, :fh] = up_h[s, e, r, fh:] * slope
+                up_h[s, e, r, fh:] = value
+
+            if s == 0:
+                tiles(block, 128, heavy_slopes)
     stats[...] = jnp.zeros(stats.shape, F32)
 
-    def misfit(r):
-        m = out[r, :] - teach[r, :].astype(F32)
+    def light_back(r):
+        dz = dot_back(dl[r, :], w_dn[...])
+        dup_l[r, :fl] = (dz * up_l[r, :fl]).astype(BF)
+        dup_l[r, fl:] = (dz * up_l[r, fl:]).astype(BF)
+
+    for s in seqs:
+        r = span(s)
+        high, low = halves(folded(s, s, sums[s]) * score[slots(s), :])
+        total = out[r, :] + (dot(select_t[s], high) + dot(select_t[s], low))
+        m = total - teach[r, :].astype(F32)
         stats[1:2, :] += jnp.sum(mask[r, :] * m * m, axis=0, keepdims=True)
         d = scale[r, :] * m
         out[r, :] = d
         dl[r, :] = d.astype(BF)
-
-    tiles(tokens, 128, misfit)
-    for s in range(group):
-        high, low = halves(out[s * width : (s + 1) * width, :])
+        high, low = halves(d)
         picked = dot(select[s], high) + dot(select[s], low)
-        q = slice(s * cap, (s + 1) * cap)
-        d_every[c, home, q, :] = (picked * score[q, :]).astype(BF)
-    there, back = spread(d_every, 1)
-
-    def light_back(r):
-        dz = dot_back(dl[r, :], w_dn[...])
-        dup_l[r, :fl] = (dz * up_l[r, :fl]).astype(BF)
-        dup_l[r, fl:] = (dz * up_l[r, fl:]).astype(BF)
-
-    tiles(tokens, 256, light_back)
-    def light_in_back(r):
-        dhn[r, :] = dot_back(dup_l[r, :], w_in[...])
-
-    tiles(tokens, 256, light_in_back)
-    relay(d_every, 1, there, back)
+        d_every[s, c, home] = (picked * score[slots(s), :]).astype(BF)
+        moves[s] = spread(d_every, s, group + s)
+        light_back(r)
+        if s > 0:
+            for e in (0, 1):
+
+                def more_slopes(r, s=s, e=e):
+                    value, slope = gelu_parts(up_h[s, e, r, :fh])
+                    up_h[s, e, r, :fh] = up_h[s, e, r, fh:] * slope
+                    up_h[s, e, r, fh:] = value
+
+                tiles(block, 128, more_slopes)
+
+    def heavy_back(s, e):
+        dz = dot_back(d_every[s, e].reshape(block, D), w_hdn[...])
+        dup_h[s, e, :, :fh] = (dz * up_h[s, e, :, :fh]).astype(BF)
+        dup_h[s, e, :, fh:] = (dz * up_h[s, e, :, fh:]).astype(BF)
+        v = dot_back(dup_h[s, e], w_hin[...]).astype(BF)
+        part[s, e] = v.reshape(4, cap, D)
+
+    for s in seqs:
+        relay(d_every, s, group + s, *moves[s])
+        dhn[span(s), :] = dot_back(dup_l[span(s), :], w_in[...])
+    for s in seqs:
+        for copy in moves[s][1]:
+            copy.wait()
+        heavy_back(s, 1 - c)
+        i = group + s
+        second = send(part.at[s, 1 - c], near.at[i], es.at[i], er.at[i], partner)
+        heavy_back(s, c)
+        sums[s] = fold(s, i, second)
+    count = group * 2 * block
+    d_rows = d_every[...].reshape(count, D)
+    g_line[...] = dot_grad(zh[...].reshape(count, fh), d_rows).astype(BF)
+    g_view = g_line.reshape(nz, -1, D)
+    hdn_back = [
+        send(g_view.at[k], g_in_line.at[n], zs.at[1, n], zr.at[1, n], z_to[n])
+        for n, k in enumerate(z_index)
+    ]
 
     def light_grad(j):
         g_dn[j, :] = dot_grad(z[:, j], dl[...]).astype(BF)
 
     tiles(fl, 512, light_grad)
-    for copy in back:
-        copy.wait()
-
-    def heavy_back(e):
-        def run(i, carry):
-            d = d_every[e, pl.ds(2 * i, 2)].reshape(2 * group * cap, D)
-            r = pl.ds(pl.multiple_of(i * 256, 256), 256)
-            dz = dot_back(d, w_hdn[...])
-            dup_h[e, r, :fh] = (dz * up_h[e, r, :fh]).astype(BF)
-            dup_h[e, r, fh:] = (dz * up_h[e, r, fh:]).astype(BF)
-            v = dot_back(dup_h[e, r, :], w_hin[...]).astype(BF)
-            part[e, pl.ds(2 * i, 2)] = v.reshape(2, group * cap, D)
-            return carry
-
-        lax.fori_loop(0, 2, run, 0)
-
-    heavy_back(1 - c)
-    second = send(part.at[1 - c], near2, es.at[1], er.at[1], partner)
-    heavy_back(c)
-    there = fold(near2, far2, 1, second)
 
     def light_in_grad(j):
         g_in[:, j] = dot_grad(hn[...], dup_l[:, j]).astype(BF)
 
     tiles(2 * fl, 1024, light_in_grad)
-
-    every_rows = every[...].reshape(2 * rows_h, D)
+    every_rows = every[...].reshape(count, D)
 
     def heavy_grad(j):
-        g_hin[:, j] = dot_grad(every_rows, dup_h[:, :, j].reshape(2 * rows_h, 512)).astype(BF)
+        g_hin[:, j] = dot_grad(every_rows, dup_h[:, :, :, j].reshape(count, 512)).astype(BF)
 
     tiles(2 * fh, 512, heavy_grad)
-    d_rows = d_every[...].reshape(2 * rows_h, D)
-
-    def heavy_down_grad(j):
-        g_hdn[j, :] = dot_grad(zh[:, :, j].reshape(2 * rows_h, 512), d_rows).astype(BF)
-
-    tiles(fh, 512, heavy_down_grad)
-    d_high, d_low = halves(folded(near2, far2, there))
-    for s in range(group):
-        r = slice(s * width, (s + 1) * width)
-        q = slice(s * cap, (s + 1) * cap)
-        dhn[r, :] += dot(select_t[s], d_high[q]) + dot(select_t[s], d_low[q])
-
-    def norm_back(r):
+    for s in seqs:
+        r = span(s)
+        high, low = halves(folded(s, group + s, sums[s]))
+        d = dhn[r, :] + (dot(select_t[s], high) + dot(select_t[s], low))
         h = hidden[r, :]
         inv = lax.rsqrt(jnp.mean(h * h, axis=-1, keepdims=True) + EPSILON)
-        d = dhn[r, :]
         dh = d * h
         stats[0:1, :] += jnp.sum(dh * inv, axis=0, keepdims=True)
         mean = jnp.mean(gain[1:2, :] * dh, axis=-1, keepdims=True)
         d_hidden[r, :] = out[r, :] + inv * gain[1:2, :] * d - h * (inv * inv * inv * mean)
-
-    tiles(tokens, 128, norm_back)
-
-
-def feed_forward(hidden, select, select_t, score, gain, teach, mask, scale, w_in, w_dn, w_hin, w_hdn):
+    for copy in hdn_back:
+        copy.wait()
+    value = g_view[hi].astype(F32)
+    for n in range(nz - 1):
+        value += g_in_line[n].astype(F32)
+    hdn_o[...] = value
+
+
+def feed_forward(nz, hidden, select, select_t, score, gain, teach, mask, scale, w_in, w_dn, w_hin, hdn):
     tokens = hidden.shape[0]
     group, cap, _ = select.shape
-    rows = group * cap
-    fl, fh = w_dn.shape[0], w_hdn.shape[0]
-    block = (2, 4, rows, D)
-    operands = [hidden, select, select_t, score, gain, teach, mask, scale, w_in, w_dn, w_hin, w_hdn]
+    fl, fh = w_dn.shape[0], w_hin.shape[1] // 2
+    block = (group, 2, 4, cap, D)
+    line = (nz,) + hdn.shape
+    operands = [hidden, select, select_t, score, gain, teach, mask, scale, w_in, w_dn, w_hin, hdn]
     return call(
-        ffn_kernel,
+        functools.partial(ffn_kernel, nz),
         [
             jax.ShapeDtypeStruct((D, 2 * fl), BF),
             jax.ShapeDtypeStruct((fl, D), BF),
             jax.ShapeDtypeStruct((D, 2 * fh), BF),
-            jax.ShapeDtypeStruct((fh, D), BF),
+            jax.ShapeDtypeStruct(hdn.shape, F32),
             jax.ShapeDtypeStruct((tokens, D), F32),
             jax.ShapeDtypeStruct((8, D), F32),
         ],
         operands,
-        [VM] * len(operands),
+        [VM] * (len(operands) - 1) + [ANY],
         [VM] * 6,
         [
+            pltpu.VMEM(line, BF),
+            pltpu.VMEM((fh, D), BF),
+            pltpu.VMEM((nz - 1,) + hdn.shape, BF),
             pltpu.VMEM((tokens, D), BF),
             pltpu.VMEM(block, BF),
             pltpu.VMEM(block, BF),
             pltpu.VMEM((tokens, 2 * fl), F32),
             pltpu.VMEM((tokens, fl), BF),
-            pltpu.VMEM((2, 4 * rows, 2 * fh), F32),
-            pltpu.VMEM((2, 4 * rows, fh), BF),
+            pltpu.VMEM((group, 2, 4 * cap, 2 * fh), F32),
+            pltpu.VMEM((group, 2, 4 * cap, fh), BF),
             pltpu.VMEM(block, BF),
-            pltpu.VMEM(block[1:], BF),
-            pltpu.VMEM((3, rows, D), BF),
-            pltpu.VMEM(block[1:], BF),
-            pltpu.VMEM((3, rows, D), BF),
+            pltpu.VMEM((2 * group, 4, cap, D), BF),
+            pltpu.VMEM((2 * group, 3, cap, D), BF),
             pltpu.VMEM((tokens, D), F32),
             pltpu.VMEM((tokens, D), BF),
             pltpu.VMEM((tokens, 2 * fl), BF),
-            pltpu.VMEM((2, 4 * rows, 2 * fh), BF),
+            pltpu.VMEM((group, 2, 4 * cap, 2 * fh), BF),
             pltpu.VMEM((tokens, D), F32),
-            DMA((2, 3)),
-            DMA((2, 3)),
-            DMA((2, 4)),
-            DMA((2, 4)),
-            DMA((2, 3)),
-            DMA((2, 3)),
-            DMA((2,)),
-            DMA((2,)),
+            DMA((2 * group, 3)),
+            DMA((2 * group, 3)),
+            DMA((2 * group, 4)),
+            DMA((2 * group, 4)),
+            DMA((2 * group, 3)),
+            DMA((2 * group, 3)),
+            DMA((2 * group,)),
+            DMA((2 * group,)),
+            DMA((2, nz)),
+            DMA((2, nz)),
+            DMA,
         ],
         5,
     )
@@ -1144,15 +1153,15 @@
 
 
 def gather_attend_kernel(dp, nw, *refs):
-    n_in, n_out = 8 + nw, 3 + nw + 21
+    n_in, n_out = 7 + nw, 2 + nw + 21
     ins, outs, rest = refs[:n_in], refs[n_in : n_in + n_out], refs[n_in + n_out :]
-    xin, ws, hin, hdn = ins[0], ins[1 : 1 + nw], ins[1 + nw], ins[2 + nw]
-    integers = ins[3 + nw :]
-    xo, wos, hin_o, hdn_o = outs[0], outs[1 : 1 + nw], outs[1 + nw], outs[2 + nw]
-    gain, tables, saved = outs[3 + nw], outs[4 + nw : 13 + nw], outs[13 + nw :]
+    xin, ws, hin = ins[0], ins[1 : 1 + nw], ins[1 + nw]
+    integers = ins[2 + nw :]
+    xo, wos, hin_o = outs[0], outs[1 : 1 + nw], outs[1 + nw]
+    gain, tables, saved = outs[2 + nw], outs[3 + nw : 12 + nw], outs[12 + nw :]
     parts, rest = rest[: 3 * nw + 3], rest[3 * nw + 3 :]
     halves = (parts[:nw], parts[nw : 2 * nw], parts[2 * nw : 3 * nw], parts[3 * nw :])
-    g = Gather(dp, xin, ws, hin, hdn, xo, wos, hin_o, hdn_o, rest[:11], halves)
+    g = Gather(dp, xin, ws, hin, xo, wos, hin_o, rest[:11], halves)
     g.meet()
     for w in range(nw):
         g.swap(w)
@@ -1228,9 +1237,9 @@
     g.heavy_ready()
 
 
-def gather_attend(dp, xin, weights, hin, hdn, integers):
+def gather_attend(dp, xin, weights, hin, integers):
     nw = len(weights)
-    shapes = gather_shapes(dp, xin, weights, hin, hdn, True)
+    shapes = gather_shapes(dp, xin, weights, hin, True)
     group, width = shapes[0].shape[0], dp * xin.shape[1]
     tables = route_shapes(group, width, group * width)
     shapes.append(jax.ShapeDtypeStruct((8, D), F32))
@@ -1239,9 +1248,9 @@
     return call(
         functools.partial(gather_attend_kernel, dp, nw),
         shapes,
-        [xin, *weights, hin, hdn, *integers],
-        [ANY] * (3 + nw) + [VM] * 5,
-        [VM] * 6 + [ANY] * 4 + [VM] * 21,
+        [xin, *weights, hin, *integers],
+        [ANY] * (2 + nw) + [VM] * 5,
+        [VM] * 6 + [ANY] * 3 + [VM] * 21,
         [pltpu.VMEM((w.shape[0], w.shape[1] // 2), BF) for w in weights] * 2
         + [pltpu.VMEM((2 * w.shape[0], w.shape[1] // 2), BF) for w in weights]
         + [DMA((nw,))] * 3
@@ -1481,13 +1490,13 @@
 
 def scatter_kernel(dp, nw, *refs):
     nz = dp // 2
-    dx, stats, gs, hin, hdn = refs[0], refs[1], refs[2 : 2 + nw], refs[2 + nw], refs[3 + nw]
-    outs = refs[4 + nw :]
-    dxo, total, gos, hin_o, hdn_o = outs[0], outs[1], outs[2 : 2 + nw], outs[2 + nw], outs[3 + nw]
-    scr = outs[4 + nw :]
+    dx, stats, gs, hin = refs[0], refs[1], refs[2 : 2 + nw], refs[2 + nw]
+    outs = refs[3 + nw :]
+    dxo, total, gos, hin_o = outs[0], outs[1], outs[2 : 2 + nw], outs[2 + nw]
+    scr = outs[3 + nw :]
     nears, fars, sums, ends = (scr[i * nw : (i + 1) * nw] for i in range(4))
-    hin_r, hin_s, hdn_r, sc, sp, sz, acc, acc2 = scr[4 * nw : 4 * nw + 8]
-    own, xs, xr, cs, cr, ps, pr, zs, zr, hs, hr, ts, tr = scr[4 * nw + 8 :]
+    hin_r, hin_s, sc, sp, sz, acc, acc2 = scr[4 * nw : 4 * nw + 7]
+    own, xs, xr, cs, cr, ps, pr, zs, zr, hs, hr, ts, tr = scr[4 * nw + 7 :]
     hi, lo, x, c = place()
     d = hi * 2 + lo
     f = x * 2 + c
@@ -1517,7 +1526,6 @@
     h_sends = []
     for k, z in enumerate(z_index):
         h_sends.append(send(hin.at[z], hin_r.at[k], hs.at[1, k], hr.at[1, k], z_peers[k]))
-        h_sends.append(send(hdn.at[z], hdn_r.at[k], hs.at[2, k], hr.at[2, k], z_peers[k]))
     p_sends, z_sends = [], []
     t_c.wait()
     acc[...] = stats[...] + sc[...]
@@ -1602,9 +1610,6 @@
         )
         for k, (l2, x2, c2) in enumerate(flat8)
     ]
-    hdn_o[...] = hdn[hi].astype(F32)
-    for k in range(nz - 1):
-        hdn_o[...] += hdn_r[k].astype(F32)
     for w in range(max(nw - 2, 0), nw):
         add_plane(w)
     for copy in t_z:
@@ -1619,7 +1624,7 @@
         copy.wait()
 
 
-def scatter_all(dp, dx, stats, grads, hin, hdn):
+def scatter_all(dp, dx, stats, grads, hin):
     nz = dp // 2
     nw = len(grads)
     group, _, rows, _ = dx.shape
@@ -1632,7 +1637,6 @@
     scratch += [
         pltpu.VMEM((nz - 1,) + hin.shape[1:], BF),
         pltpu.VMEM(hin.shape[1:], BF),
-        pltpu.VMEM((nz - 1,) + hdn.shape[1:], BF),
         pltpu.VMEM(stats.shape, F32),
         pltpu.VMEM((3,) + stats.shape, F32),
         pltpu.VMEM((nz - 1,) + stats.shape, F32),
@@ -1655,13 +1659,12 @@
     shapes = [jax.ShapeDtypeStruct((dp, group, rows, D), BF), jax.ShapeDtypeStruct(stats.shape, F32)]
     shapes += [jax.ShapeDtypeStruct(t, F32) for t in tiles]
     shapes.append(jax.ShapeDtypeStruct(hin.shape[1:], BF))
-    shapes.append(jax.ShapeDtypeStruct(hdn.shape[1:], F32))
     return call(
         functools.partial(scatter_kernel, dp, nw),
         shapes,
-        [dx, stats, *grads, hin, hdn],
-        [ANY] + [VM] * (3 + nw),
-        [ANY] + [VM] * (3 + nw),
+        [dx, stats, *grads, hin],
+        [ANY] + [VM] * (2 + nw),
+        [ANY] + [VM] * (2 + nw),
         scratch,
         4,
     )
@@ -1776,16 +1779,16 @@
 def back_scatter_kernel(dp, shards, *refs):
     nz, nw = dp // 2, len(shards)
     n_ops = 7 + 4 + 10
-    ops, (g_lin, g_ldn, hin, hdn, ffn_stats) = refs[:n_ops], refs[n_ops : n_ops + 5]
-    outs, rest = refs[n_ops + 5 : n_ops + 9 + nw], refs[n_ops + 9 + nw :]
-    dxo, total, gos, hin_o, hdn_o = outs[0], outs[1], outs[2 : 2 + nw], outs[2 + nw], outs[3 + nw]
+    ops, (g_lin, g_ldn, hin, ffn_stats) = refs[:n_ops], refs[n_ops : n_ops + 4]
+    outs, rest = refs[n_ops + 4 : n_ops + 7 + nw], refs[n_ops + 7 + nw :]
+    dxo, total, gos, hin_o = outs[0], outs[1], outs[2 : 2 + nw], outs[2 + nw]
     full, rest = rest[:4], rest[4:]
     own_lin, own_ldn, stats, rest = rest[0], rest[1], rest[2], rest[3:]
     back, rest = rest[:17], rest[17:]
     dx = back[5]
     near, one, two, end, fin = (rest[k * nw : (k + 1) * nw] for k in range(5))
-    hin_own, hdn_own, hin_r, hdn_r, acc, sc, sp, sz, acc2 = rest[5 * nw : 5 * nw + 9]
-    own, xs, xr, cs, cr, ps, pr, zs, zr, hs, hr, ts, tr, *fsem = rest[5 * nw + 9 :]
+    hin_own, hin_r, acc, sc, sp, sz, acc2 = rest[5 * nw : 5 * nw + 7]
+    own, xs, xr, cs, cr, ps, pr, zs, zr, hs, hr, ts, tr, *fsem = rest[5 * nw + 7 :]
     hi, lo, x, c = place()
     d = hi * 2 + lo
     plane = (lo * 2 + x) * 2 + c
@@ -1803,14 +1806,12 @@
     h_sends = []
     for k, z in enumerate(z_index):
         h_sends.append(send(hin.at[z], hin_r.at[k], hs.at[1, k], hr.at[1, k], z_to[k]))
-        h_sends.append(send(hdn.at[z], hdn_r.at[k], hs.at[2, k], hr.at[2, k], z_to[k]))
     t.core(0)
     t.core(1)
     kept = [
         keep(g_lin.at[:, :, :, :, t.lanes(0, c)], own_lin, own.at[0]),
         keep(g_ldn.at[:, :, :, :, t.lanes(1, c)], own_ldn, own.at[1]),
         keep(hin.at[hi], hin_own, own.at[2]),
-        keep(hdn.at[hi], hdn_own, own.at[3]),
     ]
     late = []
 
@@ -1902,10 +1903,6 @@
         )
         for k, q in enumerate(others)
     ]
-    value = hdn_own[...].astype(F32)
-    for k in range(nz - 1):
-        value += hdn_r[k].astype(F32)
-    hdn_o[...] = value
     t.cross(5)
     for copy in t_p:
         copy.wait()
@@ -1924,7 +1921,7 @@
         copy.wait()
 
 
-def back_scatter(dp, rows, d_hidden, x, gain, masks, weights, saved, ffn_grads, ffn_stats, shards, hin, hdn):
+def back_scatter(dp, rows, d_hidden, x, gain, masks, weights, saved, ffn_grads, ffn_stats, shards, hin):
     nz, nw = dp // 2, len(shards)
     tokens = x.shape[0]
     group = masks[0].shape[0]
@@ -1933,11 +1930,10 @@
     paired = [
         g.reshape(nz, 2, 2, 2 * s[0], s[1]) for g, s in zip(ffn_grads, shards)
     ]
-    operands = [d_hidden, x, gain, *masks, *weights, *saved, *paired, hin, hdn, ffn_stats]
+    operands = [d_hidden, x, gain, *masks, *weights, *saved, *paired, hin, ffn_stats]
     shapes = [jax.ShapeDtypeStruct((dp, group, rows, D), BF), jax.ShapeDtypeStruct(stat_shape, F32)]
     shapes += [jax.ShapeDtypeStruct(s, F32) for s in shards]
     shapes.append(jax.ShapeDtypeStruct(hin.shape[1:], BF))
-    shapes.append(jax.ShapeDtypeStruct(hdn.shape[1:], F32))
     scratch = [pltpu.VMEM((s[0] * 8 * nz, s[1]), BF) for s in shards[2:]]
     split = [(2 * s[0], s[1] // 2) for s in shards]
     scratch += [pltpu.VMEM((nz, 2, 2) + s, BF) for s in split[:2]]
@@ -1950,9 +1946,7 @@
     scratch += [pltpu.VMEM(s, F32) for s in split]
     scratch += [
         pltpu.VMEM(hin.shape[1:], BF),
-        pltpu.VMEM(hdn.shape[1:], BF),
         pltpu.VMEM((nz - 1,) + hin.shape[1:], BF),
-        pltpu.VMEM((nz - 1,) + hdn.shape[1:], BF),
         pltpu.VMEM(stat_shape, F32),
         pltpu.VMEM(stat_shape, F32),
         pltpu.VMEM((3,) + stat_shape, F32),
@@ -1979,7 +1973,7 @@
         functools.partial(back_scatter_kernel, dp, shards),
         shapes,
         operands,
-        [VM] * (len(operands) - 5) + [ANY] * 4 + [VM],
+        [VM] * (len(operands) - 4) + [ANY] * 3 + [VM],
         [VM] * len(shapes),
         scratch,
         6,
@@ -2043,7 +2037,7 @@
     if merged:
         xin, hin_src, gains = prepare(dealing, layer_input[:, 0], heavy_in, gain_attn, gain_ffn)
         integers = (dealing.reshape(1, -1), lengths.reshape(1, -1), attn_routes, ffn_routes, ffn_scores)
-        got = gather_attend(dp, xin, [gains, *matrices], hin_src, heavy_down, integers)
+        got = gather_attend(dp, xin, [gains, *matrices], hin_src, integers)
     else:
         xin = deal_rows(dealing, layer_input[:, 0])
         owned = jnp.arange(D)[None, :] // gain_len == mine
@@ -2058,16 +2052,15 @@
         )
         if hin_rows % 8:
             hin_src = hin_src.reshape(8, -1, 128)
-        got = gather_all(dp, xin, [gains] + [packed(m) for m in matrices], hin_src, heavy_down)
+        got = gather_all(dp, xin, [gains] + [packed(m) for m in matrices], hin_src)
     flat_x = got[0].reshape(-1, D)
     w_lqkv, w_hqkv, w_lout, w_hout, w_lin, w_ldown = (
         unpacked(full, *m.shape) for full, m in zip(got[2:8], matrices)
     )
     w_hin = unpacked(got[8], hin_rows, 2 * nz * hidden_units)
-    w_hdown = got[9].reshape(-1, D)
     attn_weights = (w_lqkv, w_hqkv, w_lout, w_hout)
     if merged:
-        gain, tables, (hidden, *saved) = got[10], got[11:20], got[20:]
+        gain, tables, (hidden, *saved) = got[9], got[10:19], got[19:]
         masks, ffn_masks = tables[:4], tables[4:]
     else:
         gain = jnp.sum(got[1].reshape(n, 8, D).astype(F32), axis=0)
@@ -2076,7 +2069,8 @@
         )
         hidden, *saved = attend(flat_x, gain, *masks, *attn_weights)
     f_select, f_select_t, slot_score, weight_mask, weight_scale = ffn_masks
-    grad_lin, grad_ldown, grad_hin, grad_hdown, d_hidden, ffn_stats = feed_forward(
+    grad_lin, grad_ldown, grad_hin, g_hdown, d_hidden, ffn_stats = feed_forward(
+        nz,
         hidden,
         f_select,
         f_select_t,
@@ -2088,12 +2082,11 @@
         w_lin,
         w_ldown,
         w_hin,
-        w_hdown,
+        heavy_down,
     )
     rows = tokens // dp
     shards = (light_in, light_down, heavy_out, light_out, heavy_qkv, light_qkv)
     hin_part = grad_hin.reshape((nz, 8) + hin_src.shape[1:])
-    hdn_part = grad_hdown.reshape(nz, -1, D)
     if merged:
         done = back_scatter(
             dp,
@@ -2108,7 +2101,6 @@
             ffn_stats,
             tuple(shard.shape for shard in shards),
             hin_part,
-            hdn_part,
         )
     else:
         grad_lqkv, grad_hqkv, grad_lout, grad_hout, d_inputs, attn_stats = attend_back(
@@ -2124,7 +2116,7 @@
         grads = (grad_lin, grad_ldown, grad_hout, grad_lout, grad_hqkv, grad_lqkv)
         sent = [packed_full(grad, shard.shape, nz) for grad, shard in zip(grads, shards)]
         done = scatter_all(
-            dp, d_inputs.reshape(group, dp, rows, D), stats, sent, hin_part, hdn_part
+            dp, d_inputs.reshape(group, dp, rows, D), stats, sent, hin_part
         )
     summed = done[1]
     loss_value = summed[12, 0] / (D * token_count)
@@ -2133,12 +2125,12 @@
     back_rows = done[0].reshape(seqs, rows, D)
     if merged:
         d_layer, g_hin, *owned = finish_all(
-            n, dealing, back_rows, done[8], [*done[2:8], done[9]], heavy_in.shape
+            n, dealing, back_rows, done[8], [*done[2:8], g_hdown], heavy_in.shape
         )
     else:
         d_layer = undeal_rows(dealing, back_rows)
         owned = [full.reshape(shard.shape) for full, shard in zip(done[2:8], shards)]
-        owned.append(done[9].reshape(heavy_down.shape))
+        owned.append(g_hdown)
         g_hin = (
             done[8]
             .astype(F32)

time: 332 us -> 333 us (level)
  no operation moved by 1% of the time
where the time goes in v7:
time: 333 us; the launch traced here: 329 us
  Pallas kernels  323 us (97%)
    pallas_call x3, Pallas kernels, call(): pl.pallas_call(kernel, out_shape=out_shape, in_specs=in_specs, out_specs=...  317 us

profile of v7, /device:TPU:0, one launch (start us, length us, event | category | flops | bytes accessed | tf_op | source)
XLA Modules:
  0.0 329.0 jit_solution(11067813809608465511)
XLA Ops:
  0.6 2.4 shard_map.256
  3.1 119.7 %shard_map.257 = (bf16[2,8,32,768]{3,2,1,0:T(8,128)(2,1)}, bf16[4,2,2,16,768]{4,3,2,1,0:T(8,128)(2,1)}, bf16[4,2,2,48,1536]{4,3,2,1,0:T(8,128)(2,1)}, bf16[4,2,2...) custom-call(bf16[16,32,768]{2,1,0:T(8,128)(2,1)} %get-tuple-element., ...), custom_call_target="tpu_custom_call" | custom-call | tf_op jit(solution)/shard_map/pallas_call | solution.py:72
  122.8 81.3 %shard_map.258 = (bf16[768,2048]{1,0:T(8,128)(2,1)}, bf16[1024,768]{1,0:T(8,128)(2,1)}, bf16[768,1024]{1,0:T(8,128)(2,1)}, f32[128,768]{1,0:T(8,128)}, f32[512,768]{1,0:T(8,128)}, /*index=5*/f32[8,768]{1,0:T(8,128)}) custom-call(f32[512,768]{1,0:T(8,128)} %get-tuple-element.71.hidden, bf16[2,64,256]{2,1,0:T(8,128)(2,1)} %get-tuple-element.72.select, ...), custom_call_target="tpu_custom_call" | custom-call | tf_op jit(solution)/shard_map/pallas_call | solution.py:72
  204.0 116.4 %shard_map.259 = (bf16[8,2,32,768]{3,2,1,0:T(8,128)(2,1)}, f32[16,128]{1,0:T(8,128)}, f32[24,2048]{1,0:T(8,128)}, f32[32,768]{1,0:T(8,128)}, f32[24,768]{1,0:T(8...) custom-call(f32[512,768]{1,0:T(8,128)} %get-tuple-element.81.refs_0_, ...), custom_call_target="tpu_custom_call" | custom-call | tf_op jit(solution)/shard_map/pallas_call | solution.py:72
  320.4 0.0 copy-start
  320.5 0.0 copy-start.1
  320.5 3.6 %shard_map.260 = (f32[16,32,768]{2,1,0:T(8,128)}, f32[24,8192]{1,0:T(8,128)}, f32[24,2048]{1,0:T(8,128)}, f32[32,768]{1,0:T(8,128)}, f32[24,768]{1,0:T(8,128)}, ...) custom-call(s32[16]{0:T(128)} %deal_ref.3, bf16[16,32,768]{2,1,0:T(8,128)(2,1)} %bitcast.37, ...), custom_call_target="tpu_custom_call" | custom-call | tf_op jit(solution)/shard_map/pallas_call | solution.py:184
  324.1 0.0 copy-done
  324.1 0.6 dynamic_slice.6
  324.7 0.6 dynamic_slice.7
  325.3 0.5 slice.9
  325.8 0.0 copy-done.1
  325.8 0.6 reduce_sum.9
  (1 shorter events, 0.0 us)
Async XLA Ops:
  320.4 3.6 %copy-start = (f32[16,128]{1,0:T(8,128)S(1)}, f32[16,128]{1,0:T(8,128)}, u32[]{:S(2)}) copy-start(f32[16,128]{1,0:T(8,128)} %get-tuple-element.105) | copy-start | bytes 24580
  320.5 5.3 %copy-start.1 = (s32[16]{0:T(128)S(1)}, s32[16]{0:T(128)}, u32[]{:S(2)}) copy-start(s32[16]{0:T(128)} %param.19) | copy-start | bytes 196

commit v8 on v7

--- a/solution.py
+++ b/solution.py
@@ -534,19 +534,27 @@
     select_t,
     score,
     gain,
-    teach,
+    teach_hbm,
     mask,
     scale,
+    w_in_hbm,
+    w_dn_hbm,
+    w_hin_hbm,
+    hdn,
+    g_in_hbm,
+    g_dn_hbm,
+    g_hin_hbm,
+    hdn_o,
+    d_hidden,
+    stats,
+    teach,
     w_in,
     w_dn,
     w_hin,
-    hdn,
     g_in,
     g_dn,
     g_hin,
-    hdn_o,
-    d_hidden,
-    stats,
+    moves_sem,
     w_line,
     g_line,
     g_in_line,
@@ -590,6 +598,8 @@
     z_index = [lax.rem(hi + k, nz) for k in range(1, nz)]
     z_to = [at(k, lo, x, c) for k in z_index]
     meet([at(hi, l2, x2, c) for l2, x2 in quad] + [partner] + z_to)
+    pairs = ((w_in_hbm, w_in), (w_dn_hbm, w_dn), (w_hin_hbm, w_hin), (teach_hbm, teach))
+    fetched = [keep(source, ref, moves_sem.at[k]) for k, (source, ref) in enumerate(pairs)]
     hdn_own = keep(hdn, w_line.at[hi], own)
     hdn_far = [send(hdn, w_line.at[hi], zs.at[0, k], zr.at[0, k], to) for k, to in enumerate(z_to)]
     w_hdn = w_line.reshape(-1, D)
@@ -652,6 +662,7 @@
         up_l[r, :] = dot(hn[r, :], w_in[...])
         z[r, :] = (gelu_value(up_l[r, :fl]) * up_l[r, fl:]).astype(BF)
 
+    fetched[0].wait()
     tiles(tokens, width, light_up)
     for s in seqs:
         relay(every, s, s, *moves[s])
@@ -659,6 +670,7 @@
     def light_down(r):
         out[r, :] = hidden[r, :] + dot(z[r, :], w_dn[...])
 
+    fetched[1].wait()
     tiles(tokens, width, light_down)
 
     def light_slopes(r):
@@ -666,23 +678,29 @@
         up_l[r, :fl] = up_l[r, fl:] * slope
         up_l[r, fl:] = value
 
-    def heavy(s, e):
+    def heavy_up(s, e):
         up_h[s, e] = dot(every[s, e].reshape(block, D), w_hin[...])
         zh[s, e] = (gelu_value(up_h[s, e, :, :fh]) * up_h[s, e, :, fh:]).astype(BF)
+
+    def heavy_down(s, e):
         part[s, e] = dot(zh[s, e], w_hdn[...]).astype(BF).reshape(4, cap, D)
 
-    hdn_own.wait()
-    for copy in hdn_far:
-        copy.wait()
+    fetched[2].wait()
     sums = {}
     for s in seqs:
         for copy in moves[s][1]:
             copy.wait()
-        heavy(s, 1 - c)
+        heavy_up(s, 1 - c)
+        heavy_up(s, c)
+    tiles(tokens, 64, light_slopes)
+    hdn_own.wait()
+    for copy in hdn_far:
+        copy.wait()
+    for s in seqs:
+        heavy_down(s, 1 - c)
         first = send(part.at[s, 1 - c], near.at[s], es.at[s], er.at[s], partner)
-        heavy(s, c)
+        heavy_down(s, c)
         sums[s] = fold(s, s, first)
-    tiles(tokens, 64, light_slopes)
     for s in seqs:
         for e in (0, 1):
 
@@ -694,6 +712,7 @@
             if s == 0:
                 tiles(block, 128, heavy_slopes)
     stats[...] = jnp.zeros(stats.shape, F32)
+    fetched[3].wait()
 
     def light_back(r):
         dz = dot_back(dl[r, :], w_dn[...])
@@ -755,17 +774,20 @@
         g_dn[j, :] = dot_grad(z[:, j], dl[...]).astype(BF)
 
     tiles(fl, 512, light_grad)
+    flushed = [keep(g_dn, g_dn_hbm, moves_sem.at[4])]
 
     def light_in_grad(j):
         g_in[:, j] = dot_grad(hn[...], dup_l[:, j]).astype(BF)
 
     tiles(2 * fl, 1024, light_in_grad)
+    flushed.append(keep(g_in, g_in_hbm, moves_sem.at[5]))
     every_rows = every[...].reshape(count, D)
 
     def heavy_grad(j):
         g_hin[:, j] = dot_grad(every_rows, dup_h[:, :, :, j].reshape(count, 512)).astype(BF)
 
     tiles(2 * fh, 512, heavy_grad)
+    flushed.append(keep(g_hin, g_hin_hbm, moves_sem.at[6]))
     for s in seqs:
         r = span(s)
         high, low = halves(folded(s, group + s, sums[s]))
@@ -776,7 +798,7 @@
         stats[0:1, :] += jnp.sum(dh * inv, axis=0, keepdims=True)
         mean = jnp.mean(gain[1:2, :] * dh, axis=-1, keepdims=True)
         d_hidden[r, :] = out[r, :] + inv * gain[1:2, :] * d - h * (inv * inv * inv * mean)
-    for copy in hdn_back:
+    for copy in hdn_back + flushed:
         copy.wait()
     value = g_view[hi].astype(F32)
     for n in range(nz - 1):
@@ -802,9 +824,17 @@
             jax.ShapeDtypeStruct((8, D), F32),
         ],
         operands,
-        [VM] * (len(operands) - 1) + [ANY],
-        [VM] * 6,
+        [VM] * 5 + [ANY] + [VM] * 2 + [ANY] * 4,
+        [ANY] * 3 + [VM] * 3,
         [
+            pltpu.VMEM((tokens, D), BF),
+            pltpu.VMEM((D, 2 * fl), BF),
+            pltpu.VMEM((fl, D), BF),
+            pltpu.VMEM((D, 2 * fh), BF),
+            pltpu.VMEM((D, 2 * fl), BF),
+            pltpu.VMEM((fl, D), BF),
+            pltpu.VMEM((D, 2 * fh), BF),
+            DMA((7,)),
             pltpu.VMEM(line, BF),
             pltpu.VMEM((fh, D), BF),
             pltpu.VMEM((nz - 1,) + hdn.shape, BF),
@@ -972,6 +1002,7 @@
     other = kvh.at[:, (1 - x_) * 2 + c]
     relay = send(other, other, ss.at[2], sr.at[2], partner)
     finish()
+    stages[3]()
     blocks = width // WIN
 
     def light(i, carry):
@@ -992,9 +1023,9 @@
         return carry
 
     lax.fori_loop(0, group * blocks // 2, light, 0)
-    stages[3]()
+    stages[4]()
     lax.fori_loop(group * blocks // 2, group * blocks, light, 0)
-    stages[4]()
+    stages[5]()
     beside.wait()
     relay.wait()
     heavy_kv = kvh.reshape(group, 4 * cap, 2 * wh)
@@ -1016,7 +1047,7 @@
         return carry
 
     lax.fori_loop(0, group, heavy, 0)
-    stages[5]()
+    stages[6]()
     high, low = halves(dot(ho[...], w_hout[...]))
     for s in range(group):
         r = slice(s * width, (s + 1) * width)
@@ -1030,7 +1061,7 @@
 
 def attend_kernel(*refs):
     meet(line_peers())
-    attend_body([lambda: None] * 6, *refs)
+    attend_body([lambda: None] * 7, *refs)
 
 
 def attend_shapes(tokens, select):
@@ -1154,7 +1185,19 @@
 
 def gather_attend_kernel(dp, nw, *refs):
     n_in, n_out = 7 + nw, 2 + nw + 21
-    ins, outs, rest = refs[:n_in], refs[n_in : n_in + n_out], refs[n_in + n_out :]
+    ins, outs, rest = refs[:n_in], list(refs[n_in : n_in + n_out]), refs[n_in + n_out :]
+    count = len(STAGED)
+    held, flush_sem, rest = rest[:count], rest[count], rest[count + 1 :]
+    final = [outs[k] for k in STAGED]
+    for k, ref in zip(STAGED, held):
+        outs[k] = ref
+    flushed = []
+
+    def flush(*which):
+        for k in which:
+            n = STAGED.index(k)
+            flushed.append(keep(held[n], final[n], flush_sem.at[n]))
+
     xin, ws, hin = ins[0], ins[1 : 1 + nw], ins[1 + nw]
     integers = ins[2 + nw :]
     xo, wos, hin_o = outs[0], outs[1 : 1 + nw], outs[1 + nw]
@@ -1165,22 +1208,18 @@
     g.meet()
     for w in range(nw):
         g.swap(w)
-    for w in (0, 1, 2):
-        g.join(w)
-    for w in (0, 1, 2):
-        g.plane(w)
+    g.join(0)
+    g.join(2)
+    g.plane(0)
+    g.plane(2)
+    g.join(1)
     g.rows()
-    for w in (3, 4, 5, 6):
-        g.join(w)
-    g.heavy_plane()
     route_part(*integers, tables)
     g.cross(0)
+    g.cross(2)
     g.core(0)
-    g.cross(1)
-    g.cross(2)
-    g.heavy_line()
-    g.plane(3)
-    g.plane(4)
+    g.plane(1)
+    g.core(2)
     g.ready(0)
     total = jnp.zeros(gain.shape, F32)
     for z in range(dp // 2):
@@ -1189,37 +1228,58 @@
             total += pair[:8] + pair[8:]
     gain[...] = total
     g.rows_ready()
+    for w in (4, 3, 5, 6):
+        g.join(w)
+    g.heavy_plane()
+    flush(0)
 
     def heavy_projection():
+        g.cross(1)
+        g.ready(2)
+        flush(20, 3)
+
+    def light_projection():
         g.core(1)
-        g.core(2)
-        g.ready(2)
-
-    def light_projection():
+        g.ready(1)
+        flush(2)
+
+    def keys_travel():
+        g.plane(4)
+        g.plane(3)
+        flush(21)
+
+    def keys_there():
         g.plane(5)
         g.plane(6)
-        g.ready(1)
-
-    def keys_travel():
+        g.heavy_line()
+        flush(22)
+
+    def half_way():
+        g.cross(4)
         g.cross(3)
-        g.cross(4)
-
-    def half_way():
+
+    def light_done():
+        g.core(4)
         g.core(3)
-        g.core(4)
-
-    def light_done():
+        flush(23)
+
+    def heavy_done():
         g.cross(5)
         g.cross(6)
-
-    def heavy_done():
-        g.core(5)
-        g.core(6)
+        g.ready(4)
         g.ready(3)
-        g.ready(4)
+        flush(27, 4, 5)
 
     full = [wos[w].reshape(-1, wos[w].shape[-1]) for w in range(nw)]
-    stages = [heavy_projection, light_projection, keys_travel, half_way, light_done, heavy_done]
+    stages = [
+        heavy_projection,
+        light_projection,
+        keys_travel,
+        keys_there,
+        half_way,
+        light_done,
+        heavy_done,
+    ]
     attend_body(
         stages,
         xo.reshape(-1, D),
@@ -1232,9 +1292,16 @@
         *saved,
         *rest[11:],
     )
+    g.core(5)
+    g.core(6)
     g.ready(5)
     g.ready(6)
     g.heavy_ready()
+    for copy in flushed:
+        copy.wait()
+
+
+STAGED = (0, 2, 3, 4, 5, 20, 21, 22, 23, 27)
 
 
 def gather_attend(dp, xin, weights, hin, integers):
@@ -1250,8 +1317,10 @@
         shapes,
         [xin, *weights, hin, *integers],
         [ANY] * (2 + nw) + [VM] * 5,
-        [VM] * 6 + [ANY] * 3 + [VM] * 21,
-        [pltpu.VMEM((w.shape[0], w.shape[1] // 2), BF) for w in weights] * 2
+        [ANY if k in STAGED + (6, 7, 8) else VM for k in range(len(shapes))],
+        [pltpu.VMEM(shapes[k].shape, BF) for k in STAGED]
+        + [DMA((len(STAGED),))]
+        + [pltpu.VMEM((w.shape[0], w.shape[1] // 2), BF) for w in weights] * 2
         + [pltpu.VMEM((2 * w.shape[0], w.shape[1] // 2), BF) for w in weights]
         + [DMA((nw,))] * 3
         + gather_sems(dp, nw)
@@ -1782,6 +1851,11 @@
     ops, (g_lin, g_ldn, hin, ffn_stats) = refs[:n_ops], refs[n_ops : n_ops + 4]
     outs, rest = refs[n_ops + 4 : n_ops + 7 + nw], refs[n_ops + 7 + nw :]
     dxo, total, gos, hin_o = outs[0], outs[1], outs[2 : 2 + nw], outs[2 + nw]
+    count = len(FETCHED)
+    held, fetch_sem, rest = rest[:count], rest[count], rest[count + 1 :]
+    sources, ops = [ops[k] for k in FETCHED], list(ops)
+    for k, ref in zip(FETCHED, held):
+        ops[k] = ref
     full, rest = rest[:4], rest[4:]
     own_lin, own_ldn, stats, rest = rest[0], rest[1], rest[2], rest[3:]
     back, rest = rest[:17], rest[17:]
@@ -1803,6 +1877,15 @@
         g_views.append(full[k].reshape(nz, 2, 2, 2 * rows, columns))
     t = Scatter(nz, shards, g_views, near, one, two, end, (cs, cr, ps, pr, zs, zr))
     meet(rows_to + [at(hi, *q[:3]) for q in others if q[3]])
+    fetched = {
+        k: keep(source, ref, fetch_sem.at[n])
+        for n, (k, source, ref) in enumerate(zip(FETCHED, sources, held))
+    }
+
+    def fetch(*which):
+        for k in which:
+            fetched[k].wait()
+
     h_sends = []
     for k, z in enumerate(z_index):
         h_sends.append(send(hin.at[z], hin_r.at[k], hs.at[1, k], hr.at[1, k], z_to[k]))
@@ -1816,6 +1899,7 @@
     late = []
 
     def first_plane():
+        fetch(9, 14)
         kept[0].wait()
         kept[1].wait()
         t.own_plane(0, own_lin)
@@ -1826,25 +1910,26 @@
         t.core(3)
 
     def before_light():
+        fetch(12, 13)
+
+    def half_way():
+        t.core(4)
         t.cross(0)
         t.cross(1)
         t.plane(2)
-
-    def half_way():
-        t.core(4)
         t.plane(3)
+
+    def rims_left():
+        fetch(8, 11)
+        t.plane(4)
         t.line(0)
         t.line(1)
-
-    def rims_left():
-        t.plane(4)
         t.cross(2)
         t.cross(3)
 
     def light_grad_done():
         t.core(5)
-        t.line(2)
-        t.line(3)
+        fetch(7, 1)
 
     def rows_done():
         rows = dx.reshape(dxo.shape[1], dp, dxo.shape[2], D)
@@ -1873,14 +1958,16 @@
     acc[12:16, :] = jnp.broadcast_to(loss, (4, 128))
     t_c = send(acc, sc, ts.at[0], tr.at[0], partner)
     t.plane(5)
+    t.line(2)
+    t.line(3)
     t.cross(4)
-    t.line(4)
     t_c.wait()
     acc2[...] = acc[...] + sc[...]
     t_p = [
         send(acc2, sp.at[k], ts.at[1 + k], tr.at[1 + k], at(hi, l2, x2, c))
         for k, (l2, x2) in enumerate(quad)
     ]
+    t.line(4)
     for copy in h_sends + kept[2:]:
         copy.wait()
 
@@ -1921,6 +2008,9 @@
         copy.wait()
 
 
+FETCHED = (9, 14, 12, 13, 8, 11, 7, 1)
+
+
 def back_scatter(dp, rows, d_hidden, x, gain, masks, weights, saved, ffn_grads, ffn_stats, shards, hin):
     nz, nw = dp // 2, len(shards)
     tokens = x.shape[0]
@@ -1934,7 +2024,9 @@
     shapes = [jax.ShapeDtypeStruct((dp, group, rows, D), BF), jax.ShapeDtypeStruct(stat_shape, F32)]
     shapes += [jax.ShapeDtypeStruct(s, F32) for s in shards]
     shapes.append(jax.ShapeDtypeStruct(hin.shape[1:], BF))
-    scratch = [pltpu.VMEM((s[0] * 8 * nz, s[1]), BF) for s in shards[2:]]
+    scratch = [pltpu.VMEM(operands[k].shape, operands[k].dtype) for k in FETCHED]
+    scratch.append(DMA((len(FETCHED),)))
+    scratch += [pltpu.VMEM((s[0] * 8 * nz, s[1]), BF) for s in shards[2:]]
     split = [(2 * s[0], s[1] // 2) for s in shards]
     scratch += [pltpu.VMEM((nz, 2, 2) + s, BF) for s in split[:2]]
     scratch += [pltpu.VMEM((8, D), F32)]
@@ -1973,7 +2065,7 @@
         functools.partial(back_scatter_kernel, dp, shards),
         shapes,
         operands,
-        [VM] * (len(operands) - 4) + [ANY] * 3 + [VM],
+        [ANY if k in FETCHED else VM for k in range(len(operands) - 4)] + [ANY] * 3 + [VM],
         [VM] * len(shapes),
         scratch,
         6,

time: 333 us -> 298 us (0.89)
  Pallas kernels: 323 us -> 289 us
    pallas_call x3, Pallas kernels: 317 us -> 283 us  [call(): pl.pallas_call(kernel, out_shape=out_shape, in_specs=in_specs, out_specs=...]
where the time goes in v8:
time: 298 us; the launch traced here: 294 us
  Pallas kernels  289 us (97%)
  between operations  3.31 us (1%)
    pallas_call x3, Pallas kernels, call(): pl.pallas_call(kernel, out_shape=out_shape, in_specs=in_specs, out_specs=...  283 us

profile of v8, /device:TPU:0, one launch (start us, length us, event | category | flops | bytes accessed | tf_op | source)
XLA Modules:
  0.0 294.4 jit_solution(3850703532234009183)
XLA Ops:
  0.6 2.4 shard_map.256
  3.1 104.3 %shard_map.257 = (bf16[2,8,32,768]{3,2,1,0:T(8,128)(2,1)}, bf16[4,2,2,16,768]{4,3,2,1,0:T(8,128)(2,1)}, bf16[4,2,2,48,1536]{4,3,2,1,0:T(8,128)(2,1)}, bf16[4,2,2...) custom-call(bf16[16,32,768]{2,1,0:T(8,128)(2,1)} %get-tuple-element., ...), custom_call_target="tpu_custom_call" | custom-call | tf_op jit(solution)/shard_map/pallas_call | solution.py:72
  107.3 71.0 %shard_map.258 = (bf16[768,2048]{1,0:T(8,128)(2,1)}, bf16[1024,768]{1,0:T(8,128)(2,1)}, bf16[768,1024]{1,0:T(8,128)(2,1)}, f32[128,768]{1,0:T(8,128)}, f32[512,768]{1,0:T(8,128)}, /*index=5*/f32[8,768]{1,0:T(8,128)}) custom-call(f32[512,768]{1,0:T(8,128)} %get-tuple-element.71.hidden, bf16[2,64,256]{2,1,0:T(8,128)(2,1)} %get-tuple-element.72.select, ...), custom_call_target="tpu_custom_call" | custom-call | tf_op jit(solution)/shard_map/pallas_call | solution.py:72
  178.3 107.5 %shard_map.259 = (bf16[8,2,32,768]{3,2,1,0:T(8,128)(2,1)}, f32[16,128]{1,0:T(8,128)}, f32[24,2048]{1,0:T(8,128)}, f32[32,768]{1,0:T(8,128)}, f32[24,768]{1,0:T(8...) custom-call(f32[512,768]{1,0:T(8,128)} %get-tuple-element.81.refs_0_, ...), custom_call_target="tpu_custom_call" | custom-call | tf_op jit(solution)/shard_map/pallas_call | solution.py:72
  285.8 0.0 copy-start
  285.8 0.0 copy-start.1
  285.8 3.6 %shard_map.260 = (f32[16,32,768]{2,1,0:T(8,128)}, f32[24,8192]{1,0:T(8,128)}, f32[24,2048]{1,0:T(8,128)}, f32[32,768]{1,0:T(8,128)}, f32[24,768]{1,0:T(8,128)}, ...) custom-call(s32[16]{0:T(128)} %deal_ref.3, bf16[16,32,768]{2,1,0:T(8,128)(2,1)} %bitcast.37, ...), custom_call_target="tpu_custom_call" | custom-call | tf_op jit(solution)/shard_map/pallas_call | solution.py:184
  289.4 0.0 copy-done
  289.4 0.6 dynamic_slice.6
  290.0 0.6 dynamic_slice.7
  290.6 0.5 slice.9
  291.1 0.0 copy-done.1
  291.1 0.6 reduce_sum.9
  (1 shorter events, 0.0 us)
Async XLA Ops:
  285.8 3.6 %copy-start = (f32[16,128]{1,0:T(8,128)S(1)}, f32[16,128]{1,0:T(8,128)}, u32[]{:S(2)}) copy-start(f32[16,128]{1,0:T(8,128)} %get-tuple-element.105) | copy-start | bytes 24580
  285.8 5.3 %copy-start.1 = (s32[16]{0:T(128)S(1)}, s32[16]{0:T(128)}, u32[]{:S(2)}) copy-start(s32[16]{0:T(128)} %param.19) | copy-start | bytes 196

commit v9 on v8

--- a/solution.py
+++ b/solution.py
@@ -696,11 +696,14 @@
     hdn_own.wait()
     for copy in hdn_far:
         copy.wait()
+    first = {}
     for s in seqs:
         heavy_down(s, 1 - c)
-        first = send(part.at[s, 1 - c], near.at[s], es.at[s], er.at[s], partner)
+        first[s] = send(part.at[s, 1 - c], near.at[s], es.at[s], er.at[s], partner)
+        if s > 0:
+            sums[s - 1] = fold(s - 1, s - 1, first[s - 1])
         heavy_down(s, c)
-        sums[s] = fold(s, s, first)
+    sums[group - 1] = fold(group - 1, group - 1, first[group - 1])
     for s in seqs:
         for e in (0, 1):
 
@@ -756,11 +759,6 @@
     for s in seqs:
         for copy in moves[s][1]:
             copy.wait()
-        heavy_back(s, 1 - c)
-        i = group + s
-        second = send(part.at[s, 1 - c], near.at[i], es.at[i], er.at[i], partner)
-        heavy_back(s, c)
-        sums[s] = fold(s, i, second)
     count = group * 2 * block
     d_rows = d_every[...].reshape(count, D)
     g_line[...] = dot_grad(zh[...].reshape(count, fh), d_rows).astype(BF)
@@ -769,6 +767,14 @@
         send(g_view.at[k], g_in_line.at[n], zs.at[1, n], zr.at[1, n], z_to[n])
         for n, k in enumerate(z_index)
     ]
+    for s in seqs:
+        i = group + s
+        heavy_back(s, 1 - c)
+        first[s] = send(part.at[s, 1 - c], near.at[i], es.at[i], er.at[i], partner)
+        if s > 0:
+            sums[s - 1] = fold(s - 1, i - 1, first[s - 1])
+        heavy_back(s, c)
+    sums[group - 1] = fold(group - 1, 2 * group - 1, first[group - 1])
 
     def light_grad(j):
         g_dn[j, :] = dot_grad(z[:, j], dl[...]).astype(BF)
@@ -1246,12 +1252,12 @@
     def keys_travel():
         g.plane(4)
         g.plane(3)
+        g.heavy_line()
         flush(21)
 
     def keys_there():
         g.plane(5)
         g.plane(6)
-        g.heavy_line()
         flush(22)
 
     def half_way():
@@ -1261,11 +1267,11 @@
     def light_done():
         g.core(4)
         g.core(3)
-        flush(23)
-
-    def heavy_done():
         g.cross(5)
         g.cross(6)
+        flush(23)
+
+    def heavy_done():
         g.ready(4)
         g.ready(3)
         flush(27, 4, 5)

time: 298 us -> 290 us (0.973)
  Pallas kernels: 289 us -> 281 us
    pallas_call x3, Pallas kernels: 283 us -> 275 us  [call(): pl.pallas_call(kernel, out_shape=out_shape, in_specs=in_specs, out_specs=...]
where the time goes in v9:
time: 290 us; the launch traced here: 286 us
  Pallas kernels  281 us (97%)
  between operations  3.31 us (1%)
    pallas_call x3, Pallas kernels, call(): pl.pallas_call(kernel, out_shape=out_shape, in_specs=in_specs, out_specs=...  275 us

profile of v9, /device:TPU:0, one launch (start us, length us, event | category | flops | bytes accessed | tf_op | source)
XLA Modules:
  0.0 286.4 jit_solution(17117579656523336114)
XLA Ops:
  0.6 2.4 shard_map.256
  3.1 102.7 %shard_map.257 = (bf16[2,8,32,768]{3,2,1,0:T(8,128)(2,1)}, bf16[4,2,2,16,768]{4,3,2,1,0:T(8,128)(2,1)}, bf16[4,2,2,48,1536]{4,3,2,1,0:T(8,128)(2,1)}, bf16[4,2,2...) custom-call(bf16[16,32,768]{2,1,0:T(8,128)(2,1)} %get-tuple-element., ...), custom_call_target="tpu_custom_call" | custom-call | tf_op jit(solution)/shard_map/pallas_call | solution.py:72
  105.8 65.9 %shard_map.258 = (bf16[768,2048]{1,0:T(8,128)(2,1)}, bf16[1024,768]{1,0:T(8,128)(2,1)}, bf16[768,1024]{1,0:T(8,128)(2,1)}, f32[128,768]{1,0:T(8,128)}, f32[512,768]{1,0:T(8,128)}, /*index=5*/f32[8,768]{1,0:T(8,128)}) custom-call(f32[512,768]{1,0:T(8,128)} %get-tuple-element.71.hidden, bf16[2,64,256]{2,1,0:T(8,128)(2,1)} %get-tuple-element.72.select, ...), custom_call_target="tpu_custom_call" | custom-call | tf_op jit(solution)/shard_map/pallas_call | solution.py:72
  171.6 106.2 %shard_map.259 = (bf16[8,2,32,768]{3,2,1,0:T(8,128)(2,1)}, f32[16,128]{1,0:T(8,128)}, f32[24,2048]{1,0:T(8,128)}, f32[32,768]{1,0:T(8,128)}, f32[24,768]{1,0:T(8...) custom-call(f32[512,768]{1,0:T(8,128)} %get-tuple-element.81.refs_0_, ...), custom_call_target="tpu_custom_call" | custom-call | tf_op jit(solution)/shard_map/pallas_call | solution.py:72
  277.8 0.0 copy-start
  277.8 0.0 copy-start.1
  277.8 3.6 %shard_map.260 = (f32[16,32,768]{2,1,0:T(8,128)}, f32[24,8192]{1,0:T(8,128)}, f32[24,2048]{1,0:T(8,128)}, f32[32,768]{1,0:T(8,128)}, f32[24,768]{1,0:T(8,128)}, ...) custom-call(s32[16]{0:T(128)} %deal_ref.3, bf16[16,32,768]{2,1,0:T(8,128)(2,1)} %bitcast.37, ...), custom_call_target="tpu_custom_call" | custom-call | tf_op jit(solution)/shard_map/pallas_call | solution.py:184
  281.4 0.0 copy-done
  281.5 0.6 dynamic_slice.6
  282.0 0.6 dynamic_slice.7
  282.6 0.5 slice.9
  283.1 0.0 copy-done.1
  283.1 0.6 reduce_sum.9
  (1 shorter events, 0.0 us)
Async XLA Ops:
  277.8 3.6 %copy-start = (f32[16,128]{1,0:T(8,128)S(1)}, f32[16,128]{1,0:T(8,128)}, u32[]{:S(2)}) copy-start(f32[16,128]{1,0:T(8,128)} %get-tuple-element.105) | copy-start | bytes 24580
  277.8 5.3 %copy-start.1 = (s32[16]{0:T(128)S(1)}, s32[16]{0:T(128)}, u32[]{:S(2)}) copy-start(s32[16]{0:T(128)} %param.19) | copy-start | bytes 196

commit v10 on v9

--- a/solution.py
+++ b/solution.py
@@ -529,6 +529,7 @@
 
 def ffn_kernel(
     nz,
+    swapped,
     hidden,
     select,
     select_t,
@@ -584,6 +585,7 @@
     zs,
     zr,
     own,
+    *mates,
 ):
     hi, lo, x, c = place()
     quad = quad_peers()
@@ -780,13 +782,42 @@
         g_dn[j, :] = dot_grad(z[:, j], dl[...]).astype(BF)
 
     tiles(fl, 512, light_grad)
-    flushed = [keep(g_dn, g_dn_hbm, moves_sem.at[4])]
+    halved = []
+
+    def swap(k, grad):
+        rows, lanes = mates[k].shape[3:]
+        view = grad.reshape(nz, 2, 2, rows, 2 * lanes)
+        other = pl.ds(pl.multiple_of((1 - c) * lanes, 128), lanes)
+        halved.append(view)
+        sem = mates[2:]
+        return send(view.at[:, :, :, :, other], mates[k], sem[0].at[k], sem[1].at[k], partner)
+
+    def join(k):
+        near_k, view, lanes = mates[k], halved[k], mates[k].shape[4]
+        own_lanes = pl.ds(pl.multiple_of(c * lanes, 128), lanes)
+
+        def add(n, carry):
+            a, b, e = n // 4, (n // 2) % 2, n % 2
+            value = near_k[a, b, e].astype(F32) + view[a, b, e, :, own_lanes].astype(F32)
+            near_k[a, b, e] = value.astype(BF)
+            return carry
+
+        lax.fori_loop(0, nz * 4, add, 0)
+
+    flushed, swaps = [], []
+    if swapped:
+        swaps.append(swap(0, g_dn))
+    else:
+        flushed.append(keep(g_dn, g_dn_hbm, moves_sem.at[4]))
 
     def light_in_grad(j):
         g_in[:, j] = dot_grad(hn[...], dup_l[:, j]).astype(BF)
 
     tiles(2 * fl, 1024, light_in_grad)
-    flushed.append(keep(g_in, g_in_hbm, moves_sem.at[5]))
+    if swapped:
+        swaps.append(swap(1, g_in))
+    else:
+        flushed.append(keep(g_in, g_in_hbm, moves_sem.at[5]))
     every_rows = every[...].reshape(count, D)
 
     def heavy_grad(j):
@@ -794,6 +825,11 @@
 
     tiles(2 * fh, 512, heavy_grad)
     flushed.append(keep(g_hin, g_hin_hbm, moves_sem.at[6]))
+    if swapped:
+        for k, target in enumerate((g_dn_hbm, g_in_hbm)):
+            swaps[k].wait()
+            join(k)
+            flushed.append(keep(mates[k], target, moves_sem.at[4 + k]))
     for s in seqs:
         r = span(s)
         high, low = halves(folded(s, group + s, sums[s]))
@@ -812,18 +848,21 @@
     hdn_o[...] = value
 
 
-def feed_forward(nz, hidden, select, select_t, score, gain, teach, mask, scale, w_in, w_dn, w_hin, hdn):
+def feed_forward(nz, swapped, hidden, select, select_t, score, gain, teach, mask, scale, w_in, w_dn, w_hin, hdn):
     tokens = hidden.shape[0]
     group, cap, _ = select.shape
     fl, fh = w_dn.shape[0], w_hin.shape[1] // 2
     block = (group, 2, 4, cap, D)
     line = (nz,) + hdn.shape
+    half_in = (nz, 2, 2, D // (nz * 4), fl)
+    half_dn = (nz, 2, 2, fl // (nz * 4), D // 2)
+    extra = [pltpu.VMEM(half_dn, BF), pltpu.VMEM(half_in, BF), DMA((2,)), DMA((2,))]
     operands = [hidden, select, select_t, score, gain, teach, mask, scale, w_in, w_dn, w_hin, hdn]
     return call(
-        functools.partial(ffn_kernel, nz),
+        functools.partial(ffn_kernel, nz, swapped),
         [
-            jax.ShapeDtypeStruct((D, 2 * fl), BF),
-            jax.ShapeDtypeStruct((fl, D), BF),
+            jax.ShapeDtypeStruct(half_in if swapped else (D, 2 * fl), BF),
+            jax.ShapeDtypeStruct(half_dn if swapped else (fl, D), BF),
             jax.ShapeDtypeStruct((D, 2 * fh), BF),
             jax.ShapeDtypeStruct(hdn.shape, F32),
             jax.ShapeDtypeStruct((tokens, D), F32),
@@ -870,7 +909,8 @@
             DMA((2, nz)),
             DMA((2, nz)),
             DMA,
-        ],
+        ]
+        + (extra if swapped else []),
         5,
     )
 
@@ -1772,9 +1812,6 @@
         g, own = self.gs[w], self.lanes(w, self.c)
         self.add_plane(w, lambda z, a, b: g[z, a, b, :, own])
 
-    def own_plane(self, w, kept):
-        self.add_plane(w, lambda z, a, b: kept[z, a, b])
-
     def add_plane(self, w, own):
         self.wait(w, 0)
         near = self.near[w]
@@ -1790,6 +1827,15 @@
         self.copies[w, 1] = [
             send(near.at[low, :, 1 - x], self.one[w].at[low], self.ps.at[w, 0], self.pr.at[w, 0], self.by_x),
             send(near.at[high, 1 - lo], self.one[w].at[high], self.ps.at[w, 1], self.pr.at[w, 1], self.by_y),
+        ]
+
+    def begin(self, w, source, sem):
+        near, lo, x, half = self.near[w], self.lo, self.x, self.nz // 2
+        low, high = pl.ds(0, half), pl.ds(half, self.nz - half)
+        self.copies[w, 1] = [
+            keep(source, near, sem),
+            send(source.at[low, :, 1 - x], self.one[w].at[low], self.ps.at[w, 0], self.pr.at[w, 0], self.by_x),
+            send(source.at[high, 1 - lo], self.one[w].at[high], self.ps.at[w, 1], self.pr.at[w, 1], self.by_y),
         ]
 
     def cross(self, w):
@@ -1863,7 +1909,7 @@
     for k, ref in zip(FETCHED, held):
         ops[k] = ref
     full, rest = rest[:4], rest[4:]
-    own_lin, own_ldn, stats, rest = rest[0], rest[1], rest[2], rest[3:]
+    stats, rest = rest[0], rest[1:]
     back, rest = rest[:17], rest[17:]
     dx = back[5]
     near, one, two, end, fin = (rest[k * nw : (k + 1) * nw] for k in range(5))
@@ -1877,7 +1923,7 @@
     z_index = [lax.rem(hi + k, nz) for k in range(1, nz)]
     z_to = [at(z, lo, x, c) for z in z_index]
     quad = quad_peers()
-    g_views = [g_lin, g_ldn]
+    g_views = [None, None]
     for k, w in enumerate((2, 3, 4, 5)):
         rows, columns = shards[w]
         g_views.append(full[k].reshape(nz, 2, 2, 2 * rows, columns))
@@ -1895,21 +1941,13 @@
     h_sends = []
     for k, z in enumerate(z_index):
         h_sends.append(send(hin.at[z], hin_r.at[k], hs.at[1, k], hr.at[1, k], z_to[k]))
-    t.core(0)
-    t.core(1)
-    kept = [
-        keep(g_lin.at[:, :, :, :, t.lanes(0, c)], own_lin, own.at[0]),
-        keep(g_ldn.at[:, :, :, :, t.lanes(1, c)], own_ldn, own.at[1]),
-        keep(hin.at[hi], hin_own, own.at[2]),
-    ]
+    t.begin(0, g_lin, own.at[0])
+    t.begin(1, g_ldn, own.at[1])
+    kept = [keep(hin.at[hi], hin_own, own.at[2])]
     late = []
 
     def first_plane():
         fetch(9, 14)
-        kept[0].wait()
-        kept[1].wait()
-        t.own_plane(0, own_lin)
-        t.own_plane(1, own_ldn)
         t.core(2)
 
     def out_core():
@@ -1974,7 +2012,7 @@
         for k, (l2, x2) in enumerate(quad)
     ]
     t.line(4)
-    for copy in h_sends + kept[2:]:
+    for copy in h_sends + kept:
         copy.wait()
 
     def body(i, carry):
@@ -2023,10 +2061,7 @@
     group = masks[0].shape[0]
     most = max(7, nz)
     stat_shape = (16, 128)
-    paired = [
-        g.reshape(nz, 2, 2, 2 * s[0], s[1]) for g, s in zip(ffn_grads, shards)
-    ]
-    operands = [d_hidden, x, gain, *masks, *weights, *saved, *paired, hin, ffn_stats]
+    operands = [d_hidden, x, gain, *masks, *weights, *saved, *ffn_grads, hin, ffn_stats]
     shapes = [jax.ShapeDtypeStruct((dp, group, rows, D), BF), jax.ShapeDtypeStruct(stat_shape, F32)]
     shapes += [jax.ShapeDtypeStruct(s, F32) for s in shards]
     shapes.append(jax.ShapeDtypeStruct(hin.shape[1:], BF))
@@ -2034,7 +2069,6 @@
     scratch.append(DMA((len(FETCHED),)))
     scratch += [pltpu.VMEM((s[0] * 8 * nz, s[1]), BF) for s in shards[2:]]
     split = [(2 * s[0], s[1] // 2) for s in shards]
-    scratch += [pltpu.VMEM((nz, 2, 2) + s, BF) for s in split[:2]]
     scratch += [pltpu.VMEM((8, D), F32)]
     scratch += attend_back_scratch(tokens, masks[0])
     scratch += [pltpu.VMEM((nz, 2, 2) + s, BF) for s in split]
@@ -2169,6 +2203,7 @@
     f_select, f_select_t, slot_score, weight_mask, weight_scale = ffn_masks
     grad_lin, grad_ldown, grad_hin, g_hdown, d_hidden, ffn_stats = feed_forward(
         nz,
+        merged,
         hidden,
         f_select,
         f_select_t,

time: 290 us -> 284 us (0.979)
  Pallas kernels: 281 us -> 275 us
    pallas_call x3, Pallas kernels: 275 us -> 269 us  [call(): pl.pallas_call(kernel, out_shape=out_shape, in_specs=in_specs, out_specs=...]
where the time goes in v10:
time: 284 us; the launch traced here: 281 us
  Pallas kernels  275 us (97%)
  between operations  3.31 us (1%)
    pallas_call x3, Pallas kernels, call(): pl.pallas_call(kernel, out_shape=out_shape, in_specs=in_specs, out_specs=...  269 us

profile of v10, /device:TPU:0, one launch (start us, length us, event | category | flops | bytes accessed | tf_op | source)
XLA Modules:
  0.0 280.8 jit_solution(8799423583453763228)
XLA Ops:
  0.6 2.4 shard_map.256
  3.1 102.8 %shard_map.257 = (bf16[2,8,32,768]{3,2,1,0:T(8,128)(2,1)}, bf16[4,2,2,16,768]{4,3,2,1,0:T(8,128)(2,1)}, bf16[4,2,2,48,1536]{4,3,2,1,0:T(8,128)(2,1)}, bf16[4,2,2...) custom-call(bf16[16,32,768]{2,1,0:T(8,128)(2,1)} %get-tuple-element., ...), custom_call_target="tpu_custom_call" | custom-call | tf_op jit(solution)/shard_map/pallas_call | solution.py:72
  105.8 65.9 %shard_map.258 = (bf16[4,2,2,48,1024]{4,3,2,1,0:T(8,128)(2,1)}, bf16[4,2,2,64,384]{4,3,2,1,0:T(8,128)(2,1)}, bf16[768,1024]{1,0:T(8,128)(2,1)}, f32[128,768]{1,0...) custom-call(f32[512,768]{1,0:T(8,128)} %get-tuple-element.71.hidden, bf16[2,64,256]{2,1,0:T(8,128)(2,1)} %get-tuple-element.72.select, ...), custom_call_target="tpu_custom_call" | custom-call | tf_op jit(solution)/shard_map/pallas_call | solution.py:72
  171.7 100.5 %shard_map.259 = (bf16[8,2,32,768]{3,2,1,0:T(8,128)(2,1)}, f32[16,128]{1,0:T(8,128)}, f32[24,2048]{1,0:T(8,128)}, f32[32,768]{1,0:T(8,128)}, f32[24,768]{1,0:T(8...) custom-call(f32[512,768]{1,0:T(8,128)} %get-tuple-element.81.refs_0_, ...), custom_call_target="tpu_custom_call" | custom-call | tf_op jit(solution)/shard_map/pallas_call | solution.py:72
  272.2 0.0 copy-start
  272.2 0.0 copy-start.1
  272.2 3.6 %shard_map.260 = (f32[16,32,768]{2,1,0:T(8,128)}, f32[24,8192]{1,0:T(8,128)}, f32[24,2048]{1,0:T(8,128)}, f32[32,768]{1,0:T(8,128)}, f32[24,768]{1,0:T(8,128)}, ...) custom-call(s32[16]{0:T(128)} %deal_ref.3, bf16[16,32,768]{2,1,0:T(8,128)(2,1)} %bitcast.31, ...), custom_call_target="tpu_custom_call" | custom-call | tf_op jit(solution)/shard_map/pallas_call | solution.py:184
  275.8 0.0 copy-done
  275.9 0.6 dynamic_slice.6
  276.4 0.6 dynamic_slice.7
  277.0 0.5 slice.9
  277.5 0.0 copy-done.1
  277.5 0.6 reduce_sum.9
  (1 shorter events, 0.0 us)
Async XLA Ops:
  272.2 3.6 %copy-start = (f32[16,128]{1,0:T(8,128)S(1)}, f32[16,128]{1,0:T(8,128)}, u32[]{:S(2)}) copy-start(f32[16,128]{1,0:T(8,128)} %get-tuple-element.105) | copy-start | bytes 24580
  272.2 5.3 %copy-start.1 = (s32[16]{0:T(128)S(1)}, s32[16]{0:T(128)}, u32[]{:S(2)}) copy-start(s32[16]{0:T(128)} %param.19) | copy-start | bytes 196

commit v11 on v10

--- a/solution.py
+++ b/solution.py
@@ -158,9 +158,22 @@
     )(dealing, rows, heavy_in, gain_one.reshape(1, count), gain_two.reshape(1, count))
 
 
-def finish_kernel(units, deal_ref, x_ref, hin, *refs):
-    count = (len(refs) - 2) // 2
-    ins, (rows, heavy), outs = refs[:count], refs[count : count + 2], refs[count + 2 :]
+def finish_kernel(units, deal_ref, x_ref, hin, summed, lengths, *refs):
+    count = (len(refs) - 5) // 2
+    ins, (rows, heavy, loss, one, two), outs = refs[:count], refs[count : count + 5], refs[count + 5 :]
+    tokens = jnp.sum(lengths[...].astype(F32), axis=1, keepdims=True)
+    loss[...] = summed[12:13, 0:1] / (D * tokens)
+    owned = one.shape[1]
+    mine = lax.axis_index("dp") * 4 + lax.axis_index("fsdp")
+    row = lax.broadcasted_iota(jnp.int32, (128, owned), 0)
+    lane = lax.broadcasted_iota(jnp.int32, (128, owned), 1)
+    gains = [jnp.zeros((1, owned), F32)] * 2
+    for k in range(D // 128):
+        hot = jnp.where(row + k * 128 == lane + mine * owned, 1.0, 0.0)
+        part = jnp.dot(summed[...], hot, precision=lax.Precision.HIGHEST, preferred_element_type=F32)
+        gains = [gains[0] + part[k : k + 1], gains[1] + part[6 + k : 7 + k]]
+    one[...] = gains[0]
+    two[...] = gains[1]
 
     def body(i, carry):
         rows[deal_ref[i]] = x_ref[i].astype(F32)
@@ -178,16 +191,17 @@
         out[...] = source[...]
 
 
-def finish_all(units, dealing, rows, hin, grads, heavy_shape):
+def finish_all(units, dealing, rows, hin, summed, lengths, grads, heavy_shape, owned):
     shapes = [jax.ShapeDtypeStruct(rows.shape, F32), jax.ShapeDtypeStruct(heavy_shape, F32)]
+    shapes += [jax.ShapeDtypeStruct(shape, F32) for shape in ((1, 1), (1, owned), (1, owned))]
     shapes += [jax.ShapeDtypeStruct(g.shape, F32) for g in grads]
     return pl.pallas_call(
         functools.partial(finish_kernel, units),
         out_shape=shapes,
-        in_specs=[pl.BlockSpec(memory_space=pltpu.SMEM)] + [VM] * (2 + len(grads)),
+        in_specs=[pl.BlockSpec(memory_space=pltpu.SMEM)] + [VM] * (4 + len(grads)),
         out_specs=[VM] * len(shapes),
         compiler_params=pltpu.CompilerParams(vmem_limit_bytes=VMEM_BYTES),
-    )(dealing, rows, hin, *grads)
+    )(dealing, rows, hin, summed, lengths, *grads)
 
 
 def packed(matrix):
@@ -2252,15 +2266,28 @@
             dp, d_inputs.reshape(group, dp, rows, D), stats, sent, hin_part
         )
     summed = done[1]
-    loss_value = summed[12, 0] / (D * token_count)
-    own_one = lax.dynamic_slice_in_dim(summed[:6].reshape(-1), mine * gain_len, gain_len)
-    own_two = lax.dynamic_slice_in_dim(summed[6:12].reshape(-1), mine * gain_len, gain_len)
     back_rows = done[0].reshape(seqs, rows, D)
     if merged:
-        d_layer, g_hin, *owned = finish_all(
-            n, dealing, back_rows, done[8], [*done[2:8], g_hdown], heavy_in.shape
+        d_layer, g_hin, loss_value, own_one, own_two, *owned = finish_all(
+            n,
+            dealing,
+            back_rows,
+            done[8],
+            summed,
+            integers[1],
+            [*done[2:8], g_hdown],
+            heavy_in.shape,
+            gain_len,
+        )
+        loss_value, own_one, own_two = (
+            loss_value.reshape(()),
+            own_one.reshape(gain_len),
+            own_two.reshape(gain_len),
         )
     else:
+        loss_value = summed[12, 0] / (D * token_count)
+        own_one = lax.dynamic_slice_in_dim(summed[:6].reshape(-1), mine * gain_len, gain_len)
+        own_two = lax.dynamic_slice_in_dim(summed[6:12].reshape(-1), mine * gain_len, gain_len)
         d_layer = undeal_rows(dealing, back_rows)
         owned = [full.reshape(shard.shape) for full, shard in zip(done[2:8], shards)]
         owned.append(g_hdown)

time: 284 us -> 280 us (0.986)
  no operation moved by 1% of the time
where the time goes in v11:
time: 280 us; the launch traced here: 277 us
  Pallas kernels  276 us (99%)
    pallas_call x3, Pallas kernels, call(): pl.pallas_call(kernel, out_shape=out_shape, in_specs=in_specs, out_specs=...  269 us

profile of v11, /device:TPU:0, one launch (start us, length us, event | category | flops | bytes accessed | tf_op | source)
XLA Modules:
  0.0 276.6 jit_solution(8602336649372070056)
XLA Ops:
  0.6 2.4 shard_map.256
  3.1 102.7 %shard_map.257 = (bf16[2,8,32,768]{3,2,1,0:T(8,128)(2,1)}, bf16[4,2,2,16,768]{4,3,2,1,0:T(8,128)(2,1)}, bf16[4,2,2,48,1536]{4,3,2,1,0:T(8,128)(2,1)}, bf16[4,2,2...) custom-call(bf16[16,32,768]{2,1,0:T(8,128)(2,1)} %get-tuple-element., ...), custom_call_target="tpu_custom_call" | custom-call | tf_op jit(solution)/shard_map/pallas_call | solution.py:72
  105.8 65.9 %shard_map.258 = (bf16[4,2,2,48,1024]{4,3,2,1,0:T(8,128)(2,1)}, bf16[4,2,2,64,384]{4,3,2,1,0:T(8,128)(2,1)}, bf16[768,1024]{1,0:T(8,128)(2,1)}, f32[128,768]{1,0...) custom-call(f32[512,768]{1,0:T(8,128)} %get-tuple-element.74.hidden, bf16[2,64,256]{2,1,0:T(8,128)(2,1)} %get-tuple-element.75.select, ...), custom_call_target="tpu_custom_call" | custom-call | tf_op jit(solution)/shard_map/pallas_call | solution.py:72
  171.7 100.5 %shard_map.259 = (bf16[8,2,32,768]{3,2,1,0:T(8,128)(2,1)}, f32[16,128]{1,0:T(8,128)}, f32[24,2048]{1,0:T(8,128)}, f32[32,768]{1,0:T(8,128)}, f32[24,768]{1,0:T(8...) custom-call(f32[512,768]{1,0:T(8,128)} %get-tuple-element.84.refs_0_, ...), custom_call_target="tpu_custom_call" | custom-call | tf_op jit(solution)/shard_map/pallas_call | solution.py:72
  272.2 4.1 %shard_map.260 = (f32[16,32,768]{2,1,0:T(8,128)}, f32[24,8192]{1,0:T(8,128)}, f32[1,1]{1,0:T(1,128)}, f32[1,24]{1,0:T(1,128)}, f32[1,24]{1,0:T(1,128)}, /*index=...) custom-call(s32[16]{0:T(128)} %deal_ref.3, ...), custom_call_target="tpu_custom_call" | custom-call | tf_op jit(solution)/shard_map/pallas_call | solution.py:198
